TPU v7x, 512 devices: a whole 4x8x8 slice. The times are simulated.
512 devices in a mesh: gx: 64 (over z, x, core), ta: 8 (over y).
Axes of the slice: x: 4, y: 8, z: 8, core: 2. Of those that a mesh axis runs over, the one named last changes fastest.
Arguments:
- d_out: bfloat16 [16384, 4096], P('gx', 'ta'), may hold values from -0.75 to 0.75
- kept: int32 [2048], P('gx'), may hold values from 0 to 16383, as said below
- expert_ids: int32 [2048, 8], P('gx'), may hold values from 0 to 63, all different within a row; in each aligned block of 32 rows (0 to 31, 32 to 63, ...) at most 8 rows name the same one
- gates: bfloat16 [2048, 8], P('gx'), may hold values from 0.049804688 to 1
- down_weight: bfloat16 [64, 1536, 4096], P('gx', 'ta'), may hold values from -0.15625 to 0.15625
- gate_pre: bfloat16 [64, 1536, 512], P('gx', 'ta'), may hold values from -6 to 6
- up_pre: bfloat16 [64, 1536, 512], P('gx', 'ta'), may hold values from -6 to 6
- query: bfloat16 [2048, 8192], P('gx', 'ta'), may hold values from -6 to 6
- keys: bfloat16 [2048, 512], P('gx'), may hold values from -6 to 6
- values: bfloat16 [2048, 512], P('gx'), may hold values from -6 to 6
- d_attn: bfloat16 [2048, 8192], P('gx', 'ta'), may hold values from -12 to 12
Outputs:
- d_down: bfloat16 [64, 1536, 4096], P('gx', 'ta')
- d_gate_pre: bfloat16 [64, 1536, 512], P('gx', 'ta')
- d_up_pre: bfloat16 [64, 1536, 512], P('gx', 'ta')
- d_gates: float32 [2048, 8], P('gx')
- d_query: bfloat16 [2048, 8192], P('gx', 'ta')
- d_key: float32 [2048, 512], P('gx')
- d_value: float32 [2048, 512], P('gx')
Inputs may be any that keep to these rules, and one draw needn't show every extreme that they name: `kept`: rising; the 32 selected tokens of block i lie in positions i * 256 to (i + 1) * 256 - 1 and include both ends. `expert_ids`: each row names 8 different experts; in each aligned block of 32 rows no expert is named more than 8 times.
All inputs are finite; a program needn't handle non-finite values.
Results may differ from a plain program's by a relative error of at most 0.0068.
Values may be sent and summed in bfloat16 or wider, within the bound.
No kernel may reach another device: no remote copies, remote signals or barrier semaphores. Data moves between devices by JAX's collectives and lax.ppermute only.
A program may use at most 64 MiB of HBM per device.

v0:
```python
import jax
import jax.numpy as jnp
from jax import lax
from jax.sharding import PartitionSpec as P

H = 64
KVH = 4
HD = 128


def on_device(
    d_out, kept, expert_ids, gates, down_weight, gate_pre, up_pre, query, keys, values, d_attn
):
    n_experts = lax.axis_size("gx")
    keep_dev = kept.shape[0]
    tok_dev = d_out.shape[0]
    top = expert_ids.shape[1]
    slot_count = gate_pre.shape[2]
    cap = slot_count // n_experts
    picked = jnp.take(d_out, kept % tok_dev, axis=0)
    flat_ids = expert_ids.reshape(-1)
    onehot = (flat_ids[:, None] == jnp.arange(n_experts, dtype=jnp.int32)[None, :]).astype(
        jnp.int32
    )
    rank = jnp.sum((jnp.cumsum(onehot, axis=0) - onehot) * onehot, axis=1)
    dest = flat_ids * cap + rank
    match = dest[:, None] == jnp.arange(slot_count, dtype=jnp.int32)[None, :]
    match_rows = jnp.sum(
        match.reshape(keep_dev, top, slot_count).astype(jnp.float32), axis=1
    ).astype(jnp.bfloat16)
    gate_slots = jnp.sum(jnp.where(match, gates.reshape(-1, 1).astype(jnp.float32), 0.0), axis=0)
    gate_slots = gate_slots.astype(jnp.bfloat16).reshape(n_experts, cap)
    full_rows = lax.all_gather(picked, "ta", axis=1, tiled=True)
    packed = lax.dot_general(
        match_rows, full_rows, (((0,), (0,)), ((), ())), preferred_element_type=jnp.float32
    )
    arrived = lax.all_to_all(
        packed.astype(jnp.bfloat16).reshape(n_experts, cap, full_rows.shape[1]),
        "gx",
        split_axis=0,
        concat_axis=0,
        tiled=True,
    )
    arrived_gates = lax.all_to_all(gate_slots, "gx", split_axis=0, concat_axis=0, tiled=True)
    slot_rows = arrived.reshape(slot_count, -1)
    slot_weight = arrived_gates.reshape(-1).astype(jnp.float32)
    weight = down_weight[0]
    z = lax.dot_general(
        weight, slot_rows, (((1,), (1,)), ((), ())), preferred_element_type=jnp.float32
    )
    g = gate_pre[0].astype(jnp.float32)
    u = up_pre[0].astype(jnp.float32)
    sig = jax.nn.sigmoid(g)
    act = g * sig
    hidden = act * u
    slot_dots = jnp.sum(hidden * z, axis=0)
    grad_hidden = z * slot_weight[None, :]
    grad_up = (grad_hidden * act).astype(jnp.bfloat16)[None]
    grad_gate = (grad_hidden * u * sig * (1.0 + g * (1.0 - sig))).astype(jnp.bfloat16)[None]
    weighted = (hidden * slot_weight[None, :]).astype(jnp.bfloat16)
    grad_weight = jnp.dot(weighted, slot_rows, preferred_element_type=jnp.float32).astype(
        jnp.bfloat16
    )[None]
    returned = lax.all_to_all(
        slot_dots.reshape(n_experts, cap), "gx", split_axis=0, concat_axis=0, tiled=True
    )
    gate_terms = jnp.sum(jnp.where(match, returned.reshape(1, -1), 0.0), axis=1).reshape(
        keep_dev, top
    )
    local_heads = query.shape[1] // HD
    group = H // KVH
    kv_local = max(1, local_heads // group)
    per_kv = local_heads // kv_local
    first_kv = lax.axis_index("ta") * local_heads // group
    key_local = lax.dynamic_slice_in_dim(keys, first_kv * HD, kv_local * HD, 1)
    value_local = lax.dynamic_slice_in_dim(values, first_kv * HD, kv_local * HD, 1)
    key_all, value_all = (
        lax.all_gather(key_local, "gx", axis=0, tiled=True),
        lax.all_gather(value_local, "gx", axis=0, tiled=True),
    )
    total = key_all.shape[0]
    key_three = key_all.reshape(total, kv_local, HD)
    value_three = value_all.reshape(total, kv_local, HD)
    query_four = query.reshape(keep_dev, kv_local, per_kv, HD)
    grad_four = d_attn.reshape(keep_dev, kv_local, per_kv, HD)
    scale = HD ** (-0.5)
    scores = (
        jnp.einsum("qcgd,kcd->cgqk", query_four, key_three, preferred_element_type=jnp.float32)
        * scale
    )
    query_pos = lax.axis_index("gx") * keep_dev + jnp.arange(keep_dev)
    causal = jnp.arange(total)[None, :] <= query_pos[:, None]
    scores = jnp.where(causal[None, None], scores, -1e30)
    top_score = jnp.max(scores, axis=3, keepdims=True)
    expo = jnp.exp(scores - top_score)
    probs = expo / jnp.sum(expo, axis=3, keepdims=True)
    grad_probs = jnp.einsum(
        "qcgd,kcd->cgqk", grad_four, value_three, preferred_element_type=jnp.float32
    )
    grad_scores = probs * (grad_probs - jnp.sum(probs * grad_probs, axis=3, keepdims=True))
    probs_b = probs.astype(jnp.bfloat16)
    grad_b = grad_scores.astype(jnp.bfloat16)
    grad_query = (
        jnp.einsum("cgqk,kcd->qcgd", grad_b, key_three, preferred_element_type=jnp.float32) * scale
    )
    grad_query = grad_query.astype(jnp.bfloat16).reshape(keep_dev, -1)
    key_part = (
        jnp.einsum("cgqk,qcgd->kcd", grad_b, query_four, preferred_element_type=jnp.float32) * scale
    )
    value_part = jnp.einsum(
        "cgqk,qcgd->kcd", probs_b, grad_four, preferred_element_type=jnp.float32
    )
    owned = lax.psum_scatter(
        jnp.concatenate(
            [
                key_part.reshape(keep_dev * lax.axis_size("gx"), -1),
                value_part.reshape(keep_dev * lax.axis_size("gx"), -1),
            ],
            axis=1,
        ),
        "gx",
        scatter_dimension=0,
        tiled=True,
    )
    width = kv_local * HD
    empty = jnp.zeros((keep_dev, KVH * HD), jnp.float32)
    key_full = lax.dynamic_update_slice(empty, owned[:, :width], (0, first_kv * HD))
    value_full = lax.dynamic_update_slice(empty, owned[:, width:], (0, first_kv * HD))
    grad_gates, grad_key, grad_value = lax.psum((gate_terms, key_full, value_full), "ta")
    return (grad_weight, grad_gate, grad_up, grad_gates, grad_query, grad_key, grad_value)


def solution(mesh):
    in_specs = (
        P("gx", "ta"),
        P("gx"),
        P("gx", None),
        P("gx", None),
        P("gx", "ta", None),
        P("gx", "ta", None),
        P("gx", "ta", None),
        P("gx", "ta"),
        P("gx", None),
        P("gx", None),
        P("gx", "ta"),
    )
    out_specs = (
        P("gx", "ta", None),
        P("gx", "ta", None),
        P("gx", "ta", None),
        P("gx", None),
        P("gx", "ta"),
        P("gx", None),
        P("gx", None),
    )
    return jax.shard_map(
        on_device, mesh=mesh, in_specs=in_specs, out_specs=out_specs, check_vma=False
    )
```

profile of v0, /device:TPU:6, one launch (start us, length us, event | category | flops | bytes accessed | tf_op | source)
XLA Modules:
  0.0 499.3 jit_solution(1224681247285578095)
XLA Ops:
  7.2 0.9 copy.53
  8.2 0.7 compare_and_fusion
  8.9 1.6 gather_fusion
  10.6 26.4 %all_gather.9 = bf16[32,4096]{1,0:T(8,128)(2,1)S(1)} all-gather(bf16[32,512]{1,0:T(8,128)(2,1)S(1)} %broadcast_select_fusion), channel_id=1, replica_groups=mesh['gx'=64,'ta'=8] {'ta'}, dimensions={1}, use_global_device_ids=true | all-gather | bytes 294912 | tf_op jit(solution)/shard_map/all_gather | solution.py:33
  38.3 3.2 fusion
  41.6 14.1 %all-to-all-start.1 = ((bf16[64,8,4096]{2,1,0:T(8,128)(2,1)}), bf16[64,8,4096]{2,1,0:T(8,128)(2,1)}, u32[]{:S(2)}, u32[]{:S(2)}) async-start(bf16[64,8,4096]{2,1,0:T(8,128)(2,1)} %fusion), calls=%async_computation.1 | async-start | bytes 8388608 | tf_op jit(solution)/shard_map/all_to_all | solution.py:37
  55.8 0.7 constant_dynamic-slice_fusion.1
  56.5 0.7 constant_dynamic-slice_fusion
  57.2 134.1 %all_gather.10 = bf16[2048,128]{1,0:T(8,128)(2,1)S(1)} all-gather(bf16[32,128]{1,0:T(8,128)(2,1)S(1)} %constant_dynamic-slice_fusion.1), channel_id=1, replica_groups=mesh['gx'=64,'ta'=8] {'gx'}, dimensions={0}, use_global_device_ids=true | all-gather | bytes 532480 | tf_op jit(solution)/shard_map/all_gather | solution.py:78
  191.2 48.2 %all_gather.11 = bf16[2048,128]{1,0:T(8,128)(2,1)S(1)} all-gather(bf16[32,128]{1,0:T(8,128)(2,1)S(1)} %constant_dynamic-slice_fusion), channel_id=1, replica_groups=mesh['gx'=64,'ta'=8] {'gx'}, dimensions={0}, use_global_device_ids=true | all-gather | bytes 532480 | tf_op jit(solution)/shard_map/all_gather | solution.py:79
  240.9 0.7 multiply_reduce_fusion
  243.2 1.4 pad_maximum_fusion
  244.6 3.0 copy.68
  247.6 0.8 copy.56
  248.4 0.7 reshape.214
  249.5 0.6 copy.98
  250.2 3.8 fusion.33
  254.0 0.7 all_to_all.15
  254.7 9.2 %all-to-all-start.2 = ((f32[64,1,8]{2,1,0:T(1,128)}), f32[64,1,8]{2,1,0:T(1,128)S(1)}, u32[]{:S(2)}, u32[]{:S(2)}) async-start(f32[64,1,8]{2,1,0:T(1,128)} %bitcast.11), calls=%async_computation.2 | async-start | bytes 65536 | tf_op jit(solution)/shard_map/all_to_all | solution.py:64
  263.9 132.1 %reduce-scatter.4.cloned.1.call-done = f32[32,256]{1,0:T(8,128)} async-done(((f32[2048,256]{1,0:T(8,128)}), f32[32,256]{1,0:T(8,128)}) %reduce-scatter.4.cloned.1.call-update) | async-done | bytes 32784
  396.1 0.7 slice_dynamic-update-slice_fusion.1
  397.3 0.7 reduce.12
  398.4 0.7 convert_element_type.130
  399.1 8.1 %all-to-all-start = ((bf16[64,1,8]{2,1,0:T(2,128)(2,1)}), bf16[64,1,8]{2,1,0:T(2,128)(2,1)S(1)}, u32[]{:S(2)}, u32[]{:S(2)}) async-start(bf16[64,1,8]{2,1,0:T(2,128)(2,1)} %convert_element_type.130), calls=%async_computation | async-start | bytes 65536 | tf_op jit(solution)/shard_map/all_to_all | solution.py:44
  407.3 0.7 slice_dynamic-update-slice_fusion
  408.8 29.7 %psum.21 = f32[32,8]{1,0:T(8,128)S(1)} all-reduce(f32[32,8]{1,0:T(8,128)S(1)} %reshape.208), channel_id=1, replica_groups=mesh['gx'=64,'ta'=8] {'ta'}, use_global_device_ids=true, to_apply=%region_7.8 | all-reduce | flops 256 | bytes 2048 | tf_op jit(solution)/shard_map/psum | solution.py:129
  438.5 0.7 copy.67
  439.3 4.4 fusion.1
  443.7 0.9 fusion.43
  444.7 44.8 %all-reduce.3.cloned.1.call-done = (f32[32,512]{1,0:T(8,128)}, f32[32,512]{1,0:T(8,128)}) async-done(((f32[32,512]{1,0:T(8,128)}, f32[32,512]{1,0:T(8,128)}), (f32[32,512]{1,0:T(8,128)}, f32[32,512]{1,0:T(8,128)})) %all-reduce.3.cloned.1.call-update) | async-done | bytes 131088 | tf_op jit(solution)/shard_map/psum | solution.py:129
  489.5 1.5 copy.103
  491.0 1.5 copy.104
  (62 shorter events, 7.0 us)
Async XLA Ops:
  7.2 243.1 %copy-start = (bf16[1,192,4096]{2,1,0:T(8,128)(2,1)S(1)}, bf16[1,192,4096]{2,1,0:T(8,128)(2,1)}, u32[]{:S(2)}) copy-start(bf16[1,192,4096]{2,1,0:T(8,128)(2,1)} %param.15) | copy-start | bytes 4718596
  8.2 33.4 %copy-start.6 = (s32[256]{0:T(256)}, s32[256]{0:T(256)S(1)}, u32[]{:S(2)}) copy-start(s32[256]{0:T(256)S(1)} %reshape.204) | copy-start | bytes 3076
  38.0 3.6 copy-start.8
  41.6 198.0 %copy-start.1 = (bf16[32,1024]{1,0:T(8,128)(2,1)S(1)}, bf16[32,1024]{1,0:T(8,128)(2,1)}, u32[]{:S(2)}) copy-start(bf16[32,1024]{1,0:T(8,128)(2,1)} %param.18) | copy-start | bytes 196612
  41.6 208.7 %all-to-all-start.1 = ((bf16[64,8,4096]{2,1,0:T(8,128)(2,1)}), bf16[64,8,4096]{2,1,0:T(8,128)(2,1)}, u32[]{:S(2)}, u32[]{:S(2)}) async-start(bf16[64,8,4096]{2,1,0:T(8,128)(2,1)} %fusion), calls=%async_computation.1 | async-start | bytes 8388608 | tf_op jit(solution)/shard_map/all_to_all | solution.py:37
  55.7 340.4 %reduce-scatter.4.cloned.1.call-start = ((), (), s32[]{:S(2)}) async-start(), calls=%async_computation.4 | async-start | bytes 2129920
  240.1 0.8 copy-start.11
  247.6 2.7 copy-start.4
  247.6 2.7 copy-start.5
  249.1 1.1 copy-start.7
  249.1 1.1 copy-start.9
  250.2 147.9 %copy-start.10 = (f32[256]{0:T(256)S(1)}, f32[256]{0:T(256)}, u32[]{:S(2)}) copy-start(f32[256]{0:T(256)} %reshape.214) | copy-start | bytes 3076
  254.7 142.1 %all-to-all-start.2 = ((f32[64,1,8]{2,1,0:T(1,128)}), f32[64,1,8]{2,1,0:T(1,128)S(1)}, u32[]{:S(2)}, u32[]{:S(2)}) async-start(f32[64,1,8]{2,1,0:T(1,128)} %bitcast.11), calls=%async_computation.2 | async-start | bytes 65536 | tf_op jit(solution)/shard_map/all_to_all | solution.py:64
  396.8 11.3 %copy-start.3 = (f32[32,512]{1,0:T(8,128)}, f32[32,512]{1,0:T(8,128)S(1)}, u32[]{:S(2)}) copy-start(f32[32,512]{1,0:T(8,128)S(1)} %slice_dynamic-update-slice_fusion.1) | copy-start | bytes 196612
  399.1 40.0 %all-to-all-start = ((bf16[64,1,8]{2,1,0:T(2,128)(2,1)}), bf16[64,1,8]{2,1,0:T(2,128)(2,1)S(1)}, u32[]{:S(2)}, u32[]{:S(2)}) async-start(bf16[64,1,8]{2,1,0:T(2,128)(2,1)} %convert_element_type.130), calls=%async_computation | async-start | bytes 65536 | tf_op jit(solution)/shard_map/all_to_all | solution.py:44
  407.2 82.3 %all-reduce.3.cloned.1.call-start = ((), (), s32[]{:S(2)}) async-start(), calls=%async_computation.5 | async-start | bytes 262144 | tf_op jit(solution)/shard_map/psum | solution.py:129
  408.0 0.6 copy-start.2
Sparse Core Ops, SparseCore 0:
  247.7 148.2 reduce-scatter.3
  411.0 78.4 all-reduce.2
where the time goes:
time: 500 us; the launch traced here: 499 us
  blocking collectives  238 us (48%)
  waiting for transfers between devices  177 us (35%)
  starting transfers between devices  31.5 us (6%)
  local copies, waits for them, and re-layouts  17.8 us (4%)
  between operations  14.3 us (3%)
  matrix products  14 us (3%)
  other arithmetic  6.37 us (1%)
    all_gather x1, blocking collectives, on_device(): lax.all_gather(key_local, 'gx', axis=0, tiled=True)  134 us
    unnamed x3, waiting for transfers between devices  132 us
    all_gather x1, blocking collectives, on_device(): lax.all_gather(value_local, 'gx', axis=0, tiled=True)  48.2 us
    psum x1, waiting for transfers between devices, on_device(): lax.psum((gate_terms, key_full, value_full), 'ta')  44.8 us
    psum x1, blocking collectives, on_device(): lax.psum((gate_terms, key_full, value_full), 'ta')  29.7 us
    all_gather x1, blocking collectives, on_device(): full_rows = lax.all_gather(picked, 'ta', axis=1, tiled=True)  26.4 us
    all_to_all x1, starting transfers between devices, on_device(): lax.all_to_all(packed.astype(jnp.bfloat16).reshape(n_experts, cap, full_r...  14.1 us
  transfers between devices with their start and end apart: 5, of which 2 were waited for; matrix products, arithmetic and copies ran while one was open for 5% of the time, Pallas kernels for 0%

commit v1 on v0

v1 whole, which is shorter than its diff:
```python
import jax
import jax.numpy as jnp
from jax import lax
from jax.sharding import Mesh, PartitionSpec as P

H = 64
KVH = 4
HD = 128
GX = ("z", "x", "c")
ZX = ("z", "x")


def exchange(values, axes):
    return lax.all_to_all(values, axes, split_axis=0, concat_axis=0, tiled=True)


def to_partner(values):
    return lax.ppermute(values, "c", [(0, 1), (1, 0)])


def slot_tables(expert_ids, gates, slots, cap):
    rows, top = expert_ids.shape
    lane = lax.broadcasted_iota(jnp.int32, (rows, slots), 1)
    expert = lane // cap
    named = jnp.zeros((rows, slots), jnp.float32)
    weight = jnp.zeros((rows, slots), jnp.float32)
    for j in range(top):
        hit = expert_ids[:, j : j + 1] == expert
        named = named + hit.astype(jnp.float32)
        weight = weight + jnp.where(hit, gates[:, j : j + 1].astype(jnp.float32), 0.0)
    below = lax.broadcasted_iota(jnp.int32, (rows, rows), 0) > lax.broadcasted_iota(
        jnp.int32, (rows, rows), 1
    )
    rank = jnp.dot(
        below.astype(jnp.bfloat16), named.astype(jnp.bfloat16), preferred_element_type=jnp.float32
    )
    taken = (named > 0.0) & (rank.astype(jnp.int32) == lane % cap)
    return taken, weight


def on_device(
    d_out, kept, expert_ids, gates, down_weight, gate_pre, up_pre, query, keys, values, d_attn
):
    core = lax.axis_index("c")
    chip = lax.axis_index(ZX)
    chips = lax.axis_size(ZX)
    n_experts = lax.axis_size(GX)
    n_ta = lax.axis_size("ta")
    keep_dev = kept.shape[0]
    tok_dev, width = d_out.shape
    top = expert_ids.shape[1]
    slots = gate_pre.shape[2]
    cap = slots // n_experts

    local_heads = query.shape[1] // HD
    group = H // KVH
    first_kv = lax.axis_index("ta") * local_heads // group
    kv = jnp.concatenate(
        [
            lax.dynamic_slice_in_dim(keys, first_kv * HD, HD, 1),
            lax.dynamic_slice_in_dim(values, first_kv * HD, HD, 1),
        ],
        axis=1,
    )

    at = kept % tok_dev
    pick = (at[:, None] == lax.broadcasted_iota(jnp.int32, (keep_dev, tok_dev), 1)).astype(
        jnp.bfloat16
    )
    picked = jnp.dot(pick, d_out, preferred_element_type=jnp.float32).astype(jnp.bfloat16)
    taken, weight_of = slot_tables(expert_ids, gates, slots, cap)
    taken_b = taken.astype(jnp.bfloat16)
    packed = lax.dot_general(
        taken_b, picked, (((0,), (0,)), ((), ())), preferred_element_type=jnp.float32
    ).astype(jnp.bfloat16)
    gate_row = jnp.sum(jnp.where(taken, weight_of, 0.0), axis=0).astype(jnp.bfloat16)
    message = jnp.concatenate(
        [packed, jnp.broadcast_to(gate_row[:, None], (slots, HD))], axis=1
    ).reshape(n_experts, cap, width + HD)
    arrived = exchange(message, GX).reshape(slots, width + HD)
    slot_weight = arrived[:, width].astype(jnp.float32)
    slot_rows = lax.all_gather(arrived[:, :width], "ta", axis=1, tiled=True)

    kv_own = exchange(jnp.broadcast_to(kv[None], (chips,) + kv.shape), ZX).reshape(-1, 2 * HD)
    kv_other = to_partner(kv_own)

    half = chips * keep_dev
    total = 2 * half
    kv_all = jnp.concatenate([kv_own, kv_other], axis=0)
    key_all = kv_all[:, :HD]
    value_all = kv_all[:, HD:]
    rows = keep_dev * local_heads
    query_rows = query.reshape(rows, HD)
    grad_rows = d_attn.reshape(rows, HD)
    scale = HD ** (-0.5)
    nt = (((1,), (1,)), ((), ()))
    tn = (((0,), (0,)), ((), ()))
    scores = lax.dot_general(query_rows, key_all, nt, preferred_element_type=jnp.float32) * scale
    column = lax.broadcasted_iota(jnp.int32, (rows, total), 1)
    at_core = jnp.where(column < half, core, 1 - core)
    inner = column % half
    key_pos = (inner // keep_dev * 2 + at_core) * keep_dev + inner % keep_dev
    query_pos = (chip * 2 + core) * keep_dev + lax.broadcasted_iota(
        jnp.int32, (rows, total), 0
    ) // local_heads
    scores = jnp.where(key_pos <= query_pos, scores, -1e30)
    top_score = jnp.max(scores, axis=1, keepdims=True)
    expo = jnp.exp(scores - top_score)
    probs = expo / jnp.sum(expo, axis=1, keepdims=True)
    grad_probs = lax.dot_general(grad_rows, value_all, nt, preferred_element_type=jnp.float32)
    grad_scores = probs * (grad_probs - jnp.sum(probs * grad_probs, axis=1, keepdims=True))
    probs_b = probs.astype(jnp.bfloat16)
    grad_b = grad_scores.astype(jnp.bfloat16)
    grad_query = jnp.dot(grad_b, key_all, preferred_element_type=jnp.float32) * scale
    grad_query = grad_query.astype(jnp.bfloat16).reshape(keep_dev, -1)
    key_part = lax.dot_general(grad_b, query_rows, tn, preferred_element_type=jnp.float32) * scale
    value_part = lax.dot_general(probs_b, grad_rows, tn, preferred_element_type=jnp.float32)
    part = jnp.concatenate([key_part, value_part], axis=1)
    from_other = to_partner(part[half:].astype(jnp.bfloat16))
    chip_part = (part[:half] + from_other.astype(jnp.float32)).astype(jnp.bfloat16)
    owned = jnp.sum(
        exchange(chip_part.reshape(chips, keep_dev, 2 * HD), ZX).astype(jnp.float32), axis=0
    )

    z = lax.dot_general(down_weight[0], slot_rows, nt, preferred_element_type=jnp.float32)
    g = gate_pre[0].astype(jnp.float32)
    u = up_pre[0].astype(jnp.float32)
    sig = jax.nn.sigmoid(g)
    act = g * sig
    hidden = act * u
    slot_dots = jnp.sum(hidden * z, axis=0)
    grad_hidden = z * slot_weight[None, :]
    grad_up = (grad_hidden * act).astype(jnp.bfloat16)[None]
    grad_gate = (grad_hidden * u * sig * (1.0 + g * (1.0 - sig))).astype(jnp.bfloat16)[None]
    weighted = (hidden * slot_weight[None, :]).astype(jnp.bfloat16)
    grad_weight = jnp.dot(weighted, slot_rows, preferred_element_type=jnp.float32).astype(
        jnp.bfloat16
    )[None]

    returned = exchange(slot_dots.reshape(n_experts, cap), GX).reshape(1, slots)
    mine = jnp.where(taken, returned, 0.0)
    expert = lax.broadcasted_iota(jnp.int32, (keep_dev, slots), 1) // cap
    gate_terms = jnp.concatenate(
        [
            jnp.sum(jnp.where(expert_ids[:, j : j + 1] == expert, mine, 0.0), axis=1, keepdims=True)
            for j in range(top)
        ],
        axis=1,
    )

    high = lax.reduce_precision(gate_terms, 8, 7)
    low = (gate_terms - high).astype(jnp.bfloat16)
    last = jnp.concatenate(
        [
            owned.astype(jnp.bfloat16),
            high.astype(jnp.bfloat16),
            low,
            jnp.zeros((keep_dev, HD - 2 * top), jnp.bfloat16),
        ],
        axis=1,
    )
    terms = exchange(jnp.broadcast_to(last[None], (n_ta,) + last.shape), "ta").astype(jnp.float32)
    gate_sum = jnp.sum(terms[:, :, 2 * HD : 2 * HD + 2 * top], axis=0)
    grad_gates = gate_sum[:, :top] + gate_sum[:, top:]
    heads = jnp.sum(
        terms[:, :, : 2 * HD].reshape(KVH, n_ta // KVH, keep_dev, 2 * HD), axis=1
    )
    grad_key = jnp.concatenate([heads[i, :, :HD] for i in range(KVH)], axis=1)
    grad_value = jnp.concatenate([heads[i, :, HD:] for i in range(KVH)], axis=1)
    return (grad_weight, grad_gate, grad_up, grad_gates, grad_query, grad_key, grad_value)


def solution(mesh):
    shape = dict(mesh.shape)
    fine = Mesh(mesh.devices.reshape(8, shape["gx"] // 16, 2, shape["ta"]), GX + ("ta",))
    in_specs = (
        P(GX, "ta"),
        P(GX),
        P(GX, None),
        P(GX, None),
        P(GX, "ta", None),
        P(GX, "ta", None),
        P(GX, "ta", None),
        P(GX, "ta"),
        P(GX, None),
        P(GX, None),
        P(GX, "ta"),
    )
    out_specs = (
        P(GX, "ta", None),
        P(GX, "ta", None),
        P(GX, "ta", None),
        P(GX, None),
        P(GX, "ta"),
        P(GX, None),
        P(GX, None),
    )
    return jax.shard_map(
        on_device, mesh=fine, in_specs=in_specs, out_specs=out_specs, check_vma=False
    )
```

time: 500 us -> 154 us (0.31)
  blocking collectives: 238 us -> 34.1 us
  waiting for transfers between devices: 177 us -> 42.4 us
  local copies, waits for them, and re-layouts: 17.8 us -> 9.13 us
    all_gather x3 -> x0, blocking collectives: 209 us -> none  [the longest x1 134 us: on_device(): lax.all_gather(key_local, 'gx', axis=0, tiled=True)]
    unnamed x3 -> x1, waiting for transfers between devices: 132 us -> 0.02 us
    psum x1 -> x0, waiting for transfers between devices: 44.8 us -> none  [on_device(): lax.psum((gate_terms, key_full, value_full), 'ta')]
    all_to_all x0 -> x1, blocking collectives: none -> 34.1 us  [exchange(): return lax.all_to_all(values, axes, split_axis=0, concat_axis=0, tiled=True)]
    psum x1 -> x0, blocking collectives: 29.7 us -> none  [on_device(): lax.psum((gate_terms, key_full, value_full), 'ta')]
    all_to_all x3 -> x4, waiting for transfers between devices: 0.01 us -> 29.4 us  [exchange(): return lax.all_to_all(values, axes, split_axis=0, concat_axis=0, tiled=True)]
    all_gather x0 -> x1, waiting for transfers between devices: none -> 9.39 us  [on_device(): slot_rows = lax.all_gather(arrived[:, :width], 'ta', axis=1, tiled=True)]
    unnamed x30 -> x60, local copies, waits for them, and re-layouts: 9.17 us -> 0.26 us
  transfers between devices with their start and end apart: 5 -> 7, of which waited for: 2 -> 7; matrix products, arithmetic and copies ran while one was open for 5% -> 14% of each run, Pallas kernels for 0% -> 0%
where the time goes in v1:
time: 154 us; the launch traced here: 152 us
  waiting for transfers between devices  42.4 us (28%)
  blocking collectives  34.1 us (22%)
  starting transfers between devices  28.3 us (18%)
  matrix products  15.4 us (10%)
  between operations  14.7 us (10%)
  local copies, waits for them, and re-layouts  9.13 us (6%)
  other arithmetic  7.96 us (5%)
    all_to_all x1, blocking collectives, exchange(): return lax.all_to_all(values, axes, split_axis=0, concat_axis=0, tiled=True)  34.1 us
    all_to_all x4, waiting for transfers between devices, exchange(): return lax.all_to_all(values, axes, split_axis=0, concat_axis=0, tiled=True)  29.4 us
    all_to_all x4, starting transfers between devices, exchange(): return lax.all_to_all(values, axes, split_axis=0, concat_axis=0, tiled=True)  24.2 us
    all_gather x1, waiting for transfers between devices, on_device(): slot_rows = lax.all_gather(arrived[:, :width], 'ta', axis=1, tiled=True)  9.39 us
    dot_general x1, matrix products, on_device(): lax.dot_general(down_weight[0], slot_rows, nt, preferred_element_type=jnp...  4.61 us
    dot_general x1, matrix products, on_device(): jnp.dot(weighted, slot_rows, preferred_element_type=jnp.float32)  4.49 us
    ppermute x2, starting transfers between devices, to_partner(): return lax.ppermute(values, 'c', [(0, 1), (1, 0)])  4.09 us
    ppermute x2, waiting for transfers between devices, to_partner(): return lax.ppermute(values, 'c', [(0, 1), (1, 0)])  3.56 us
  transfers between devices with their start and end apart: 7, of which 7 were waited for; matrix products, arithmetic and copies ran while one was open for 14% of the time, Pallas kernels for 0%

profile of v1, /device:TPU:6, one launch (start us, length us, event | category | flops | bytes accessed | tf_op | source)
XLA Modules:
  0.0 151.9 jit_solution(8518392509325831410)
XLA Ops:
  7.3 1.0 slice_bitcast_fusion.15
  8.4 1.0 bitcast_convert_fusion.7
  9.3 0.7 and_select_fusion
  10.4 1.5 convolution_convert_fusion.1
  12.3 34.1 %all_to_all.29 = bf16[64,8,640]{2,1,0:T(8,128)(2,1)S(1)} all-to-all(bf16[64,8,640]{2,1,0:T(8,128)(2,1)S(1)} %bitcast.129), channel_id=1, replica_groups=mesh['z'=8,'x'=4,'c'=2,'ta'=8] {'z','x','c'}, dimensions={0} | all-to-all | bytes 1310720 | tf_op jit(solution)/shard_map/all_to_all | solution.py:14
  46.4 0.8 slice.146
  47.2 0.7 constant_dynamic-slice_fusion
  48.0 0.9 broadcast_in_dim.216
  48.8 5.4 %all-to-all-start.1 = ((bf16[32,32,256]{2,1,0:T(8,128)(2,1)}), bf16[32,32,256]{2,1,0:T(8,128)(2,1)S(1)}, u32[]{:S(2)}, u32[]{:S(2)}) async-start(bf16[32,32,256]{2,1,0:T(8,128)(2,1)} %broadcast_in_dim.216), calls=%async_computation.1 | async-start | bytes 1048576 | tf_op jit(solution)/shard_map/all_to_all | solution.py:14
  54.3 16.6 %all-to-all-done.1 = bf16[32,32,256]{2,1,0:T(8,128)(2,1)S(1)} async-done(((bf16[32,32,256]{2,1,0:T(8,128)(2,1)}), bf16[32,32,256]{2,1,0:T(8,128)(2,1)S(1)}, u32[]{:S(2)}, u32[]{:S(2)}) %all-to-all-start.1) | async-done | bytes 524320 | tf_op jit(solution)/shard_map/all_to_all | solution.py:14
  70.9 1.9 %collective-permute-start = (bf16[1024,256]{1,0:T(8,128)(2,1)S(1)}, bf16[1024,256]{1,0:T(8,128)(2,1)S(1)}, u32[]{:S(2)}, u32[]{:S(2)}) collective-permute-start(bf16[1024,256]{1,0:T(8,128)(2,1)S(1)} %bitcast.131), channel_id=1, source_target_pairs={{0,8},{8,0},{1,9},{9,1},{2,10},{10,2},{3,11},{11,3},{4,12},{12,4},... | collective-permute-start | bytes 1572872 | tf_op jit(solution)/shard_map/ppermute | solution.py:18
  72.9 1.8 %collective-permute-done = bf16[1024,256]{1,0:T(8,128)(2,1)S(1)} collective-permute-done((bf16[1024,256]{1,0:T(8,128)(2,1)S(1)}, bf16[1024,256]{1,0:T(8,128)(2,1)S(1)}, u32[]{:S(2)}, u32[]{:S(2)}) %collective-permute-start) | collective-permute-done | bytes 524320 | tf_op jit(solution)/shard_map/ppermute | solution.py:18
  74.7 1.5 fusion.114
  78.8 2.2 %collective-permute-start.1 = (bf16[1024,256]{0,1:T(8,128)(2,1)S(1)}, bf16[1024,256]{0,1:T(8,128)(2,1)S(1)}, u32[]{:S(2)}, u32[]{:S(2)}) collective-permute-start(bf16[1024,256]{0,1:T(8,128)(2,1)S(1)} %fusion.25), channel_id=1, source_target_pairs={{0,8},{8,0},{1,9},{9,1},{2,10},{10,2},{3,11},{11,3},{4,12},{12,4},... | collective-permute-start | bytes 1572872 | tf_op jit(solution)/shard_map/ppermute | solution.py:18
  81.0 1.7 %collective-permute-done.1 = bf16[1024,256]{0,1:T(8,128)(2,1)S(1)} collective-permute-done((bf16[1024,256]{0,1:T(8,128)(2,1)S(1)}, bf16[1024,256]{0,1:T(8,128)(2,1)S(1)}, u32[]{:S(2)}, u32[]{:S(2)}) %collective-permute-start.1) | collective-permute-done | bytes 524320 | tf_op jit(solution)/shard_map/ppermute | solution.py:18
  82.8 1.0 fusion.24
  83.7 2.0 %copy.38 = bf16[1024,256]{1,0:T(8,128)(2,1)} copy(bf16[1024,256]{0,1:T(8,128)(2,1)} %fusion.24) | data formatting | bytes 1048576 | tf_op jit(solution)/shard_map/convert_element_type | solution.py:120
  85.8 5.6 %all-to-all-start.2 = ((bf16[32,32,256]{2,1,0:T(8,128)(2,1)}), bf16[32,32,256]{2,1,0:T(8,128)(2,1)}, u32[]{:S(2)}, u32[]{:S(2)}) async-start(bf16[32,32,256]{2,1,0:T(8,128)(2,1)} %bitcast.130), calls=%async_computation.2 | async-start | bytes 1048576 | tf_op jit(solution)/shard_map/all_to_all | solution.py:14
  91.6 9.4 %all-gather.2.cloned.1.call-done = bf16[512,4096]{1,0:T(8,128)(2,1)} async-done(((bf16[512,512]{1,0:T(8,128)(2,1)}), bf16[512,4096]{1,0:T(8,128)(2,1)}) %all-gather.2.cloned.1.call-update) | async-done | bytes 4194320 | tf_op jit(solution)/shard_map/all_gather | solution.py:82
  101.0 4.6 %multiply_reduce_fusion.1 = (f32[512]{0:T(512)S(1)}, bf16[1,192,512]{2,1,0:T(8,128)(2,1)}, bf16[1,192,512]{2,1,0:T(8,128)(2,1)}) fusion(bf16[1,192,512]{2,1,0:T(8,128)(2,1)S(1)} %copy-done.28, bf16[1,192,512]{2,1,0:T(8,128)(2,1)} %param.16, f32[512]{0:T(512)S(1)} %convert_reduce_fusion, bf16[512,4096]{1,0:T(8,128)(2,1)} %all-gather.2.cloned.1.call-done, ...), kind=kOutput, calls=%fused_computation.66 | convolution fusion | flops 807173632 | bytes 6557696 | tf_op jit(solution)/shard_map/dot_general | solution.py:125
  105.7 0.7 all_to_all.21
  106.4 2.2 %all-to-all-done.2 = bf16[32,32,256]{2,1,0:T(8,128)(2,1)} async-done(((bf16[32,32,256]{2,1,0:T(8,128)(2,1)}), bf16[32,32,256]{2,1,0:T(8,128)(2,1)}, u32[]{:S(2)}, u32[]{:S(2)}) %all-to-all-start.2) | async-done | bytes 524320 | tf_op jit(solution)/shard_map/all_to_all | solution.py:14
  108.6 8.7 %all-to-all-start.3 = ((f32[64,1,8]{2,1,0:T(1,128)}), f32[64,1,8]{2,1,0:T(1,128)S(1)}, u32[]{:S(2)}, u32[]{:S(2)}) async-start(f32[64,1,8]{2,1,0:T(1,128)} %bitcast.31), calls=%async_computation.3 | async-start | bytes 65536 | tf_op jit(solution)/shard_map/all_to_all | solution.py:14
  117.3 1.4 fusion.19
  118.8 0.7 reshape.71
  119.4 1.1 reduce_sum.141
  120.6 4.6 %all-to-all-done.3 = f32[64,1,8]{2,1,0:T(1,128)S(1)} async-done(((f32[64,1,8]{2,1,0:T(1,128)}), f32[64,1,8]{2,1,0:T(1,128)S(1)}, u32[]{:S(2)}, u32[]{:S(2)}) %all-to-all-start.3) | async-done | bytes 2080 | tf_op jit(solution)/shard_map/all_to_all | solution.py:14
  125.7 0.7 reduce.6
  127.2 0.7 broadcast_in_dim.229
  127.9 4.5 %all-to-all-start.4 = ((bf16[8,32,384]{2,1,0:T(8,128)(2,1)}), bf16[8,32,384]{2,1,0:T(8,128)(2,1)S(1)}, u32[]{:S(2)}, u32[]{:S(2)}) async-start(bf16[8,32,384]{2,1,0:T(8,128)(2,1)} %broadcast_in_dim.229), calls=%async_computation.4 | async-start | bytes 393216 | tf_op jit(solution)/shard_map/all_to_all | solution.py:14
  132.4 4.5 %fusion = bf16[1,192,4096]{2,1,0:T(8,128)(2,1)} fusion(bf16[512,4096]{1,0:T(8,128)(2,1)} %all-gather.2.cloned.1.call-done, bf16[1,192,512]{2,1,0:T(8,128)(2,1)S(1)} %copy-done.28, f32[512]{0:T(512)S(1)} %convert_reduce_fusion, bf16[1,192,512]{2,1,0:T(8,128)(2,1)} %param.16), kind=kOutput, calls=%fused_computation.5 | convolution fusion | flops 806977536 | bytes 6162432 | tf_op jit(solution)/shard_map/dot_general | solution.py:136
  136.9 6.0 %all-to-all-done.4 = bf16[8,32,384]{2,1,0:T(8,128)(2,1)S(1)} async-done(((bf16[8,32,384]{2,1,0:T(8,128)(2,1)}), bf16[8,32,384]{2,1,0:T(8,128)(2,1)S(1)}, u32[]{:S(2)}, u32[]{:S(2)}) %all-to-all-start.4) | async-done | bytes 196640 | tf_op jit(solution)/shard_map/all_to_all | solution.py:14
  (102 shorter events, 7.1 us)
Async XLA Ops:
  7.2 93.8 %copy-start = (bf16[1,192,4096]{2,1,0:T(8,128)(2,1)S(1)}, bf16[1,192,4096]{2,1,0:T(8,128)(2,1)}, u32[]{:S(2)}) copy-start(bf16[1,192,4096]{2,1,0:T(8,128)(2,1)} %param.15) | copy-start | bytes 4718596
  7.2 93.8 %all-gather.2.cloned.1.call-start = ((), (), s32[]{:S(2)}) async-start(), calls=%async_computation.5 | async-start | bytes 4718592 | tf_op jit(solution)/shard_map/all_gather | solution.py:82
  7.2 3.0 %copy-start.5 = (s32[512]{0:T(512)}, s32[512]{0:T(512)S(1)}, u32[]{:S(2)}) copy-start(s32[512]{0:T(512)S(1)} %get-tuple-element.52) | copy-start | bytes 6148
  7.3 3.0 %copy-start.7 = (s32[512]{0:T(512)}, s32[512]{0:T(512)S(1)}, u32[]{:S(2)}) copy-start(s32[512]{0:T(512)S(1)} %get-tuple-element.55) | copy-start | bytes 6148
  7.3 4.6 %copy-start.25 = (pred[512]{0:T(512)(128)(4,1)}, pred[512]{0:T(512)(128)(4,1)S(1)}, u32[]{:S(2)}) copy-start(pred[512]{0:T(512)(128)(4,1)S(1)} %get-tuple-element.56) | copy-start | bytes 1540
  8.3 2.0 %copy-start.11 = (s32[32]{0:T(128)}, s32[32]{0:T(128)S(1)}, u32[]{:S(2)}) copy-start(s32[32]{0:T(128)S(1)} %get-tuple-element.31) | copy-start | bytes 388
  8.3 2.0 %copy-start.13 = (s32[32]{0:T(128)}, s32[32]{0:T(128)S(1)}, u32[]{:S(2)}) copy-start(s32[32]{0:T(128)S(1)} %get-tuple-element.32) | copy-start | bytes 388
  8.3 2.0 %copy-start.15 = (s32[32]{0:T(128)}, s32[32]{0:T(128)S(1)}, u32[]{:S(2)}) copy-start(s32[32]{0:T(128)S(1)} %get-tuple-element.33) | copy-start | bytes 388
  8.3 2.0 %copy-start.17 = (s32[32]{0:T(128)}, s32[32]{0:T(128)S(1)}, u32[]{:S(2)}) copy-start(s32[32]{0:T(128)S(1)} %get-tuple-element.34) | copy-start | bytes 388
  8.3 2.0 %copy-start.19 = (s32[32]{0:T(128)}, s32[32]{0:T(128)S(1)}, u32[]{:S(2)}) copy-start(s32[32]{0:T(128)S(1)} %get-tuple-element.35) | copy-start | bytes 388
  12.2 42.0 %copy-start.3 = (bf16[32,1024]{1,0:T(8,128)(2,1)S(1)}, bf16[32,1024]{1,0:T(8,128)(2,1)}, u32[]{:S(2)}) copy-start(bf16[32,1024]{1,0:T(8,128)(2,1)} %param.18) | copy-start | bytes 196612
  12.2 42.1 %copy-start.4 = (bf16[32,1024]{1,0:T(8,128)(2,1)S(1)}, bf16[32,1024]{1,0:T(8,128)(2,1)}, u32[]{:S(2)}) copy-start(bf16[32,1024]{1,0:T(8,128)(2,1)} %param.21) | copy-start | bytes 196612
  48.8 22.1 %all-to-all-start.1 = ((bf16[32,32,256]{2,1,0:T(8,128)(2,1)}), bf16[32,32,256]{2,1,0:T(8,128)(2,1)S(1)}, u32[]{:S(2)}, u32[]{:S(2)}) async-start(bf16[32,32,256]{2,1,0:T(8,128)(2,1)} %broadcast_in_dim.216), calls=%async_computation.1 | async-start | bytes 1048576 | tf_op jit(solution)/shard_map/all_to_all | solution.py:14
  70.9 5.6 %copy-start.1 = (bf16[32,32,256]{2,1,0:T(8,128)(2,1)}, bf16[32,32,256]{2,1,0:T(8,128)(2,1)S(1)}, u32[]{:S(2)}) copy-start(bf16[32,32,256]{2,1,0:T(8,128)(2,1)S(1)} %all-to-all-done.1) | copy-start | bytes 1572868
  70.9 3.8 %collective-permute-start = (bf16[1024,256]{1,0:T(8,128)(2,1)S(1)}, bf16[1024,256]{1,0:T(8,128)(2,1)S(1)}, u32[]{:S(2)}, u32[]{:S(2)}) collective-permute-start(bf16[1024,256]{1,0:T(8,128)(2,1)S(1)} %bitcast.131), channel_id=1, source_target_pairs={{0,8},{8,0},{1,9},{9,1},{2,10},{10,2},{3,11},{11,3},{4,12},{12,4},... | collective-permute-start | bytes 1572872 | tf_op jit(solution)/shard_map/ppermute | solution.py:18
  78.8 22.2 %copy-start.28 = (bf16[1,192,512]{2,1,0:T(8,128)(2,1)S(1)}, bf16[1,192,512]{2,1,0:T(8,128)(2,1)}, u32[]{:S(2)}) copy-start(bf16[1,192,512]{2,1,0:T(8,128)(2,1)} %param.17) | copy-start | bytes 589828
  78.8 3.9 %collective-permute-start.1 = (bf16[1024,256]{0,1:T(8,128)(2,1)S(1)}, bf16[1024,256]{0,1:T(8,128)(2,1)S(1)}, u32[]{:S(2)}, u32[]{:S(2)}) collective-permute-start(bf16[1024,256]{0,1:T(8,128)(2,1)S(1)} %fusion.25), channel_id=1, source_target_pairs={{0,8},{8,0},{1,9},{9,1},{2,10},{10,2},{3,11},{11,3},{4,12},{12,4},... | collective-permute-start | bytes 1572872 | tf_op jit(solution)/shard_map/ppermute | solution.py:18
  85.8 22.9 %all-to-all-start.2 = ((bf16[32,32,256]{2,1,0:T(8,128)(2,1)}), bf16[32,32,256]{2,1,0:T(8,128)(2,1)}, u32[]{:S(2)}, u32[]{:S(2)}) async-start(bf16[32,32,256]{2,1,0:T(8,128)(2,1)} %bitcast.130), calls=%async_computation.2 | async-start | bytes 1048576 | tf_op jit(solution)/shard_map/all_to_all | solution.py:14
  91.6 25.7 %copy-start.2 = (bf16[32,32,256]{2,1,0:T(8,128)(2,1)S(1)}, bf16[32,32,256]{2,1,0:T(8,128)(2,1)}, u32[]{:S(2)}) copy-start(bf16[32,32,256]{2,1,0:T(8,128)(2,1)} %copy-done.1) | copy-start | bytes 1572868
  105.6 20.9 %copy-start.6 = (s32[512]{0:T(512)S(1)}, s32[512]{0:T(512)}, u32[]{:S(2)}) copy-start(s32[512]{0:T(512)} %copy-done.5) | copy-start | bytes 6148
  105.6 20.9 %copy-start.8 = (s32[512]{0:T(512)S(1)}, s32[512]{0:T(512)}, u32[]{:S(2)}) copy-start(s32[512]{0:T(512)} %copy-done.7) | copy-start | bytes 6148
  105.6 20.9 %copy-start.10 = (s32[32]{0:T(128)S(1)}, s32[32]{0:T(128)}, u32[]{:S(2)}) copy-start(s32[32]{0:T(128)} %copy-done.9) | copy-start | bytes 388
  105.6 20.9 %copy-start.12 = (s32[32]{0:T(128)S(1)}, s32[32]{0:T(128)}, u32[]{:S(2)}) copy-start(s32[32]{0:T(128)} %copy-done.11) | copy-start | bytes 388
  105.6 20.9 %copy-start.14 = (s32[32]{0:T(128)S(1)}, s32[32]{0:T(128)}, u32[]{:S(2)}) copy-start(s32[32]{0:T(128)} %copy-done.13) | copy-start | bytes 388
  105.6 20.9 %copy-start.16 = (s32[32]{0:T(128)S(1)}, s32[32]{0:T(128)}, u32[]{:S(2)}) copy-start(s32[32]{0:T(128)} %copy-done.15) | copy-start | bytes 388
  105.7 20.9 %copy-start.18 = (s32[32]{0:T(128)S(1)}, s32[32]{0:T(128)}, u32[]{:S(2)}) copy-start(s32[32]{0:T(128)} %copy-done.17) | copy-start | bytes 388
  105.7 20.9 %copy-start.20 = (s32[32]{0:T(128)S(1)}, s32[32]{0:T(128)}, u32[]{:S(2)}) copy-start(s32[32]{0:T(128)} %copy-done.19) | copy-start | bytes 388
  105.7 20.9 %copy-start.22 = (s32[32]{0:T(128)S(1)}, s32[32]{0:T(128)}, u32[]{:S(2)}) copy-start(s32[32]{0:T(128)} %copy-done.21) | copy-start | bytes 388
  105.7 20.9 %copy-start.24 = (s32[32]{0:T(128)S(1)}, s32[32]{0:T(128)}, u32[]{:S(2)}) copy-start(s32[32]{0:T(128)} %copy-done.23) | copy-start | bytes 388
  105.7 20.9 %copy-start.26 = (pred[512]{0:T(512)(128)(4,1)S(1)}, pred[512]{0:T(512)(128)(4,1)}, u32[]{:S(2)}) copy-start(pred[512]{0:T(512)(128)(4,1)} %copy-done.25) | copy-start | bytes 1540
  108.6 16.5 %all-to-all-start.3 = ((f32[64,1,8]{2,1,0:T(1,128)}), f32[64,1,8]{2,1,0:T(1,128)S(1)}, u32[]{:S(2)}, u32[]{:S(2)}) async-start(f32[64,1,8]{2,1,0:T(1,128)} %bitcast.31), calls=%async_computation.3 | async-start | bytes 65536 | tf_op jit(solution)/shard_map/all_to_all | solution.py:14
  127.9 15.0 %all-to-all-start.4 = ((bf16[8,32,384]{2,1,0:T(8,128)(2,1)}), bf16[8,32,384]{2,1,0:T(8,128)(2,1)S(1)}, u32[]{:S(2)}, u32[]{:S(2)}) async-start(bf16[8,32,384]{2,1,0:T(8,128)(2,1)} %broadcast_in_dim.229), calls=%async_computation.4 | async-start | bytes 393216 | tf_op jit(solution)/shard_map/all_to_all | solution.py:14
  (4 other events, 7.9 us)
Sparse Core Ops, SparseCore 0:
  47.3 53.6 all-gather.1

commit v2 on v1

v2 whole, which is shorter than its diff:
```python
import functools

import jax
import jax.numpy as jnp
from jax import lax
from jax.experimental import pallas as pl
from jax.experimental.pallas import tpu as pltpu
from jax.sharding import Mesh, PartitionSpec as P


H = 64
KVH = 4
HD = 128
GX = ("z", "x", "c")
ZX = ("z", "x")
NT = (((1,), (1,)), ((), ()))
TN = (((0,), (0,)), ((), ()))
F32 = jnp.float32
BF16 = jnp.bfloat16


def exchange(values, axes):
    return lax.all_to_all(values, axes, split_axis=0, concat_axis=0, tiled=True)


def to_partner(values):
    return lax.ppermute(values, "c", [(0, 1), (1, 0)])


def along(values, step):
    n = lax.axis_size("ta")
    return lax.ppermute(values, "ta", [(i, (i + step) % n) for i in range(n)])


def iota(shape, dim):
    return lax.broadcasted_iota(jnp.int32, shape, dim)


def vmem():
    return pl.BlockSpec(memory_space=pltpu.VMEM)


def smem():
    return pl.BlockSpec(memory_space=pltpu.SMEM)


def call(body, outs, ins, cost):
    return pl.pallas_call(
        body,
        out_shape=outs,
        in_specs=[smem()] + [vmem()] * (len(ins) - 1),
        out_specs=jax.tree.map(lambda _: vmem(), outs),
        cost_estimate=pl.CostEstimate(flops=cost, bytes_accessed=cost // 100, transcendentals=0),
    )(*ins)


def pack_body(where, kept, ids, gates, d_out, keys, values, message, ranks):
    rows, top = ids.shape
    slots = message.shape[0]
    tok_dev, width = d_out.shape
    cap = 8
    head = pl.multiple_of(where[0] * HD, HD)
    lane = iota((rows, slots), 1)
    expert = lane // cap
    named = jnp.zeros((rows, slots), F32)
    weight = jnp.zeros((rows, slots), F32)
    for j in range(top):
        hit = ids[:, j : j + 1] == expert
        named = jnp.where(hit, 1.0, named)
        weight = jnp.where(hit, gates[:, j : j + 1].astype(F32), weight)
    below = (iota((rows, rows), 0) > iota((rows, rows), 1)).astype(F32).astype(BF16)
    rank = jnp.dot(below, named.astype(BF16), preferred_element_type=F32)
    place = (lane % cap).astype(F32)
    taken = jnp.where((named > 0.0) & (rank == place), 1.0, 0.0)
    pick = jnp.where(kept[...] % tok_dev == iota((rows, tok_dev), 1), 1.0, 0.0).astype(BF16)
    picked = jnp.dot(pick, d_out[...], preferred_element_type=F32).astype(BF16)
    message[:, :width] = lax.dot_general(
        taken.astype(BF16), picked, TN, preferred_element_type=F32
    ).astype(BF16)
    kv = jnp.concatenate([keys[:, pl.ds(head, HD)], values[:, pl.ds(head, HD)]], axis=1)
    kv = kv.astype(F32)
    pair = jnp.concatenate(
        [
            jnp.concatenate([kv[0:8], kv[16:24]], axis=0),
            jnp.concatenate([kv[8:16], kv[24:32]], axis=0),
        ],
        axis=1,
    ).astype(BF16)
    message[:, width : width + 4 * HD] = jnp.broadcast_to(
        pair[None], (slots // 16, 16, 4 * HD)
    ).reshape(slots, 4 * HD)
    message[:, width + 4 * HD :] = lax.dot_general(
        (taken * weight).astype(BF16), jnp.ones((rows, HD), BF16), TN, preferred_element_type=F32
    ).astype(BF16)
    found = jnp.zeros((rows, top), F32)
    for j in range(top):
        mine = jnp.where((ids[:, j : j + 1] == expert) & (taken > 0.0), place, 0.0)
        found = jnp.where(
            iota((rows, top), 1) == j, jnp.sum(mine, axis=1, keepdims=True), found
        )
    ranks[...] = found.astype(jnp.int32)


def attention_body(where, query, grad, mine, other, d_query, keep, send):
    core, block = where[0], where[1]
    keep_dev = query.shape[0]
    heads = query.shape[1] // HD
    rows = keep_dev * heads
    half = mine.shape[0]
    scale = HD ** (-0.5)

    def stacked(ref):
        return jnp.concatenate([ref[:, g * HD : (g + 1) * HD] for g in range(heads)], axis=0)

    q = stacked(query)
    o = stacked(grad)
    pieces = []
    query_pos = block * keep_dev + iota((rows, half), 0) % keep_dev
    row = iota((rows, half), 1)
    key_base = row // 8 * keep_dev + row % 8
    for ref, owner in ((mine, core), (other, 1 - core)):
        for q8 in range(2):
            key = ref[:, q8 * 2 * HD : q8 * 2 * HD + HD]
            value = ref[:, q8 * 2 * HD + HD : q8 * 2 * HD + 2 * HD]
            s = lax.dot_general(q, key, NT, preferred_element_type=F32) * scale
            s = jnp.where(key_base + (owner * 16 + q8 * 8) <= query_pos, s, -1e30)
            pieces.append((key, value, s, owner * 2 + q8))
    top = functools.reduce(
        jnp.maximum, [jnp.max(s, axis=1, keepdims=True) for _, _, s, _ in pieces]
    )
    expo = [jnp.exp(s - top) for _, _, s, _ in pieces]
    total = sum(jnp.sum(e, axis=1, keepdims=True) for e in expo)
    inv = 1.0 / total
    probs = [e * inv for e in expo]
    dps = [
        lax.dot_general(o, value, NT, preferred_element_type=F32) for _, value, _, _ in pieces
    ]
    mean = sum(jnp.sum(p * dp, axis=1, keepdims=True) for p, dp in zip(probs, dps))
    dq = jnp.zeros((rows, HD), F32)
    for (key, _, _, at), p, dp in zip(pieces, probs, dps):
        ds = (p * (dp - mean)).astype(BF16)
        dq = dq + jnp.dot(ds, key, preferred_element_type=F32)
        dk = lax.dot_general(ds, q, TN, preferred_element_type=F32) * scale
        dv = lax.dot_general(p.astype(BF16), o, TN, preferred_element_type=F32)
        for which, part in ((0, dk), (1, dv)):
            split = part.reshape(half // 16, 2, 8, HD)
            own = jnp.where(core == 0, split[:, 0], split[:, 1]).reshape(half // 2, HD)
            rest = jnp.where(core == 0, split[:, 1], split[:, 0]).reshape(half // 2, HD)
            lanes = pl.ds(pl.multiple_of(at * 2 * HD + which * HD, HD), HD)
            keep[:, lanes] = own
            send[:, lanes] = rest.astype(BF16)
    dq = (dq * scale).astype(BF16)
    for g in range(heads):
        d_query[:, g * HD : (g + 1) * HD] = dq[g * keep_dev : (g + 1) * keep_dev]


def shard_list(refs):
    own, r1, r2, r3, l1, l2, l3, r4, l4 = refs
    return ((0, own), (7, r1), (1, l1), (6, r2), (2, l2), (5, r3), (3, l3)), (r4, l4)


def expert_body(where, weight, gate_pre, up_pre, slot_gate, *refs):
    shards, last = shard_list(refs[:9])
    d_gate, d_up, weighted, dots = refs[9:]
    me = where[0]
    width = refs[0].shape[1]
    n = weight.shape[1] // width
    slots = refs[0].shape[0]

    def block(k):
        return weight[:, pl.ds(pl.multiple_of(lax.rem(me + k, n) * width, width), width)]

    z = jnp.zeros((weight.shape[0], slots), F32)
    for k, ref in shards:
        z = z + lax.dot_general(block(k), ref[...], NT, preferred_element_type=F32)
    z = z + jnp.concatenate(
        [lax.dot_general(block(4), ref[...], NT, preferred_element_type=F32) for ref in last],
        axis=1,
    )
    g = gate_pre[...].astype(F32)
    u = up_pre[...].astype(F32)
    sig = 1.0 / (1.0 + jnp.exp(-g))
    act = g * sig
    hidden = act * u
    dots[...] = jnp.sum(hidden * z, axis=0, keepdims=True)
    one = jnp.where(iota((8, HD), 1) == 0, 1.0, 0.0).astype(BF16)
    scale = lax.dot_general(one, slot_gate[...], NT, preferred_element_type=F32)[0:1]
    grad_hidden = z * scale
    d_up[...] = (grad_hidden * act).astype(BF16)
    d_gate[...] = (grad_hidden * u * sig * (1.0 + g * (1.0 - sig))).astype(BF16)
    weighted[...] = (hidden * scale).astype(BF16)


def down_body(where, weighted, *refs):
    shards, last = shard_list(refs[:9])
    out = refs[9]
    me = where[0]
    width = refs[0].shape[1]
    n = out.shape[1] // width
    w = weighted[...]

    def place(k):
        return pl.ds(pl.multiple_of(lax.rem(me + k, n) * width, width), width)

    for k, ref in shards:
        out[:, place(k)] = jnp.dot(w, ref[...], preferred_element_type=F32).astype(BF16)
    half = last[0].shape[0]
    out[:, place(4)] = (
        jnp.dot(w[:, :half], last[0][...], preferred_element_type=F32)
        + jnp.dot(w[:, half:], last[1][...], preferred_element_type=F32)
    ).astype(BF16)


def middle_body(where, terms, out):
    experts = out.shape[0]
    total = jnp.sum(terms[...], axis=0)
    slots = total.shape[1]
    cap = slots // experts
    spread = jnp.where(
        iota((experts, slots), 1) // cap == iota((experts, slots), 0), total, 0.0
    )
    lanes = jnp.where(iota((slots, HD), 0) % cap == iota((slots, HD), 1), 1.0, 0.0)
    out[...] = jnp.dot(
        spread, lanes, preferred_element_type=F32, precision=lax.Precision.HIGHEST
    )[:, None, :]


def gates_body(where, ids, ranks, returned, out):
    rows, top = ids.shape
    experts = returned.shape[0]
    pick = jnp.concatenate(
        [
            jnp.where(ids[:, j : j + 1] == iota((rows, experts), 1), 1.0, 0.0)
            for j in range(top)
        ],
        axis=0,
    )
    found = jnp.dot(
        pick,
        returned[...].reshape(experts, HD),
        preferred_element_type=F32,
        precision=lax.Precision.HIGHEST,
    )
    result = jnp.zeros((rows, top), F32)
    for j in range(top):
        hit = jnp.where(
            iota((rows, HD), 1) == ranks[:, j : j + 1], found[j * rows : (j + 1) * rows], 0.0
        )
        result = jnp.where(iota((rows, top), 1) == j, jnp.sum(hit, axis=1, keepdims=True), result)
    out[...] = result


def heads_body(where, terms, d_key, d_value):
    n = terms.shape[0]
    per = n // KVH
    for h in range(KVH):
        both = sum(terms[h * per + i].astype(F32) for i in range(per))
        for p in range(4):
            tokens = slice(p * 8, (p + 1) * 8)
            d_key[tokens, h * HD : (h + 1) * HD] = both[:, p * 2 * HD : p * 2 * HD + HD]
            d_value[tokens, h * HD : (h + 1) * HD] = both[:, p * 2 * HD + HD : (p + 1) * 2 * HD]


def on_device(
    d_out, kept, expert_ids, gates, down_weight, gate_pre, up_pre, query, keys, values, d_attn
):
    core = lax.axis_index("c")
    chips = lax.axis_size(ZX)
    me = lax.axis_index("ta")
    n_experts = lax.axis_size(GX)
    n_ta = lax.axis_size("ta")
    keep_dev = kept.shape[0]
    width = d_out.shape[1]
    top = expert_ids.shape[1]
    slots = gate_pre.shape[2]
    cap = slots // n_experts
    hidden = gate_pre.shape[1]
    struct = jax.ShapeDtypeStruct

    local_heads = query.shape[1] // HD
    first_kv = (me * local_heads // (H // KVH)).astype(jnp.int32).reshape(1)
    message, ranks = call(
        pack_body,
        (struct((slots, width + 5 * HD), BF16), struct((keep_dev, top), jnp.int32)),
        (first_kv, kept.reshape(keep_dev, 1), expert_ids, gates, d_out, keys, values),
        200_000_000,
    )
    arrived = exchange(message.reshape(n_experts, cap, -1), GX).reshape(slots, -1)
    own = arrived[:, :width]
    kv_mine = arrived[:, width : width + 4 * HD]
    slot_gate = arrived[:, width + 4 * HD :]

    r1, l1 = along(own, 1), along(own, -1)
    kv_other = to_partner(kv_mine)
    where = jnp.stack([core, lax.axis_index(GX)]).astype(jnp.int32)
    d_query, keep, send = call(
        attention_body,
        (
            struct((keep_dev, local_heads * HD), BF16),
            struct((slots // 2, 8 * HD), F32),
            struct((slots // 2, 8 * HD), BF16),
        ),
        (where, query, d_attn, kv_mine, kv_other),
        4_000_000_000,
    )
    r1, l1, send = lax.optimization_barrier((r1, l1, send))
    r2, l2 = along(r1, 1), along(l1, -1)
    chip_part = (keep + to_partner(send).astype(F32)).astype(BF16)
    summed = exchange(chip_part.reshape(chips, cap, 8 * HD), ZX)
    r3, l3 = along(r2, 1), along(l2, -1)
    r4, l4 = along(r3[: slots // 2], 1), along(l3[slots // 2 :], -1)
    shards = (own, r1, r2, r3, l1, l2, l3, r4, l4)
    owned = jnp.sum(summed.astype(F32), axis=0).astype(BF16)
    copies = exchange(jnp.broadcast_to(owned[None], (n_ta,) + owned.shape), "ta")
    d_key, d_value = call(
        heads_body,
        (struct((keep_dev, KVH * HD), F32), struct((keep_dev, KVH * HD), F32)),
        (where, copies),
        1_000_000,
    )

    at = me.astype(jnp.int32).reshape(1)
    d_gate, d_up, weighted, dots = call(
        expert_body,
        (
            struct((hidden, slots), BF16),
            struct((hidden, slots), BF16),
            struct((hidden, slots), BF16),
            struct((1, slots), F32),
        ),
        (at, down_weight[0], gate_pre[0], up_pre[0], slot_gate) + shards,
        3_000_000_000,
    )
    d_down = call(
        down_body, struct(down_weight.shape[1:], BF16), (at, weighted) + shards, 3_000_000_000
    )
    terms = exchange(jnp.broadcast_to(dots[None], (n_ta, 1, slots)), "ta")
    sums = call(middle_body, struct((n_experts, 1, HD), F32), (at, terms), 1_000_000)
    returned = exchange(sums, GX)
    d_gates = call(
        gates_body, struct((keep_dev, top), F32), (at, expert_ids, ranks, returned), 1_000_000
    )
    return (d_down[None], d_gate[None], d_up[None], d_gates, d_query, d_key, d_value)


def solution(mesh):
    shape = dict(mesh.shape)
    fine = Mesh(mesh.devices.reshape(8, shape["gx"] // 16, 2, shape["ta"]), GX + ("ta",))
    in_specs = (
        P(GX, "ta"),
        P(GX),
        P(GX, None),
        P(GX, None),
        P(GX, "ta", None),
        P(GX, "ta", None),
        P(GX, "ta", None),
        P(GX, "ta"),
        P(GX, None),
        P(GX, None),
        P(GX, "ta"),
    )
    out_specs = (
        P(GX, "ta", None),
        P(GX, "ta", None),
        P(GX, "ta", None),
        P(GX, None),
        P(GX, "ta"),
        P(GX, None),
        P(GX, None),
    )
    return jax.shard_map(
        on_device, mesh=fine, in_specs=in_specs, out_specs=out_specs, check_vma=False
    )
```

time: 154 us -> 191 us (1.24)
  starting transfers between devices: 28.3 us -> 51.9 us
  Pallas kernels: 0 us -> 22.5 us
  matrix products: 15.4 us -> 0 us
  waiting for transfers between devices: 42.4 us -> 57.3 us
  between operations: 14.7 us -> 0.9 us
  blocking collectives: 34.1 us -> 45.4 us
  other arithmetic: 7.96 us -> 1.61 us
    ppermute x0 -> x8, waiting for transfers between devices: none -> 28.7 us  [along(): return lax.ppermute(values, 'ta', [(i, (i + step) % n) for i in range(n)])]
    ppermute x0 -> x8, starting transfers between devices: none -> 28.4 us  [along(): return lax.ppermute(values, 'ta', [(i, (i + step) % n) for i in range(n)])]
    pallas_call x0 -> x7, Pallas kernels: none -> 22.5 us  [call(): pl.pallas_call(body, out_shape=outs, in_specs=[smem()] + [vmem()] * (len(...]
    dot_general x9 -> x0, matrix products: 15.4 us -> none  [the longest x1 4.61 us: on_device(): lax.dot_general(down_weight[0], slot_rows, nt, preferred_element_type=jnp...]
    all_to_all x1, blocking collectives: 34.1 us -> 45.4 us  [exchange(): return lax.all_to_all(values, axes, split_axis=0, concat_axis=0, tiled=True)]
    all_gather x1 -> x0, waiting for transfers between devices: 9.39 us -> none  [on_device(): slot_rows = lax.all_gather(arrived[:, :width], 'ta', axis=1, tiled=True)]
    unnamed x60 -> x31, local copies, waits for them, and re-layouts: 0.26 us -> 5.5 us
    all_to_all x4, starting transfers between devices: 24.2 us -> 19.7 us  [exchange(): return lax.all_to_all(values, axes, split_axis=0, concat_axis=0, tiled=True)]
  transfers between devices with their start and end apart: 7 -> 14, of which waited for: 7 -> 9; matrix products, arithmetic and copies ran while one was open for 14% -> 3% of each run, Pallas kernels for 0% -> 10%
where the time goes in v2:
time: 191 us; the launch traced here: 189 us
  waiting for transfers between devices  57.3 us (30%)
  starting transfers between devices  51.9 us (27%)
  blocking collectives  45.4 us (24%)
  Pallas kernels  22.5 us (12%)
  local copies, waits for them, and re-layouts  9.57 us (5%)
    all_to_all x1, blocking collectives, exchange(): return lax.all_to_all(values, axes, split_axis=0, concat_axis=0, tiled=True)  45.4 us
    ppermute x8, waiting for transfers between devices, along(): return lax.ppermute(values, 'ta', [(i, (i + step) % n) for i in range(n)])  28.7 us
    all_to_all x4, waiting for transfers between devices, exchange(): return lax.all_to_all(values, axes, split_axis=0, concat_axis=0, tiled=True)  28.6 us
    ppermute x8, starting transfers between devices, along(): return lax.ppermute(values, 'ta', [(i, (i + step) % n) for i in range(n)])  28.4 us
    pallas_call x7, Pallas kernels, call(): pl.pallas_call(body, out_shape=outs, in_specs=[smem()] + [vmem()] * (len(...  22.5 us
    all_to_all x4, starting transfers between devices, exchange(): return lax.all_to_all(values, axes, split_axis=0, concat_axis=0, tiled=True)  19.7 us
    unnamed x31, local copies, waits for them, and re-layouts  5.5 us
    ppermute x2, starting transfers between devices, to_partner(): return lax.ppermute(values, 'c', [(0, 1), (1, 0)])  3.84 us
  transfers between devices with their start and end apart: 14, of which 9 were waited for; matrix products, arithmetic and copies ran while one was open for 3% of the time, Pallas kernels for 10%

profile of v2, /device:TPU:6, one launch (start us, length us, event | category | flops | bytes accessed | tf_op | source)
XLA Modules:
  0.0 189.1 jit_solution(185824429785970389)
XLA Ops:
  2.0 1.4 copy.19.ids
  4.7 2.9 %shard_map.162 = (bf16[512,1152]{1,0:T(8,128)(2,1)}, s32[32,8]{1,0:T(8,128)}) custom-call(s32[1]{0:T(128)} %bitcast.4.where, s32[32,1]{1,0:T(8,128)} %copy.18.kept, s32[32,8]{1,0:T(8,128)} %copy.19.ids, bf16[32,8]{1,0:T(8,128)(2,1)} %copy.20.gates, bf16[256,512]{1,0:T(8,128)(2,1)} %d_out.1, bf16[32,512]{1,0:T(8,128)(2,1)} %keys.1, bf16[32,512]{1,0:T(8,128)(2,1)} %values.1), custom_call_target="tpu_custom_call" | custom-call | flops 200000000 | bytes 2000000 | tf_op jit(solution)/shard_map/pallas_call | solution.py:48
  7.6 45.4 %all_to_all.25 = bf16[64,8,1152]{2,1,0:T(8,128)(2,1)S(1)} all-to-all(bf16[64,8,1152]{2,1,0:T(8,128)(2,1)} %bitcast.18), channel_id=1, replica_groups=mesh['z'=8,'x'=4,'c'=2,'ta'=8] {'z','x','c'}, dimensions={0} | all-to-all | bytes 2359296 | tf_op jit(solution)/shard_map/all_to_all | solution.py:23
  53.1 1.9 %collective-permute-start.2 = (bf16[512,512]{1,0:T(8,128)(2,1)S(1)}, bf16[512,512]{1,0:T(8,128)(2,1)}, u32[]{:S(2)}, u32[]{:S(2)}) collective-permute-start(bf16[512,512]{1,0:T(8,128)(2,1)S(1)} %get-tuple-element.42.mine), channel_id=1, source_target_pairs={{0,8},{8,0},{1,9},{9,1},{2,10},{10,2},{3,11},{11,3},{4,12},{12,4},... | collective-permute-start | bytes 1572872 | tf_op jit(solution)/shard_map/ppermute | solution.py:27
  55.1 5.4 %collective-permute-start.1 = (bf16[512,512]{1,0:T(8,128)(2,1)S(1)}, bf16[512,512]{1,0:T(8,128)(2,1)S(1)}, u32[]{:S(2)}, u32[]{:S(2)}) collective-permute-start(bf16[512,512]{1,0:T(8,128)(2,1)S(1)} %get-tuple-element.43.refs_0_), channel_id=1, source_target_pairs={{0,7},{1,0},{2,1},{3,2},{4,3},{5,4},{6,5},{7,6},{8,15},{9,8},{10,9... | collective-permute-start | bytes 1572872 | tf_op jit(solution)/shard_map/ppermute | solution.py:32
  60.4 1.9 %collective-permute-start = (bf16[512,512]{1,0:T(8,128)(2,1)S(1)}, bf16[512,512]{1,0:T(8,128)(2,1)S(1)}, u32[]{:S(2)}, u32[]{:S(2)}) collective-permute-start(bf16[512,512]{1,0:T(8,128)(2,1)S(1)} %get-tuple-element.43.refs_0_), channel_id=1, source_target_pairs={{0,1},{1,2},{2,3},{3,4},{4,5},{5,6},{6,7},{7,0},{8,9},{9,10},{10,1... | collective-permute-start | bytes 1572872 | tf_op jit(solution)/shard_map/ppermute | solution.py:32
  63.0 4.8 %shard_map.163 = (bf16[32,1024]{1,0:T(8,128)(2,1)}, f32[256,1024]{1,0:T(8,128)}, bf16[256,1024]{1,0:T(8,128)(2,1)}) custom-call(s32[2]{0:T(128)} %pad_add_fusion.where, bf16[32,1024]{1,0:T(8,128)(2,1)} %query.1, bf16[32,1024]{1,0:T(8,128)(2,1)} %grad.1, bf16[512,512]{1,0:T(8,128)(2,1)} %copy-done.3, bf16[512,512]{1,0:T(8,128)(2,1)} %collective-permute-done.2.other), custom_call_target="tpu_custom_call" | custom-call | flops 4000000000 | bytes 40000000 | tf_op jit(solution)/shard_map/pallas_call | solution.py:48
  67.7 4.5 %collective-permute-done.1.refs_4_ = bf16[512,512]{1,0:T(8,128)(2,1)S(1)} collective-permute-done((bf16[512,512]{1,0:T(8,128)(2,1)S(1)}, bf16[512,512]{1,0:T(8,128)(2,1)S(1)}, u32[]{:S(2)}, u32[]{:S(2)}) %collective-permute-start.1) | collective-permute-done | bytes 524320 | tf_op jit(solution)/shard_map/ppermute | solution.py:32
  72.3 5.3 %collective-permute-done.refs_1_ = bf16[512,512]{1,0:T(8,128)(2,1)S(1)} collective-permute-done((bf16[512,512]{1,0:T(8,128)(2,1)S(1)}, bf16[512,512]{1,0:T(8,128)(2,1)S(1)}, u32[]{:S(2)}, u32[]{:S(2)}) %collective-permute-start) | collective-permute-done | bytes 524320 | tf_op jit(solution)/shard_map/ppermute | solution.py:32
  77.6 1.9 %collective-permute-start.3 = (bf16[512,512]{1,0:T(8,128)(2,1)S(1)}, bf16[512,512]{1,0:T(8,128)(2,1)S(1)}, u32[]{:S(2)}, u32[]{:S(2)}) collective-permute-start(bf16[512,512]{1,0:T(8,128)(2,1)S(1)} %collective-permute-done.refs_1_), channel_id=1, source_target_pairs={{0,1},{1,2},{2,3},{3,4},{4,5},{5,6},{6,7},{7,0},{8,9},{9,10},{10,1... | collective-permute-start | bytes 1572872 | tf_op jit(solution)/shard_map/ppermute | solution.py:32
  79.5 5.1 %collective-permute-start.5 = (bf16[512,512]{1,0:T(8,128)(2,1)S(1)}, bf16[512,512]{1,0:T(8,128)(2,1)S(1)}, u32[]{:S(2)}, u32[]{:S(2)}) collective-permute-start(bf16[512,512]{1,0:T(8,128)(2,1)S(1)} %collective-permute-done.1.refs_4_), channel_id=1, source_target_pairs={{0,7},{1,0},{2,1},{3,2},{4,3},{5,4},{6,5},{7,6},{8,15},{9,8},{10,9... | collective-permute-start | bytes 1572872 | tf_op jit(solution)/shard_map/ppermute | solution.py:32
  84.7 9.2 %collective-permute-done.3.refs_2_ = bf16[512,512]{1,0:T(8,128)(2,1)S(1)} collective-permute-done((bf16[512,512]{1,0:T(8,128)(2,1)S(1)}, bf16[512,512]{1,0:T(8,128)(2,1)S(1)}, u32[]{:S(2)}, u32[]{:S(2)}) %collective-permute-start.3) | collective-permute-done | bytes 524320 | tf_op jit(solution)/shard_map/ppermute | solution.py:32
  93.9 1.9 %collective-permute-start.4 = (bf16[512,512]{1,0:T(8,128)(2,1)S(1)}, bf16[512,512]{1,0:T(8,128)(2,1)S(1)}, u32[]{:S(2)}, u32[]{:S(2)}) collective-permute-start(bf16[512,512]{1,0:T(8,128)(2,1)S(1)} %collective-permute-done.3.refs_2_), channel_id=1, source_target_pairs={{0,1},{1,2},{2,3},{3,4},{4,5},{5,6},{6,7},{7,0},{8,9},{9,10},{10,1... | collective-permute-start | bytes 1572872 | tf_op jit(solution)/shard_map/ppermute | solution.py:32
  95.8 5.1 %collective-permute-start.6 = (bf16[512,512]{1,0:T(8,128)(2,1)S(1)}, bf16[512,512]{1,0:T(8,128)(2,1)S(1)}, u32[]{:S(2)}, u32[]{:S(2)}) collective-permute-start(bf16[512,512]{1,0:T(8,128)(2,1)S(1)} %collective-permute-done.5.refs_5_), channel_id=1, source_target_pairs={{0,7},{1,0},{2,1},{3,2},{4,3},{5,4},{6,5},{7,6},{8,15},{9,8},{10,9... | collective-permute-start | bytes 1572872 | tf_op jit(solution)/shard_map/ppermute | solution.py:32
  101.0 8.3 %collective-permute-done.4.refs_3_ = bf16[512,512]{1,0:T(8,128)(2,1)S(1)} collective-permute-done((bf16[512,512]{1,0:T(8,128)(2,1)S(1)}, bf16[512,512]{1,0:T(8,128)(2,1)S(1)}, u32[]{:S(2)}, u32[]{:S(2)}) %collective-permute-start.4) | collective-permute-done | bytes 524320 | tf_op jit(solution)/shard_map/ppermute | solution.py:32
  109.3 1.9 %collective-permute-start.7 = (bf16[256,512]{1,0:T(8,128)(2,1)S(1)}, bf16[256,512]{1,0:T(8,128)(2,1)S(1)}, u32[]{:S(2)}, u32[]{:S(2)}) collective-permute-start(bf16[256,512]{1,0:T(8,128)(2,1)S(1)} %slice.23), channel_id=1, source_target_pairs={{0,1},{1,2},{2,3},{3,4},{4,5},{5,6},{6,7},{7,0},{8,9},{9,10},{10,1... | collective-permute-start | bytes 786440 | tf_op jit(solution)/shard_map/ppermute | solution.py:32
  111.3 5.1 %collective-permute-start.8 = (bf16[256,512]{1,0:T(8,128)(2,1)S(1)}, bf16[256,512]{1,0:T(8,128)(2,1)S(1)}, u32[]{:S(2)}, u32[]{:S(2)}) collective-permute-start(bf16[256,512]{1,0:T(8,128)(2,1)S(1)} %slice.24), channel_id=1, source_target_pairs={{0,7},{1,0},{2,1},{3,2},{4,3},{5,4},{6,5},{7,6},{8,15},{9,8},{10,9... | collective-permute-start | bytes 786440 | tf_op jit(solution)/shard_map/ppermute | solution.py:32
  116.5 1.9 %collective-permute-start.9 = (bf16[256,1024]{1,0:T(8,128)(2,1)}, bf16[256,1024]{1,0:T(8,128)(2,1)S(1)}, u32[]{:S(2)}, u32[]{:S(2)}) collective-permute-start(bf16[256,1024]{1,0:T(8,128)(2,1)} %get-tuple-element.32), channel_id=1, source_target_pairs={{0,8},{8,0},{1,9},{9,1},{2,10},{10,2},{3,11},{11,3},{4,12},{12,4},... | collective-permute-start | bytes 1572872 | tf_op jit(solution)/shard_map/ppermute | solution.py:27
  121.1 5.5 %shard_map.164 = (bf16[192,512]{1,0:T(8,128)(2,1)}, bf16[192,512]{1,0:T(8,128)(2,1)}, bf16[192,512]{1,0:T(8,128)(2,1)}, f32[1,512]{1,0:T(1,128)}) custom-call(s32[1]{0:T(128)} %bitcast.where, bf16[192,4096]{1,0:T(8,128)(2,1)} %bitcast.21, bf16[192,512]{1,0:T(8,128)(2,1)} %bitcast.22, bf16[192,512]{1,0:T(8,128)(2,1)} %bitcast.23, ...), custom_call_target="tpu_custom_call" | custom-call | flops 3000000000 | bytes 30000000 | tf_op jit(solution)/shard_map/pallas_call | solution.py:48
  127.8 5.1 %all-to-all-start.1 = ((f32[8,1,512]{2,1,0:T(1,128)}), f32[8,1,512]{2,1,0:T(1,128)S(1)}, u32[]{:S(2)}, u32[]{:S(2)}) async-start(f32[8,1,512]{2,1,0:T(1,128)} %broadcast_in_dim.27), calls=%async_computation.1 | async-start | bytes 32768 | tf_op jit(solution)/shard_map/all_to_all | solution.py:23
  133.9 6.8 %all-to-all-done.1.terms = f32[8,1,512]{2,1,0:T(1,128)S(1)} async-done(((f32[8,1,512]{2,1,0:T(1,128)}), f32[8,1,512]{2,1,0:T(1,128)S(1)}, u32[]{:S(2)}, u32[]{:S(2)}) %all-to-all-start.1) | async-done | bytes 16416 | tf_op jit(solution)/shard_map/all_to_all | solution.py:23
  140.7 5.2 %all-to-all-start.3 = ((bf16[32,8,1024]{2,1,0:T(8,128)(2,1)}), bf16[32,8,1024]{2,1,0:T(8,128)(2,1)S(1)}, u32[]{:S(2)}, u32[]{:S(2)}) async-start(bf16[32,8,1024]{2,1,0:T(8,128)(2,1)} %fusion), calls=%async_computation.3 | async-start | bytes 1048576 | tf_op jit(solution)/shard_map/all_to_all | solution.py:23
  145.9 1.6 shard_map.166
  147.6 12.2 %all-to-all-done.3 = bf16[32,8,1024]{2,1,0:T(8,128)(2,1)S(1)} async-done(((bf16[32,8,1024]{2,1,0:T(8,128)(2,1)}), bf16[32,8,1024]{2,1,0:T(8,128)(2,1)S(1)}, u32[]{:S(2)}, u32[]{:S(2)}) %all-to-all-start.3) | async-done | bytes 524320 | tf_op jit(solution)/shard_map/all_to_all | solution.py:23
  159.8 6.0 %all-to-all-start.2 = ((f32[64,1,128]{2,1,0:T(1,128)}), f32[64,1,128]{2,1,0:T(1,128)S(1)}, u32[]{:S(2)}, u32[]{:S(2)}) async-start(f32[64,1,128]{2,1,0:T(1,128)} %shard_map.166), calls=%async_computation.2 | async-start | bytes 65536 | tf_op jit(solution)/shard_map/all_to_all | solution.py:23
  165.9 7.7 %all-to-all-done.2.returned = f32[64,1,128]{2,1,0:T(1,128)S(1)} async-done(((f32[64,1,128]{2,1,0:T(1,128)}), f32[64,1,128]{2,1,0:T(1,128)S(1)}, u32[]{:S(2)}, u32[]{:S(2)}) %all-to-all-start.2) | async-done | bytes 32800 | tf_op jit(solution)/shard_map/all_to_all | solution.py:23
  174.3 3.4 %all-to-all-start.4 = ((bf16[8,8,1024]{2,1,0:T(8,128)(2,1)}), bf16[8,8,1024]{2,1,0:T(8,128)(2,1)S(1)}, u32[]{:S(2)}, u32[]{:S(2)}) async-start(bf16[8,8,1024]{2,1,0:T(8,128)(2,1)} %broadcast_in_dim.28), calls=%async_computation.4 | async-start | bytes 262144 | tf_op jit(solution)/shard_map/all_to_all | solution.py:23
  177.7 4.3 %shard_map.165 = bf16[192,4096]{1,0:T(8,128)(2,1)} custom-call(s32[1]{0:T(128)} %bitcast.where, bf16[192,512]{1,0:T(8,128)(2,1)} %get-tuple-element.25.weighted, bf16[512,512]{1,0:T(8,128)(2,1)} %copy-done.2, bf16[512,512]{1,0:T(8,128)(2,1)} %copy-done.9, bf16[512,512]{1,0:T(8,128)(2,1)} %copy-done.10, bf16[512,512]{1,0:T(8,128)(2,1)} %copy-done.4, ...), custom_call_target="tpu_custom_call" | custom-call | flops 3000000000 | bytes 30000000 | tf_op jit(solution)/shard_map/pallas_call | solution.py:48
  182.0 1.8 shard_map.167
  183.8 1.4 copy.22
  185.1 1.8 all-to-all-done.4.terms
  187.6 1.6 shard_map.168
  (45 shorter events, 9.7 us)
Async XLA Ops:
  53.1 9.9 %copy-start.3 = (bf16[512,512]{1,0:T(8,128)(2,1)}, bf16[512,512]{1,0:T(8,128)(2,1)S(1)}, u32[]{:S(2)}) copy-start(bf16[512,512]{1,0:T(8,128)(2,1)S(1)} %get-tuple-element.42.mine) | copy-start | bytes 1572868
  53.1 14.6 %copy-start.2 = (bf16[512,512]{1,0:T(8,128)(2,1)}, bf16[512,512]{1,0:T(8,128)(2,1)S(1)}, u32[]{:S(2)}) copy-start(bf16[512,512]{1,0:T(8,128)(2,1)S(1)} %get-tuple-element.43.refs_0_) | copy-start | bytes 1572868
  53.1 9.8 %collective-permute-start.2 = (bf16[512,512]{1,0:T(8,128)(2,1)S(1)}, bf16[512,512]{1,0:T(8,128)(2,1)}, u32[]{:S(2)}, u32[]{:S(2)}) collective-permute-start(bf16[512,512]{1,0:T(8,128)(2,1)S(1)} %get-tuple-element.42.mine), channel_id=1, source_target_pairs={{0,8},{8,0},{1,9},{9,1},{2,10},{10,2},{3,11},{11,3},{4,12},{12,4},... | collective-permute-start | bytes 1572872 | tf_op jit(solution)/shard_map/ppermute | solution.py:27
  55.1 17.2 %collective-permute-start.1 = (bf16[512,512]{1,0:T(8,128)(2,1)S(1)}, bf16[512,512]{1,0:T(8,128)(2,1)S(1)}, u32[]{:S(2)}, u32[]{:S(2)}) collective-permute-start(bf16[512,512]{1,0:T(8,128)(2,1)S(1)} %get-tuple-element.43.refs_0_), channel_id=1, source_target_pairs={{0,7},{1,0},{2,1},{3,2},{4,3},{5,4},{6,5},{7,6},{8,15},{9,8},{10,9... | collective-permute-start | bytes 1572872 | tf_op jit(solution)/shard_map/ppermute | solution.py:32
  60.4 17.2 %collective-permute-start = (bf16[512,512]{1,0:T(8,128)(2,1)S(1)}, bf16[512,512]{1,0:T(8,128)(2,1)S(1)}, u32[]{:S(2)}, u32[]{:S(2)}) collective-permute-start(bf16[512,512]{1,0:T(8,128)(2,1)S(1)} %get-tuple-element.43.refs_0_), channel_id=1, source_target_pairs={{0,1},{1,2},{2,3},{3,4},{4,5},{5,6},{6,7},{7,0},{8,9},{9,10},{10,1... | collective-permute-start | bytes 1572872 | tf_op jit(solution)/shard_map/ppermute | solution.py:32
  72.3 48.8 %copy-start.8 = (bf16[512,512]{1,0:T(8,128)(2,1)}, bf16[512,512]{1,0:T(8,128)(2,1)S(1)}, u32[]{:S(2)}) copy-start(bf16[512,512]{1,0:T(8,128)(2,1)S(1)} %collective-permute-done.1.refs_4_) | copy-start | bytes 1572868
  77.6 18.2 %copy-start.9 = (bf16[512,512]{1,0:T(8,128)(2,1)}, bf16[512,512]{1,0:T(8,128)(2,1)S(1)}, u32[]{:S(2)}) copy-start(bf16[512,512]{1,0:T(8,128)(2,1)S(1)} %collective-permute-done.refs_1_) | copy-start | bytes 1572868
  77.6 16.3 %collective-permute-start.3 = (bf16[512,512]{1,0:T(8,128)(2,1)S(1)}, bf16[512,512]{1,0:T(8,128)(2,1)S(1)}, u32[]{:S(2)}, u32[]{:S(2)}) collective-permute-start(bf16[512,512]{1,0:T(8,128)(2,1)S(1)} %collective-permute-done.refs_1_), channel_id=1, source_target_pairs={{0,1},{1,2},{2,3},{3,4},{4,5},{5,6},{6,7},{7,0},{8,9},{9,10},{10,1... | collective-permute-start | bytes 1572872 | tf_op jit(solution)/shard_map/ppermute | solution.py:32
  79.5 16.3 %collective-permute-start.5 = (bf16[512,512]{1,0:T(8,128)(2,1)S(1)}, bf16[512,512]{1,0:T(8,128)(2,1)S(1)}, u32[]{:S(2)}, u32[]{:S(2)}) collective-permute-start(bf16[512,512]{1,0:T(8,128)(2,1)S(1)} %collective-permute-done.1.refs_4_), channel_id=1, source_target_pairs={{0,7},{1,0},{2,1},{3,2},{4,3},{5,4},{6,5},{7,6},{8,15},{9,8},{10,9... | collective-permute-start | bytes 1572872 | tf_op jit(solution)/shard_map/ppermute | solution.py:32
  93.9 17.4 %copy-start.10 = (bf16[512,512]{1,0:T(8,128)(2,1)}, bf16[512,512]{1,0:T(8,128)(2,1)S(1)}, u32[]{:S(2)}) copy-start(bf16[512,512]{1,0:T(8,128)(2,1)S(1)} %collective-permute-done.3.refs_2_) | copy-start | bytes 1572868
  93.9 15.4 %collective-permute-start.4 = (bf16[512,512]{1,0:T(8,128)(2,1)S(1)}, bf16[512,512]{1,0:T(8,128)(2,1)S(1)}, u32[]{:S(2)}, u32[]{:S(2)}) collective-permute-start(bf16[512,512]{1,0:T(8,128)(2,1)S(1)} %collective-permute-done.3.refs_2_), channel_id=1, source_target_pairs={{0,1},{1,2},{2,3},{3,4},{4,5},{5,6},{6,7},{7,0},{8,9},{9,10},{10,1... | collective-permute-start | bytes 1572872 | tf_op jit(solution)/shard_map/ppermute | solution.py:32
  95.8 15.4 %copy-start.11 = (bf16[512,512]{1,0:T(8,128)(2,1)}, bf16[512,512]{1,0:T(8,128)(2,1)S(1)}, u32[]{:S(2)}) copy-start(bf16[512,512]{1,0:T(8,128)(2,1)S(1)} %collective-permute-done.5.refs_5_) | copy-start | bytes 1572868
  95.8 15.4 %collective-permute-start.6 = (bf16[512,512]{1,0:T(8,128)(2,1)S(1)}, bf16[512,512]{1,0:T(8,128)(2,1)S(1)}, u32[]{:S(2)}, u32[]{:S(2)}) collective-permute-start(bf16[512,512]{1,0:T(8,128)(2,1)S(1)} %collective-permute-done.5.refs_5_), channel_id=1, source_target_pairs={{0,7},{1,0},{2,1},{3,2},{4,3},{5,4},{6,5},{7,6},{8,15},{9,8},{10,9... | collective-permute-start | bytes 1572872 | tf_op jit(solution)/shard_map/ppermute | solution.py:32
  109.3 11.7 %copy-start.4 = (bf16[512,512]{1,0:T(8,128)(2,1)}, bf16[512,512]{1,0:T(8,128)(2,1)S(1)}, u32[]{:S(2)}) copy-start(bf16[512,512]{1,0:T(8,128)(2,1)S(1)} %collective-permute-done.4.refs_3_) | copy-start | bytes 1572868
  109.3 9.7 %collective-permute-start.7 = (bf16[256,512]{1,0:T(8,128)(2,1)S(1)}, bf16[256,512]{1,0:T(8,128)(2,1)S(1)}, u32[]{:S(2)}, u32[]{:S(2)}) collective-permute-start(bf16[256,512]{1,0:T(8,128)(2,1)S(1)} %slice.23), channel_id=1, source_target_pairs={{0,1},{1,2},{2,3},{3,4},{4,5},{5,6},{6,7},{7,0},{8,9},{9,10},{10,1... | collective-permute-start | bytes 786440 | tf_op jit(solution)/shard_map/ppermute | solution.py:32
  111.3 9.8 %copy-start.5 = (bf16[512,512]{1,0:T(8,128)(2,1)}, bf16[512,512]{1,0:T(8,128)(2,1)S(1)}, u32[]{:S(2)}) copy-start(bf16[512,512]{1,0:T(8,128)(2,1)S(1)} %collective-permute-done.6.refs_6_) | copy-start | bytes 1572868
  111.3 9.0 %collective-permute-start.8 = (bf16[256,512]{1,0:T(8,128)(2,1)S(1)}, bf16[256,512]{1,0:T(8,128)(2,1)S(1)}, u32[]{:S(2)}, u32[]{:S(2)}) collective-permute-start(bf16[256,512]{1,0:T(8,128)(2,1)S(1)} %slice.24), channel_id=1, source_target_pairs={{0,7},{1,0},{2,1},{3,2},{4,3},{5,4},{6,5},{7,6},{8,15},{9,8},{10,9... | collective-permute-start | bytes 786440 | tf_op jit(solution)/shard_map/ppermute | solution.py:32
  116.5 16.5 %collective-permute-start.9 = (bf16[256,1024]{1,0:T(8,128)(2,1)}, bf16[256,1024]{1,0:T(8,128)(2,1)S(1)}, u32[]{:S(2)}, u32[]{:S(2)}) collective-permute-start(bf16[256,1024]{1,0:T(8,128)(2,1)} %get-tuple-element.32), channel_id=1, source_target_pairs={{0,8},{8,0},{1,9},{9,1},{2,10},{10,2},{3,11},{11,3},{4,12},{12,4},... | collective-permute-start | bytes 1572872 | tf_op jit(solution)/shard_map/ppermute | solution.py:27
  119.1 2.0 %copy-start.12 = (bf16[256,512]{1,0:T(8,128)(2,1)}, bf16[256,512]{1,0:T(8,128)(2,1)S(1)}, u32[]{:S(2)}) copy-start(bf16[256,512]{1,0:T(8,128)(2,1)S(1)} %collective-permute-done.7.refs_7_) | copy-start | bytes 786436
  120.3 0.7 copy-start.13
  121.1 11.9 %copy-start = (f32[256,1024]{1,0:T(8,128)S(1)}, f32[256,1024]{1,0:T(8,128)}, u32[]{:S(2)}) copy-start(f32[256,1024]{1,0:T(8,128)} %get-tuple-element.31) | copy-start | bytes 3145732
  127.8 12.9 %all-to-all-start.1 = ((f32[8,1,512]{2,1,0:T(1,128)}), f32[8,1,512]{2,1,0:T(1,128)S(1)}, u32[]{:S(2)}, u32[]{:S(2)}) async-start(f32[8,1,512]{2,1,0:T(1,128)} %broadcast_in_dim.27), calls=%async_computation.1 | async-start | bytes 32768 | tf_op jit(solution)/shard_map/all_to_all | solution.py:23
  140.7 5.2 %copy-start.7 = (f32[8,1,512]{2,1,0:T(1,128)}, f32[8,1,512]{2,1,0:T(1,128)S(1)}, u32[]{:S(2)}) copy-start(f32[8,1,512]{2,1,0:T(1,128)S(1)} %all-to-all-done.1.terms) | copy-start | bytes 49156
  140.7 19.1 %all-to-all-start.3 = ((bf16[32,8,1024]{2,1,0:T(8,128)(2,1)}), bf16[32,8,1024]{2,1,0:T(8,128)(2,1)S(1)}, u32[]{:S(2)}, u32[]{:S(2)}) async-start(bf16[32,8,1024]{2,1,0:T(8,128)(2,1)} %fusion), calls=%async_computation.3 | async-start | bytes 1048576 | tf_op jit(solution)/shard_map/all_to_all | solution.py:23
  159.8 13.8 %all-to-all-start.2 = ((f32[64,1,128]{2,1,0:T(1,128)}), f32[64,1,128]{2,1,0:T(1,128)S(1)}, u32[]{:S(2)}, u32[]{:S(2)}) async-start(f32[64,1,128]{2,1,0:T(1,128)} %shard_map.166), calls=%async_computation.2 | async-start | bytes 65536 | tf_op jit(solution)/shard_map/all_to_all | solution.py:23
  173.6 8.4 %copy-start.6 = (f32[64,1,128]{2,1,0:T(1,128)}, f32[64,1,128]{2,1,0:T(1,128)S(1)}, u32[]{:S(2)}) copy-start(f32[64,1,128]{2,1,0:T(1,128)S(1)} %all-to-all-done.2.returned) | copy-start | bytes 98308
  174.3 12.6 %all-to-all-start.4 = ((bf16[8,8,1024]{2,1,0:T(8,128)(2,1)}), bf16[8,8,1024]{2,1,0:T(8,128)(2,1)S(1)}, u32[]{:S(2)}, u32[]{:S(2)}) async-start(bf16[8,8,1024]{2,1,0:T(8,128)(2,1)} %broadcast_in_dim.28), calls=%async_computation.4 | async-start | bytes 262144 | tf_op jit(solution)/shard_map/all_to_all | solution.py:23
  186.9 0.6 copy-start.1

commit v3 on v1

v3 whole, which is shorter than its diff:
```python
import jax
import jax.numpy as jnp
from jax import lax
from jax.experimental import pallas as pl
from jax.experimental.pallas import tpu as pltpu
from jax.sharding import Mesh, PartitionSpec as P

H = 64
KVH = 4
HD = 128
GX = ("z", "x", "c")
ZX = ("z", "x")
NT = (((1,), (1,)), ((), ()))
TN = (((0,), (0,)), ((), ()))
F32 = jnp.float32
BF16 = jnp.bfloat16


def exchange(values, axes):
    return lax.all_to_all(values, axes, split_axis=0, concat_axis=0, tiled=True)


def to_partner(values):
    return lax.ppermute(values, "c", [(0, 1), (1, 0)])


def iota(shape, dim):
    return lax.broadcasted_iota(jnp.int32, shape, dim)


def call(body, outs, ins, flops, size, name):
    vmem = pl.BlockSpec(memory_space=pltpu.VMEM)
    return pl.pallas_call(
        body,
        out_shape=outs,
        in_specs=[pl.BlockSpec(memory_space=pltpu.SMEM)] + [vmem] * (len(ins) - 1),
        out_specs=jax.tree.map(lambda _: vmem, outs),
        cost_estimate=pl.CostEstimate(flops=flops, bytes_accessed=size, transcendentals=0),
        name=name,
    )(*ins)


def pack_body(where, kept, ids, gates, d_out, keys, values, message, kv, ranks):
    top, rows = ids.shape
    slots = message.shape[0]
    tok_dev, width = d_out.shape
    chips = kv.shape[0] // rows
    cap = 8
    head = pl.multiple_of(where[0] * HD, HD)
    slot = iota((slots, rows), 0)
    expert = slot // cap
    place = (slot % cap).astype(F32)
    named = jnp.zeros((slots, rows), F32)
    weight = jnp.zeros((slots, rows), F32)
    for j in range(top):
        hit = ids[j : j + 1, :] == expert
        named = jnp.where(hit, 1.0, named)
        weight = jnp.where(hit, gates[j : j + 1, :].astype(F32), weight)
    before = jnp.where(iota((rows, rows), 0) < iota((rows, rows), 1), 1.0, 0.0).astype(BF16)
    rank = jnp.dot(named.astype(BF16), before, preferred_element_type=F32)
    taken = jnp.where((named > 0.0) & (rank == place), 1.0, 0.0)
    pick = jnp.where(kept[...] % tok_dev == iota((tok_dev, rows), 0), 1.0, 0.0).astype(BF16)
    picked = lax.dot_general(pick, d_out[...], TN, preferred_element_type=F32).astype(BF16)
    message[:, :width] = jnp.dot(
        taken.astype(BF16), picked, preferred_element_type=F32
    ).astype(BF16)
    message[:, width:] = jnp.dot(
        (taken * weight).astype(BF16), jnp.ones((rows, HD), BF16), preferred_element_type=F32
    ).astype(BF16)
    for at, source in ((0, keys), (HD, values)):
        kv[:, at : at + HD] = jnp.broadcast_to(
            source[:, pl.ds(head, HD)][None], (chips, rows, HD)
        ).reshape(chips * rows, HD)
    for j in range(top):
        mine = jnp.where((ids[j : j + 1, :] == expert) & (taken > 0.0), place, 0.0)
        ranks[j : j + 1, :] = jnp.sum(mine, axis=0, keepdims=True).astype(jnp.int32)


def attention_body(where, query, grad, mine, other, d_query, keep, send):
    core, block = where[0], where[1]
    keep_dev = query.shape[0]
    heads = query.shape[1] // HD
    rows = keep_dev * heads
    half = mine.shape[0]
    scale = HD ** (-0.5)

    def stacked(ref):
        return jnp.concatenate([ref[:, g * HD : (g + 1) * HD] for g in range(heads)], axis=0)

    q = stacked(query)
    o = stacked(grad)
    query_pos = block * keep_dev + iota((rows, half), 0) % keep_dev
    column = iota((rows, half), 1)
    base = column // keep_dev * (2 * keep_dev) + column % keep_dev
    scores = []
    for ref, owner in ((mine, core), (other, 1 - core)):
        s = lax.dot_general(q, ref[:, :HD], NT, preferred_element_type=F32) * scale
        scores.append(jnp.where(base + owner * keep_dev <= query_pos, s, -1e30))
    top = jnp.maximum(*[jnp.max(s, axis=1, keepdims=True) for s in scores])
    expo = [jnp.exp(s - top) for s in scores]
    inv = 1.0 / sum(jnp.sum(e, axis=1, keepdims=True) for e in expo)
    probs = [e * inv for e in expo]
    dps = [
        lax.dot_general(o, ref[:, HD:], NT, preferred_element_type=F32) for ref in (mine, other)
    ]
    mean = sum(jnp.sum(p * dp, axis=1, keepdims=True) for p, dp in zip(probs, dps))
    dq = jnp.zeros((rows, HD), F32)
    for ref, p, dp, out in zip((other, mine), probs[::-1], dps[::-1], (send, keep)):
        ds = (p * (dp - mean)).astype(BF16)
        dk = lax.dot_general(ds, q, TN, preferred_element_type=F32) * scale
        dv = lax.dot_general(p.astype(BF16), o, TN, preferred_element_type=F32)
        out[:, :HD] = dk.astype(BF16)
        out[:, HD:] = dv.astype(BF16)
        dq = dq + jnp.dot(ds, ref[:, :HD], preferred_element_type=F32)
    dq = (dq * scale).astype(BF16)
    for g in range(heads):
        d_query[:, g * HD : (g + 1) * HD] = dq[g * keep_dev : (g + 1) * keep_dev]


def expert_body(weight, rows, gate_pre, up_pre, slot_gate, d_gate, d_up, weighted, dots, acc):
    step = pl.program_id(0)
    part = lax.dot_general(weight[...], rows[...], NT, preferred_element_type=F32)

    @pl.when(step == 0)
    def _():
        acc[...] = part

    @pl.when(step > 0)
    def _():
        acc[...] += part

    @pl.when(step == pl.num_programs(0) - 1)
    def _():
        z = acc[...]
        g = gate_pre[...].astype(F32)
        u = up_pre[...].astype(F32)
        sig = 1.0 / (1.0 + jnp.exp(-g))
        act = g * sig
        hidden = act * u
        dots[...] = jnp.sum(hidden * z, axis=0, keepdims=True)
        one = jnp.where(iota((8, HD), 1) == 0, 1.0, 0.0).astype(BF16)
        scale = lax.dot_general(one, slot_gate[...], NT, preferred_element_type=F32)[0:1]
        grad_hidden = z * scale
        d_up[...] = (grad_hidden * act).astype(BF16)
        d_gate[...] = (grad_hidden * u * sig * (1.0 + g * (1.0 - sig))).astype(BF16)
        weighted[...] = (hidden * scale).astype(BF16)


def down_body(weighted, rows, out):
    out[...] = jnp.dot(weighted[...], rows[...], preferred_element_type=F32).astype(BF16)


def merge_body(where, owned, dots, out):
    copies, rows, lanes = out.shape
    keep_dev = owned.shape[0]
    value = dots[...]
    high = value.astype(BF16)
    rest = value - high.astype(F32)
    middle = rest.astype(BF16)
    low = (rest - middle.astype(F32)).astype(BF16)
    row = iota((rows - keep_dev, lanes), 0)
    tail = jnp.zeros((rows - keep_dev, lanes), F32)
    for i, part in enumerate((high, middle, low)):
        for j in range(2):
            piece = part[:, j * lanes : (j + 1) * lanes].astype(F32)
            tail = jnp.where(row == 2 * i + j, piece, tail)
    for i in range(copies):
        out[i, :keep_dev] = owned[...]
        out[i, keep_dev:] = tail.astype(BF16)


def middle_body(where, terms, out):
    keep_dev = terms.shape[1] - 8
    lanes = terms.shape[2]
    total = jnp.sum(terms[:, keep_dev:, :].astype(F32), axis=0)
    half = out.shape[0] // 2
    cap = lanes // half
    spread = jnp.concatenate(
        [
            jnp.where(
                iota((half, lanes), 1) // cap == iota((half, lanes), 0),
                total[j : j + 1] + total[2 + j : 3 + j] + total[4 + j : 5 + j],
                0.0,
            )
            for j in range(2)
        ],
        axis=0,
    )
    place = jnp.where(iota((lanes, HD), 0) % cap == iota((lanes, HD), 1), 1.0, 0.0)
    out[...] = jnp.dot(
        spread, place, preferred_element_type=F32, precision=lax.Precision.HIGHEST
    )[:, None, :]


def gates_body(where, ids, ranks, returned, out):
    top, rows = ids.shape
    experts = returned.shape[0]
    table = returned[...].reshape(experts, HD)
    for j in range(top):
        pick = jnp.where(ids[j : j + 1, :] == iota((experts, rows), 0), 1.0, 0.0)
        found = lax.dot_general(
            table, pick, TN, preferred_element_type=F32, precision=lax.Precision.HIGHEST
        )
        hit = jnp.where(iota((HD, rows), 0) == ranks[j : j + 1, :], found, 0.0)
        out[j : j + 1, :] = jnp.sum(hit, axis=0, keepdims=True)


def heads_body(where, terms, d_key, d_value):
    keep_dev = d_key.shape[0]
    per = terms.shape[0] // KVH
    for h in range(KVH):
        both = sum(terms[h * per + i, :keep_dev].astype(F32) for i in range(per))
        d_key[:, h * HD : (h + 1) * HD] = both[:, :HD]
        d_value[:, h * HD : (h + 1) * HD] = both[:, HD:]


def on_device(
    d_out, kept, expert_ids, gates, down_weight, gate_pre, up_pre, query, keys, values, d_attn
):
    core = lax.axis_index("c")
    chips = lax.axis_size(ZX)
    me = lax.axis_index("ta")
    n_experts = lax.axis_size(GX)
    n_ta = lax.axis_size("ta")
    keep_dev = kept.shape[0]
    width = d_out.shape[1]
    top = expert_ids.shape[1]
    slots = gate_pre.shape[2]
    cap = slots // n_experts
    hidden = gate_pre.shape[1]
    struct = jax.ShapeDtypeStruct
    ids = expert_ids.T

    local_heads = query.shape[1] // HD
    first_kv = (me * local_heads // (H // KVH)).astype(jnp.int32)
    where = jnp.stack([first_kv, core.astype(jnp.int32), lax.axis_index(GX).astype(jnp.int32)])
    message, kv, ranks = call(
        pack_body,
        (
            struct((slots, width + HD), BF16),
            struct((chips * keep_dev, 2 * HD), BF16),
            struct((top, keep_dev), jnp.int32),
        ),
        (where, kept.reshape(1, keep_dev), ids, gates.T, d_out, keys, values),
        200_000_000,
        3_000_000,
        "pack",
    )
    arrived = exchange(message.reshape(n_experts, cap, -1), GX).reshape(slots, -1)
    slot_rows = lax.all_gather(arrived[:, :width], "ta", axis=1, tiled=True)
    slot_gate = arrived[:, width:]

    kv_mine = exchange(kv.reshape(chips, keep_dev, 2 * HD), ZX).reshape(-1, 2 * HD)
    kv_other = to_partner(kv_mine)
    half = chips * keep_dev
    d_query, keep, send = call(
        attention_body,
        (
            struct((keep_dev, local_heads * HD), BF16),
            struct((half, 2 * HD), BF16),
            struct((half, 2 * HD), BF16),
        ),
        (where[1:], query, d_attn, kv_mine, kv_other),
        1_000_000_000,
        4_000_000,
        "attention",
    )
    chip_part = (keep.astype(F32) + to_partner(send).astype(F32)).astype(BF16)
    summed = exchange(chip_part.reshape(chips, keep_dev, 2 * HD), ZX)
    owned = jnp.sum(summed.astype(F32), axis=0).astype(BF16)

    steps = n_ta
    whole = pl.BlockSpec((hidden, slots), lambda i: (0, 0))
    d_gate, d_up, weighted, dots = pl.pallas_call(
        expert_body,
        grid=(steps,),
        in_specs=[
            pl.BlockSpec((hidden, width), lambda i: (0, i)),
            pl.BlockSpec((slots, width), lambda i: (0, i)),
            whole,
            whole,
            pl.BlockSpec((slots, HD), lambda i: (0, 0)),
        ],
        out_specs=[whole, whole, whole, pl.BlockSpec((1, slots), lambda i: (0, 0))],
        out_shape=[struct((hidden, slots), BF16)] * 3 + [struct((1, slots), F32)],
        scratch_shapes=[pltpu.VMEM((hidden, slots), F32)],
        cost_estimate=pl.CostEstimate(
            flops=1_000_000_000, bytes_accessed=7_000_000, transcendentals=0
        ),
        name="expert",
    )(down_weight[0], slot_rows, gate_pre[0], up_pre[0], slot_gate)
    d_down = pl.pallas_call(
        down_body,
        grid=(steps,),
        in_specs=[whole, pl.BlockSpec((slots, width), lambda i: (0, i))],
        out_specs=pl.BlockSpec((hidden, width), lambda i: (0, i)),
        out_shape=struct(down_weight.shape[1:], BF16),
        cost_estimate=pl.CostEstimate(
            flops=1_000_000_000, bytes_accessed=6_000_000, transcendentals=0
        ),
        name="down",
    )(weighted, slot_rows)
    merged = call(
        merge_body,
        struct((n_ta, keep_dev + 8, 2 * HD), BF16),
        (where, owned, dots),
        1_000_000,
        200_000,
        "merge",
    )
    terms = exchange(merged, "ta")
    sums = call(
        middle_body, struct((n_experts, 1, HD), F32), (where, terms), 1_000_000, 100_000, "middle"
    )
    returned = exchange(sums, GX)
    d_gates = call(
        gates_body,
        struct((top, keep_dev), F32),
        (where, ids, ranks, returned),
        1_000_000,
        100_000,
        "gates",
    ).T
    d_key, d_value = call(
        heads_body,
        (struct((keep_dev, KVH * HD), F32), struct((keep_dev, KVH * HD), F32)),
        (where, terms),
        1_000_000,
        1_000_000,
        "heads",
    )
    return (d_down[None], d_gate[None], d_up[None], d_gates, d_query, d_key, d_value)


def solution(mesh):
    shape = dict(mesh.shape)
    fine = Mesh(mesh.devices.reshape(8, shape["gx"] // 16, 2, shape["ta"]), GX + ("ta",))
    in_specs = (
        P(GX, "ta"),
        P(GX),
        P(GX, None),
        P(GX, None),
        P(GX, "ta", None),
        P(GX, "ta", None),
        P(GX, "ta", None),
        P(GX, "ta"),
        P(GX, None),
        P(GX, None),
        P(GX, "ta"),
    )
    out_specs = (
        P(GX, "ta", None),
        P(GX, "ta", None),
        P(GX, "ta", None),
        P(GX, None),
        P(GX, "ta"),
        P(GX, None),
        P(GX, None),
    )
    return jax.shard_map(
        on_device, mesh=fine, in_specs=in_specs, out_specs=out_specs, check_vma=False
    )
```

time: 154 us -> 161 us (1.045)
  blocking collectives: 34.1 us -> 72.8 us
  Pallas kernels: 0 us -> 28.8 us
  waiting for transfers between devices: 42.4 us -> 19.7 us
  matrix products: 15.4 us -> 0 us
  starting transfers between devices: 28.3 us -> 15.6 us
  local copies, waits for them, and re-layouts: 9.13 us -> 2.95 us
  other arithmetic: 7.96 us -> 3.86 us
    all_to_all x1 -> x3, blocking collectives: 34.1 us -> 72.8 us  [exchange(): return lax.all_to_all(values, axes, split_axis=0, concat_axis=0, tiled=True)]
    pallas_call x0 -> x8, Pallas kernels: none -> 28.8 us  [the longest x6 14 us: call(): pl.pallas_call(body, out_shape=outs, in_specs=[pl.BlockSpec(memory_space=...]
    dot_general x9 -> x0, matrix products: 15.4 us -> none  [the longest x1 4.61 us: on_device(): lax.dot_general(down_weight[0], slot_rows, nt, preferred_element_type=jnp...]
    all_to_all x4 -> x2, waiting for transfers between devices: 29.4 us -> 16.5 us  [exchange(): return lax.all_to_all(values, axes, split_axis=0, concat_axis=0, tiled=True)]
    all_to_all x4 -> x2, starting transfers between devices: 24.2 us -> 11.6 us  [exchange(): return lax.all_to_all(values, axes, split_axis=0, concat_axis=0, tiled=True)]
    all_gather x1, waiting for transfers between devices: 9.39 us -> 0.01 us  [on_device(): slot_rows = lax.all_gather(arrived[:, :width], 'ta', axis=1, tiled=True)]
    convert_element_type x3 -> x0, local copies, waits for them, and re-layouts: 2.22 us -> none  [the longest x1 2.04 us: on_device(): (part[:half] + from_other.astype(jnp.float32)).astype(jnp.bfloat16)]
    broadcast_in_dim x5 -> x0, local copies, waits for them, and re-layouts: 1.68 us -> none  [the longest x1 0.88 us: on_device(): jnp.broadcast_to(kv[None], (chips,) + kv.shape)]
  transfers between devices with their start and end apart: 7 -> 5, of which waited for: 7 -> 3; matrix products, arithmetic and copies ran while one was open for 14% -> 2% of each run, Pallas kernels for 0% -> 8%
where the time goes in v3:
time: 161 us; the launch traced here: 158 us
  blocking collectives  72.8 us (45%)
  Pallas kernels  28.8 us (18%)
  waiting for transfers between devices  19.7 us (12%)
  starting transfers between devices  15.6 us (10%)
  between operations  14.1 us (9%)
  other arithmetic  3.86 us (2%)
  local copies, waits for them, and re-layouts  2.95 us (2%)
    all_to_all x3, blocking collectives, exchange(): return lax.all_to_all(values, axes, split_axis=0, concat_axis=0, tiled=True)  72.8 us
    all_to_all x2, waiting for transfers between devices, exchange(): return lax.all_to_all(values, axes, split_axis=0, concat_axis=0, tiled=True)  16.5 us
    pallas_call x6, Pallas kernels, call(): pl.pallas_call(body, out_shape=outs, in_specs=[pl.BlockSpec(memory_space=...  14 us
    all_to_all x2, starting transfers between devices, exchange(): return lax.all_to_all(values, axes, split_axis=0, concat_axis=0, tiled=True)  11.6 us
    pallas_call x1, Pallas kernels, on_device(): pl.pallas_call(expert_body, grid=(steps,), in_specs=[pl.BlockSpec((hidden...  7.93 us
    pallas_call x1, Pallas kernels, on_device(): pl.pallas_call(down_body, grid=(steps,), in_specs=[whole, pl.BlockSpec((s...  6.95 us
    ppermute x2, starting transfers between devices, to_partner(): return lax.ppermute(values, 'c', [(0, 1), (1, 0)])  3.97 us
    ppermute x2, waiting for transfers between devices, to_partner(): return lax.ppermute(values, 'c', [(0, 1), (1, 0)])  3.22 us
  transfers between devices with their start and end apart: 5, of which 3 were waited for; matrix products, arithmetic and copies ran while one was open for 2% of the time, Pallas kernels for 8%

profile of v3, /device:TPU:6, one launch (start us, length us, event | category | flops | bytes accessed | tf_op | source)
XLA Modules:
  0.0 157.9 jit_solution(6667277501443639168)
XLA Ops:
  7.2 0.0 all-gather.2.cloned.1.call-start
  7.2 0.6 pad_add_fusion.where
  7.8 3.0 %pack.1 = (bf16[512,640]{1,0:T(8,128)(2,1)}, bf16[1024,256]{1,0:T(8,128)(2,1)}, s32[8,32]{1,0:T(8,128)}) custom-call(s32[3]{0:T(128)} %pad_add_fusion.where, s32[1,32]{1,0:T(1,128)} %bitcast.34, s32[8,32]{1,0:T(8,128)} %bitcast.28, bf16[8,32]{1,0:T(8,128)(2,1)} %bitcast.33, bf16[256,512]{1,0:T(8,128)(2,1)} %d_out.1, bf16[32,512]{1,0:T(8,128)(2,1)} %keys.1, ...), custom_call_target="tpu_custom_call" | custom-call | flops 200000000 | bytes 3000000 | tf_op jit(solution)/shard_map/pack/pallas_call | solution.py:33
  10.8 0.0 copy-start.1
  10.8 34.3 %all_to_all.25 = bf16[64,8,640]{2,1,0:T(8,128)(2,1)S(1)} all-to-all(bf16[64,8,640]{2,1,0:T(8,128)(2,1)} %bitcast.22), channel_id=1, replica_groups=mesh['z'=8,'x'=4,'c'=2,'ta'=8] {'z','x','c'}, dimensions={0} | all-to-all | bytes 1310720 | tf_op jit(solution)/shard_map/all_to_all | solution.py:20
  45.1 0.8 slice.10
  45.9 0.0 all-gather.2.cloned.1.call-update
  46.0 0.0 copy-done.1
  46.0 21.9 %all_to_all.26 = bf16[32,32,256]{2,1,0:T(8,128)(2,1)S(1)} all-to-all(bf16[32,32,256]{2,1,0:T(8,128)(2,1)S(1)} %bitcast.25), channel_id=1, replica_groups=mesh['z'=8,'x'=4,'c'=2,'ta'=8] {'z','x'}, dimensions={0} | all-to-all | bytes 1048576 | tf_op jit(solution)/shard_map/all_to_all | solution.py:20
  67.9 1.9 %collective-permute-start = (bf16[1024,256]{1,0:T(8,128)(2,1)S(1)}, bf16[1024,256]{1,0:T(8,128)(2,1)S(1)}, u32[]{:S(2)}, u32[]{:S(2)}) collective-permute-start(bf16[1024,256]{1,0:T(8,128)(2,1)S(1)} %bitcast.23), channel_id=1, source_target_pairs={{0,8},{8,0},{1,9},{9,1},{2,10},{10,2},{3,11},{11,3},{4,12},{12,4},... | collective-permute-start | bytes 1572872 | tf_op jit(solution)/shard_map/ppermute | solution.py:24
  69.8 0.6 pad_add_fusion.1.where
  70.4 1.3 collective-permute-done.other
  71.7 0.0 copy-done
  71.7 0.8 copy-done.3
  72.5 4.2 %attention.1 = (bf16[32,1024]{1,0:T(8,128)(2,1)}, bf16[1024,256]{1,0:T(8,128)(2,1)}, bf16[1024,256]{1,0:T(8,128)(2,1)}) custom-call(s32[2]{0:T(128)} %pad_add_fusion.1.where, bf16[32,1024]{1,0:T(8,128)(2,1)} %query.1, bf16[32,1024]{1,0:T(8,128)(2,1)} %grad.1, bf16[1024,256]{1,0:T(8,128)(2,1)} %bitcast.24, bf16[1024,256]{1,0:T(8,128)(2,1)} %copy-done.3), custom_call_target="tpu_custom_call" | custom-call | flops 1000000000 | bytes 4000000 | tf_op jit(solution)/shard_map/attention/pallas_call | solution.py:33
  76.7 2.1 %collective-permute-start.1 = (bf16[1024,256]{1,0:T(8,128)(2,1)}, bf16[1024,256]{1,0:T(8,128)(2,1)S(1)}, u32[]{:S(2)}, u32[]{:S(2)}) collective-permute-start(bf16[1024,256]{1,0:T(8,128)(2,1)} %get-tuple-element.26), channel_id=1, source_target_pairs={{0,8},{8,0},{1,9},{9,1},{2,10},{10,2},{3,11},{11,3},{4,12},{12,4},... | collective-permute-start | bytes 1572872 | tf_op jit(solution)/shard_map/ppermute | solution.py:24
  78.8 1.9 %collective-permute-done.1 = bf16[1024,256]{1,0:T(8,128)(2,1)S(1)} collective-permute-done((bf16[1024,256]{1,0:T(8,128)(2,1)}, bf16[1024,256]{1,0:T(8,128)(2,1)S(1)}, u32[]{:S(2)}, u32[]{:S(2)}) %collective-permute-start.1) | collective-permute-done | bytes 524320 | tf_op jit(solution)/shard_map/ppermute | solution.py:24
  80.7 2.0 %add_convert_fusion = bf16[1024,256]{1,0:T(8,128)(2,1)} fusion(bf16[1024,256]{1,0:T(8,128)(2,1)S(1)} %collective-permute-done.1, bf16[1024,256]{1,0:T(8,128)(2,1)} %get-tuple-element.25), kind=kLoop, calls=%fused_computation | loop fusion | flops 1048576 | bytes 1572864 | tf_op jit(solution)/shard_map/convert_element_type | solution.py:268
  82.7 5.6 %all-to-all-start.2 = ((bf16[32,32,256]{2,1,0:T(8,128)(2,1)}), bf16[32,32,256]{2,1,0:T(8,128)(2,1)S(1)}, u32[]{:S(2)}, u32[]{:S(2)}) async-start(bf16[32,32,256]{2,1,0:T(8,128)(2,1)} %bitcast.16), calls=%async_computation.2 | async-start | bytes 1048576 | tf_op jit(solution)/shard_map/all_to_all | solution.py:20
  88.3 0.7 slice.11.slot_gate
  88.9 16.5 %all-to-all-done.2 = bf16[32,32,256]{2,1,0:T(8,128)(2,1)S(1)} async-done(((bf16[32,32,256]{2,1,0:T(8,128)(2,1)}), bf16[32,32,256]{2,1,0:T(8,128)(2,1)S(1)}, u32[]{:S(2)}, u32[]{:S(2)}) %all-to-all-start.2) | async-done | bytes 524320 | tf_op jit(solution)/shard_map/all_to_all | solution.py:20
  105.4 0.7 reduce_sum.12.owned
  106.1 7.9 %expert.1 = (bf16[192,512]{1,0:T(8,128)(2,1)}, bf16[192,512]{1,0:T(8,128)(2,1)}, bf16[192,512]{1,0:T(8,128)(2,1)}, f32[1,512]{1,0:T(1,128)}) custom-call(bf16[192,4096]{1,0:T(8,128)(2,1)} %bitcast.20, bf16[512,4096]{1,0:T(8,128)(2,1)} %all-gather.2.cloned.1.call-done.rows, bf16[192,512]{1,0:T(8,128)(2,1)} %bitcast.26, bf16[192,512]{1,0:T(8,128)(2,1)} %bitcast.27, ...), custom_call_target="tpu_custom_call" | custom-call | flops 1000000000 | bytes 7000000 | tf_op jit(solution)/shard_map/expert/pallas_call | solution.py:274
  114.0 1.4 merge.1
  115.4 16.6 %all_to_all.27.terms = bf16[8,40,256]{2,1,0:T(8,128)(2,1)} all-to-all(bf16[8,40,256]{2,1,0:T(8,128)(2,1)} %merge.1), channel_id=1, replica_groups=mesh['z'=8,'x'=4,'c'=2,'ta'=8] {'ta'}, dimensions={0} | all-to-all | bytes 327680 | tf_op jit(solution)/shard_map/all_to_all | solution.py:20
  132.1 1.8 %middle.1 = f32[64,1,128]{2,1,0:T(1,128)} custom-call(s32[3]{0:T(128)} %pad_add_fusion.where, bf16[8,40,256]{2,1,0:T(8,128)(2,1)} %all_to_all.27.terms), custom_call_target="tpu_custom_call" | custom-call | flops 1000000 | bytes 100000 | tf_op jit(solution)/shard_map/middle/pallas_call | solution.py:33
  133.8 6.0 %all-to-all-start.4 = ((f32[64,1,128]{2,1,0:T(1,128)}), f32[64,1,128]{2,1,0:T(1,128)S(1)}, u32[]{:S(2)}, u32[]{:S(2)}) async-start(f32[64,1,128]{2,1,0:T(1,128)} %middle.1), calls=%async_computation.4 | async-start | bytes 65536 | tf_op jit(solution)/shard_map/all_to_all | solution.py:20
  139.8 6.9 %down.1 = bf16[192,4096]{1,0:T(8,128)(2,1)} custom-call(bf16[192,512]{1,0:T(8,128)(2,1)} %get-tuple-element.20.weighted, bf16[512,4096]{1,0:T(8,128)(2,1)} %all-gather.2.cloned.1.call-done.rows), custom_call_target="tpu_custom_call" | custom-call | flops 1000000000 | bytes 6000000 | tf_op jit(solution)/shard_map/down/pallas_call | solution.py:292
  146.8 1.6 %heads.1 = (f32[32,512]{1,0:T(8,128)}, f32[32,512]{1,0:T(8,128)}) custom-call(s32[3]{0:T(128)} %pad_add_fusion.where, bf16[8,40,256]{2,1,0:T(8,128)(2,1)} %all_to_all.27.terms), custom_call_target="tpu_custom_call" | custom-call | flops 1000000 | bytes 1000000 | tf_op jit(solution)/shard_map/heads/pallas_call | solution.py:33
  148.4 0.0 all-to-all-done.4.returned
  148.4 0.6 copy-done.2
  149.0 2.0 %gates.1 = f32[8,32]{1,0:T(8,128)} custom-call(s32[3]{0:T(128)} %pad_add_fusion.where, s32[8,32]{1,0:T(8,128)} %bitcast.29, s32[8,32]{1,0:T(8,128)} %get-tuple-element.23.ranks, f32[64,1,128]{2,1,0:T(1,128)} %copy-done.2), custom_call_target="tpu_custom_call" | custom-call | flops 1000000 | bytes 100000 | tf_op jit(solution)/shard_map/gates/pallas_call | solution.py:33
  (4 shorter events, 0.0 us)
Async XLA Ops:
  7.2 98.9 %all-gather.2.cloned.1.call-start = ((), (), s32[]{:S(2)}) async-start(), calls=%async_computation.5 | async-start | bytes 4718592 | tf_op jit(solution)/shard_map/all_gather | solution.py:250
  10.8 35.2 %copy-start.1 = (bf16[1024,256]{1,0:T(8,128)(2,1)S(1)}, bf16[1024,256]{1,0:T(8,128)(2,1)}, u32[]{:S(2)}) copy-start(bf16[1024,256]{1,0:T(8,128)(2,1)} %get-tuple-element.24) | copy-start | bytes 1572868
  67.9 3.8 %copy-start = (bf16[32,32,256]{2,1,0:T(8,128)(2,1)}, bf16[32,32,256]{2,1,0:T(8,128)(2,1)S(1)}, u32[]{:S(2)}) copy-start(bf16[32,32,256]{2,1,0:T(8,128)(2,1)S(1)} %all_to_all.26) | copy-start | bytes 1572868
  67.9 3.8 %collective-permute-start = (bf16[1024,256]{1,0:T(8,128)(2,1)S(1)}, bf16[1024,256]{1,0:T(8,128)(2,1)S(1)}, u32[]{:S(2)}, u32[]{:S(2)}) collective-permute-start(bf16[1024,256]{1,0:T(8,128)(2,1)S(1)} %bitcast.23), channel_id=1, source_target_pairs={{0,8},{8,0},{1,9},{9,1},{2,10},{10,2},{3,11},{11,3},{4,12},{12,4},... | collective-permute-start | bytes 1572872 | tf_op jit(solution)/shard_map/ppermute | solution.py:24
  71.7 0.8 copy-start.3
  76.7 4.0 %collective-permute-start.1 = (bf16[1024,256]{1,0:T(8,128)(2,1)}, bf16[1024,256]{1,0:T(8,128)(2,1)S(1)}, u32[]{:S(2)}, u32[]{:S(2)}) collective-permute-start(bf16[1024,256]{1,0:T(8,128)(2,1)} %get-tuple-element.26), channel_id=1, source_target_pairs={{0,8},{8,0},{1,9},{9,1},{2,10},{10,2},{3,11},{11,3},{4,12},{12,4},... | collective-permute-start | bytes 1572872 | tf_op jit(solution)/shard_map/ppermute | solution.py:24
  82.7 22.7 %all-to-all-start.2 = ((bf16[32,32,256]{2,1,0:T(8,128)(2,1)}), bf16[32,32,256]{2,1,0:T(8,128)(2,1)S(1)}, u32[]{:S(2)}, u32[]{:S(2)}) async-start(bf16[32,32,256]{2,1,0:T(8,128)(2,1)} %bitcast.16), calls=%async_computation.2 | async-start | bytes 1048576 | tf_op jit(solution)/shard_map/all_to_all | solution.py:20
  133.8 14.5 %all-to-all-start.4 = ((f32[64,1,128]{2,1,0:T(1,128)}), f32[64,1,128]{2,1,0:T(1,128)S(1)}, u32[]{:S(2)}, u32[]{:S(2)}) async-start(f32[64,1,128]{2,1,0:T(1,128)} %middle.1), calls=%async_computation.4 | async-start | bytes 65536 | tf_op jit(solution)/shard_map/all_to_all | solution.py:20
  148.4 0.6 copy-start.2
Sparse Core Ops, SparseCore 0:
  46.1 53.6 all-gather.1

commit v4 on v3

v4 whole, which is shorter than its diff:
```python
import jax
import jax.numpy as jnp
from jax import lax
from jax.experimental import pallas as pl
from jax.experimental.pallas import tpu as pltpu
from jax.sharding import Mesh, PartitionSpec as P

H = 64
KVH = 4
HD = 128
GX = ("z", "x", "c")
ZX = ("z", "x")
NT = (((1,), (1,)), ((), ()))
TN = (((0,), (0,)), ((), ()))
F32 = jnp.float32
BF16 = jnp.bfloat16


def exchange(values, axes):
    return lax.all_to_all(values, axes, split_axis=0, concat_axis=0, tiled=True)


def swap(values, axis, bit):
    n = lax.axis_size(axis)
    return lax.ppermute(values, axis, [(i, i ^ bit) for i in range(n)])


def iota(shape, dim):
    return lax.broadcasted_iota(jnp.int32, shape, dim)


def call(body, outs, ins, flops, size, scratch=()):
    vmem = pl.BlockSpec(memory_space=pltpu.VMEM)
    return pl.pallas_call(
        body,
        out_shape=outs,
        in_specs=[pl.BlockSpec(memory_space=pltpu.SMEM)] + [vmem] * (len(ins) - 1),
        out_specs=jax.tree.map(lambda _: vmem, outs),
        cost_estimate=pl.CostEstimate(flops=flops, bytes_accessed=size, transcendentals=0),
        scratch_shapes=scratch,
    )(*ins)


def pack_body(where, kept, ids, gates, d_out, keys, values, message, kv, ranks):
    top, rows = ids.shape
    slots = message.shape[0]
    tok_dev, width = d_out.shape
    cap = 8
    head = pl.multiple_of(where[0] * HD, HD)
    slot = iota((slots, rows), 0)
    expert = slot // cap
    place = (slot % cap).astype(F32)
    named = jnp.zeros((slots, rows), F32)
    weight = jnp.zeros((slots, rows), F32)
    for j in range(top):
        hit = ids[j : j + 1, :] == expert
        named = jnp.where(hit, 1.0, named)
        weight = jnp.where(hit, gates[j : j + 1, :].astype(F32), weight)
    before = jnp.where(iota((rows, rows), 0) < iota((rows, rows), 1), 1.0, 0.0).astype(BF16)
    rank = jnp.dot(named.astype(BF16), before, preferred_element_type=F32)
    taken = jnp.where((named > 0.0) & (rank == place), 1.0, 0.0)
    pick = jnp.where(kept[...] % tok_dev == iota((tok_dev, rows), 0), 1.0, 0.0).astype(BF16)
    picked = lax.dot_general(pick, d_out[...], TN, preferred_element_type=F32).astype(BF16)
    message[:, :width] = jnp.dot(
        taken.astype(BF16), picked, preferred_element_type=F32
    ).astype(BF16)
    message[:, width:] = jnp.dot(
        (taken * weight).astype(BF16), jnp.ones((rows, HD), BF16), preferred_element_type=F32
    ).astype(BF16)
    for at, source in ((0, keys), (HD, values)):
        kv[:, at : at + HD] = source[:, pl.ds(head, HD)]
    for j in range(top):
        mine = jnp.where((ids[j : j + 1, :] == expert) & (taken > 0.0), place, 0.0)
        ranks[j : j + 1, :] = jnp.sum(mine, axis=0, keepdims=True).astype(jnp.int32)


def attention_body(where, query, grad, mine_in, other_in, d_query, keep, send, mine, other):
    core, block = where[0], where[1]
    keep_dev = query.shape[0]
    heads = query.shape[1] // HD
    rows = keep_dev * heads
    half = mine.shape[0]
    scale = HD ** (-0.5)
    chips = half // keep_dev
    for k in range(chips):
        flip = (k % 8) * 4 + k // 8
        to = pl.ds(pl.multiple_of((block // 2 ^ flip) * keep_dev, keep_dev), keep_dev)
        mine[to, :] = mine_in[k * keep_dev : (k + 1) * keep_dev]
        other[to, :] = other_in[k * keep_dev : (k + 1) * keep_dev]

    def stacked(ref):
        return jnp.concatenate([ref[:, g * HD : (g + 1) * HD] for g in range(heads)], axis=0)

    q = stacked(query)
    o = stacked(grad)
    query_pos = block * keep_dev + iota((rows, half), 0) % keep_dev
    column = iota((rows, half), 1)
    base = column // keep_dev * (2 * keep_dev) + column % keep_dev
    scores = []
    for ref, owner in ((mine, core), (other, 1 - core)):
        s = lax.dot_general(q, ref[:, :HD], NT, preferred_element_type=F32) * scale
        scores.append(jnp.where(base + owner * keep_dev <= query_pos, s, -1e30))
    top = jnp.maximum(*[jnp.max(s, axis=1, keepdims=True) for s in scores])
    expo = [jnp.exp(s - top) for s in scores]
    inv = 1.0 / sum(jnp.sum(e, axis=1, keepdims=True) for e in expo)
    probs = [e * inv for e in expo]
    dps = [
        lax.dot_general(o, ref[:, HD:], NT, preferred_element_type=F32) for ref in (mine, other)
    ]
    mean = sum(jnp.sum(p * dp, axis=1, keepdims=True) for p, dp in zip(probs, dps))
    dq = jnp.zeros((rows, HD), F32)
    for ref, p, dp, out in zip((other, mine), probs[::-1], dps[::-1], (send, keep)):
        ds = (p * (dp - mean)).astype(BF16)
        dk = lax.dot_general(ds, q, TN, preferred_element_type=F32) * scale
        dv = lax.dot_general(p.astype(BF16), o, TN, preferred_element_type=F32)
        out[:, :HD] = dk.astype(BF16)
        out[:, HD:] = dv.astype(BF16)
        dq = dq + jnp.dot(ds, ref[:, :HD], preferred_element_type=F32)
    dq = (dq * scale).astype(BF16)
    for g in range(heads):
        d_query[:, g * HD : (g + 1) * HD] = dq[g * keep_dev : (g + 1) * keep_dev]


def expert_body(weight, rows, gate_pre, up_pre, slot_gate, d_gate, d_up, weighted, dots):
    z = lax.dot_general(weight[...], rows[...], NT, preferred_element_type=F32)
    g = gate_pre[...].astype(F32)
    u = up_pre[...].astype(F32)
    sig = 1.0 / (1.0 + jnp.exp(-g))
    act = g * sig
    hidden = act * u
    one = jnp.where(iota((8, HD), 1) == 0, 1.0, 0.0).astype(BF16)
    scale = lax.dot_general(one, slot_gate[...], NT, preferred_element_type=F32)[0:1]
    grad_hidden = z * scale
    d_up[...] = (grad_hidden * act).astype(BF16)
    d_gate[...] = (grad_hidden * u * sig * (1.0 + g * (1.0 - sig))).astype(BF16)
    weighted[...] = (hidden * scale).astype(BF16)
    blocks, _, lanes = dots.shape
    cap = z.shape[1] // blocks
    spread = jnp.where(
        iota((blocks, lanes), 1) // cap == iota((blocks, lanes), 0),
        jnp.sum(hidden * z, axis=0, keepdims=True),
        0.0,
    )
    place = jnp.where(iota((lanes, lanes), 0) % cap == iota((lanes, lanes), 1), 1.0, 0.0)
    dots[...] = jnp.dot(
        spread, place, preferred_element_type=F32, precision=lax.Precision.HIGHEST
    )[:, None, :]


def down_body(weighted, rows, out):
    out[...] = jnp.dot(weighted[...], rows[...], preferred_element_type=F32).astype(BF16)


def gates_body(where, ids, ranks, returned, out):
    top, rows = ids.shape
    experts = returned.shape[0]
    table = returned[...].reshape(experts, HD)
    result = jnp.zeros((top, HD), F32)
    for j in range(top):
        pick = jnp.where(
            jnp.concatenate([ids[j : j + 1, :]] * (HD // rows), axis=1) == iota((experts, HD), 0),
            1.0,
            0.0,
        )
        found = lax.dot_general(
            table, pick, TN, preferred_element_type=F32, precision=lax.Precision.HIGHEST
        )
        rank = jnp.concatenate([ranks[j : j + 1, :]] * (HD // rows), axis=1)
        hit = jnp.where(iota((HD, HD), 0) == rank, found, 0.0)
        result = jnp.where(iota((top, HD), 0) == j, jnp.sum(hit, axis=0, keepdims=True), result)
    for i in range(out.shape[0]):
        out[i] = result


def total_body(where, terms, out):
    out[...] = jnp.sum(terms[...], axis=0)[:, : out.shape[1]]


def heads_body(where, terms, d_key, d_value):
    keep_dev = d_key.shape[0]
    per = terms.shape[0] // KVH
    for h in range(KVH):
        both = sum(terms[h * per + i, :keep_dev].astype(F32) for i in range(per))
        d_key[:, h * HD : (h + 1) * HD] = both[:, :HD]
        d_value[:, h * HD : (h + 1) * HD] = both[:, HD:]


def on_device(
    d_out, kept, expert_ids, gates, down_weight, gate_pre, up_pre, query, keys, values, d_attn
):
    core = lax.axis_index("c")
    chips = lax.axis_size(ZX)
    me = lax.axis_index("ta")
    n_experts = lax.axis_size(GX)
    n_ta = lax.axis_size("ta")
    keep_dev = kept.shape[0]
    width = d_out.shape[1]
    top = expert_ids.shape[1]
    slots = gate_pre.shape[2]
    cap = slots // n_experts
    hidden = gate_pre.shape[1]
    struct = jax.ShapeDtypeStruct
    ids = expert_ids.T

    local_heads = query.shape[1] // HD
    first_kv = (me * local_heads // (H // KVH)).astype(jnp.int32)
    where = jnp.stack([first_kv, core.astype(jnp.int32), lax.axis_index(GX).astype(jnp.int32)])
    message, kv, ranks = call(
        pack_body,
        (
            struct((slots, width + HD), BF16),
            struct((keep_dev, 2 * HD), BF16),
            struct((top, keep_dev), jnp.int32),
        ),
        (where, kept.reshape(1, keep_dev), ids, gates.T, d_out, keys, values),
        200_000_000,
        3_000_000,
    )
    arrived = exchange(message.reshape(n_experts, cap, -1), GX)
    arrived = arrived.reshape(slots, -1)
    slot_rows = lax.all_gather(arrived[:, :width], "ta", axis=1, tiled=True)
    slot_gate = arrived[:, width:]

    kv_mine = kv
    for axis, bits in (("z", (1, 2, 4)), ("x", (1, 2))):
        for bit in bits:
            got = swap(kv_mine, axis, bit)
            kv_mine = lax.optimization_barrier(jnp.concatenate([kv_mine, got], axis=0))
    kv_other = swap(kv_mine, "c", 1)
    half = chips * keep_dev
    d_query, keep, send = call(
        attention_body,
        (
            struct((keep_dev, local_heads * HD), BF16),
            struct((half, 2 * HD), BF16),
            struct((half, 2 * HD), BF16),
        ),
        (where[1:], query, d_attn, kv_mine, kv_other),
        1_000_000_000,
        4_000_000,
        [pltpu.VMEM((half, 2 * HD), BF16)] * 2,
    )
    chip_part = (keep.astype(F32) + swap(send, "c", 1).astype(F32)).astype(BF16)
    summed = exchange(chip_part.reshape(chips, keep_dev, 2 * HD), ZX)
    owned = jnp.sum(summed.astype(F32), axis=0).astype(BF16)

    copies = exchange(jnp.broadcast_to(owned[None], (n_ta,) + owned.shape), "ta")
    d_key, d_value = call(
        heads_body,
        (struct((keep_dev, KVH * HD), F32), struct((keep_dev, KVH * HD), F32)),
        (where, copies),
        1_000_000,
        1_000_000,
    )

    steps = 4
    some = slots // steps
    few = pl.BlockSpec((hidden, some), lambda i: (0, i))
    blocks = n_experts // steps
    d_gate, d_up, weighted, dots = pl.pallas_call(
        expert_body,
        grid=(steps,),
        in_specs=[
            pl.BlockSpec((hidden, n_ta * width), lambda i: (0, 0)),
            pl.BlockSpec((some, n_ta * width), lambda i: (i, 0)),
            few,
            few,
            pl.BlockSpec((some, HD), lambda i: (i, 0)),
        ],
        out_specs=[few, few, few, pl.BlockSpec((blocks, 1, HD), lambda i: (i, 0, 0))],
        out_shape=[struct((hidden, slots), BF16)] * 3 + [struct((n_experts, 1, HD), F32)],
        cost_estimate=pl.CostEstimate(
            flops=1_000_000_000, bytes_accessed=7_000_000, transcendentals=0
        ),
        name="expert",
    )(down_weight[0], slot_rows, gate_pre[0], up_pre[0], slot_gate)
    columns = n_ta * width // steps
    d_down = pl.pallas_call(
        down_body,
        grid=(steps,),
        in_specs=[
            pl.BlockSpec((hidden, slots), lambda i: (0, 0)),
            pl.BlockSpec((slots, columns), lambda i: (0, i)),
        ],
        out_specs=pl.BlockSpec((hidden, columns), lambda i: (0, i)),
        out_shape=struct(down_weight.shape[1:], BF16),
        cost_estimate=pl.CostEstimate(
            flops=1_000_000_000, bytes_accessed=6_000_000, transcendentals=0
        ),
        name="down",
    )(weighted, slot_rows)
    returned = exchange(dots, GX)
    terms = call(
        gates_body, struct((n_ta, top, HD), F32), (where, ids, ranks, returned), 1_000_000, 100_000
    )
    d_gates = call(
        total_body, struct((top, keep_dev), F32), (where, exchange(terms, "ta")), 100_000, 100_000
    ).T
    return (d_down[None], d_gate[None], d_up[None], d_gates, d_query, d_key, d_value)


def solution(mesh):
    shape = dict(mesh.shape)
    fine = Mesh(mesh.devices.reshape(8, shape["gx"] // 16, 2, shape["ta"]), GX + ("ta",))
    in_specs = (
        P(GX, "ta"),
        P(GX),
        P(GX, None),
        P(GX, None),
        P(GX, "ta", None),
        P(GX, "ta", None),
        P(GX, "ta", None),
        P(GX, "ta"),
        P(GX, None),
        P(GX, None),
        P(GX, "ta"),
    )
    out_specs = (
        P(GX, "ta", None),
        P(GX, "ta", None),
        P(GX, "ta", None),
        P(GX, None),
        P(GX, "ta"),
        P(GX, None),
        P(GX, None),
    )
    return jax.shard_map(
        on_device, mesh=fine, in_specs=in_specs, out_specs=out_specs, check_vma=False
    )
```

time: 161 us -> 180 us (1.12)
  waiting for transfers between devices: 19.7 us -> 41.2 us
  starting transfers between devices: 15.6 us -> 36.2 us
  blocking collectives: 72.8 us -> 56.7 us
  Pallas kernels: 28.8 us -> 23.2 us
    ppermute x2 -> x7, waiting for transfers between devices: 3.22 us -> 29.5 us  [swap(): return lax.ppermute(values, axis, [(i, i ^ bit) for i in range(n)])]
    all_to_all x3 -> x2, blocking collectives: 72.8 us -> 56.7 us  [exchange(): return lax.all_to_all(values, axes, split_axis=0, concat_axis=0, tiled=True)]
    ppermute x2 -> x7, starting transfers between devices: 3.97 us -> 18 us  [swap(): return lax.ppermute(values, axis, [(i, i ^ bit) for i in range(n)])]
    all_to_all x2 -> x3, starting transfers between devices: 11.6 us -> 18.2 us  [exchange(): return lax.all_to_all(values, axes, split_axis=0, concat_axis=0, tiled=True)]
    all_to_all x2 -> x3, waiting for transfers between devices: 16.5 us -> 11.7 us  [exchange(): return lax.all_to_all(values, axes, split_axis=0, concat_axis=0, tiled=True)]
    pallas_call x1, Pallas kernels: 6.95 us -> 4.82 us  [on_device(): pl.pallas_call(down_body, grid=(steps,), in_specs=[pl.BlockSpec((hidden,...]
    pallas_call x6 -> x5, Pallas kernels: 14 us -> 12 us  [call(): pl.pallas_call(body, out_shape=outs, in_specs=[pl.BlockSpec(memory_space=...]
  transfers between devices with their start and end apart: 5 -> 11, of which waited for: 3 -> 10; matrix products, arithmetic and copies ran while one was open for 2% -> 2% of each run, Pallas kernels for 8% -> 10%
where the time goes in v4:
time: 180 us; the launch traced here: 178 us
  blocking collectives  56.7 us (32%)
  waiting for transfers between devices  41.2 us (23%)
  starting transfers between devices  36.2 us (20%)
  Pallas kernels  23.2 us (13%)
  between operations  14.2 us (8%)
  local copies, waits for them, and re-layouts  4.15 us (2%)
  other arithmetic  2.58 us (1%)
    all_to_all x2, blocking collectives, exchange(): return lax.all_to_all(values, axes, split_axis=0, concat_axis=0, tiled=True)  56.7 us
    ppermute x7, waiting for transfers between devices, swap(): return lax.ppermute(values, axis, [(i, i ^ bit) for i in range(n)])  29.5 us
    all_to_all x3, starting transfers between devices, exchange(): return lax.all_to_all(values, axes, split_axis=0, concat_axis=0, tiled=True)  18.2 us
    ppermute x7, starting transfers between devices, swap(): return lax.ppermute(values, axis, [(i, i ^ bit) for i in range(n)])  18 us
    pallas_call x5, Pallas kernels, call(): pl.pallas_call(body, out_shape=outs, in_specs=[pl.BlockSpec(memory_space=...  12 us
    all_to_all x3, waiting for transfers between devices, exchange(): return lax.all_to_all(values, axes, split_axis=0, concat_axis=0, tiled=True)  11.7 us
    pallas_call x1, Pallas kernels, on_device(): pl.pallas_call(expert_body, grid=(steps,), in_specs=[pl.BlockSpec((hidden...  6.29 us
    pallas_call x1, Pallas kernels, on_device(): pl.pallas_call(down_body, grid=(steps,), in_specs=[pl.BlockSpec((hidden,...  4.82 us
  transfers between devices with their start and end apart: 11, of which 10 were waited for; matrix products, arithmetic and copies ran while one was open for 2% of the time, Pallas kernels for 10%

profile of v4, /device:TPU:6, one launch (start us, length us, event | category | flops | bytes accessed | tf_op | source)
XLA Modules:
  0.0 178.1 jit_solution(10092747400012612012)
XLA Ops:
  7.9 2.8 %shard_map.162 = (bf16[512,640]{1,0:T(8,128)(2,1)}, bf16[32,256]{1,0:T(8,128)(2,1)}, s32[8,32]{1,0:T(8,128)}) custom-call(s32[3]{0:T(128)} %pad_add_fusion.where, s32[1,32]{1,0:T(1,128)} %bitcast.30, s32[8,32]{1,0:T(8,128)} %bitcast.24, bf16[8,32]{1,0:T(8,128)(2,1)} %bitcast.29, bf16[256,512]{1,0:T(8,128)(2,1)} %d_out.1, bf16[32,512]{1,0:T(8,128)(2,1)} %keys.1, ...), custom_call_target="tpu_custom_call" | custom-call | flops 200000000 | bytes 3000000 | tf_op jit(solution)/shard_map/pallas_call | solution.py:34
  10.7 34.3 %all_to_all.25 = bf16[64,8,640]{2,1,0:T(8,128)(2,1)S(1)} all-to-all(bf16[64,8,640]{2,1,0:T(8,128)(2,1)} %bitcast.21), channel_id=1, replica_groups=mesh['z'=8,'x'=4,'c'=2,'ta'=8] {'z','x','c'}, dimensions={0} | all-to-all | bytes 1310720 | tf_op jit(solution)/shard_map/all_to_all | solution.py:20
  45.0 0.8 slice.10
  45.9 2.6 %collective-permute-start = (bf16[32,256]{1,0:T(8,128)(2,1)S(1)}, bf16[32,256]{1,0:T(8,128)(2,1)S(1)}, u32[]{:S(2)}, u32[]{:S(2)}) collective-permute-start(bf16[32,256]{1,0:T(8,128)(2,1)S(1)} %copy-done.4), channel_id=1, source_target_pairs={{0,64},{64,0},{128,192},{192,128},{256,320},{320,256},{384,448},{4... | collective-permute-start | bytes 49160 | tf_op jit(solution)/shard_map/ppermute | solution.py:25
  48.4 3.1 %collective-permute-done = bf16[32,256]{1,0:T(8,128)(2,1)S(1)} collective-permute-done((bf16[32,256]{1,0:T(8,128)(2,1)S(1)}, bf16[32,256]{1,0:T(8,128)(2,1)S(1)}, u32[]{:S(2)}, u32[]{:S(2)}) %collective-permute-start) | collective-permute-done | bytes 16416 | tf_op jit(solution)/shard_map/ppermute | solution.py:25
  51.5 3.2 %collective-permute-start.1 = (bf16[64,256]{1,0:T(8,128)(2,1)S(1)}, bf16[64,256]{1,0:T(8,128)(2,1)S(1)}, u32[]{:S(2)}, u32[]{:S(2)}) collective-permute-start(bf16[64,256]{1,0:T(8,128)(2,1)S(1)} %pad_maximum_fusion.4), channel_id=1, source_target_pairs={{0,128},{64,192},{128,0},{192,64},{256,384},{320,448},{384,256},{4... | collective-permute-start | bytes 98312 | tf_op jit(solution)/shard_map/ppermute | solution.py:25
  54.7 3.9 %collective-permute-done.1 = bf16[64,256]{1,0:T(8,128)(2,1)S(1)} collective-permute-done((bf16[64,256]{1,0:T(8,128)(2,1)S(1)}, bf16[64,256]{1,0:T(8,128)(2,1)S(1)}, u32[]{:S(2)}, u32[]{:S(2)}) %collective-permute-start.1) | collective-permute-done | bytes 32800 | tf_op jit(solution)/shard_map/ppermute | solution.py:25
  58.5 2.4 %collective-permute-start.2 = (bf16[128,256]{1,0:T(8,128)(2,1)S(1)}, bf16[128,256]{1,0:T(8,128)(2,1)S(1)}, u32[]{:S(2)}, u32[]{:S(2)}) collective-permute-start(bf16[128,256]{1,0:T(8,128)(2,1)S(1)} %pad_maximum_fusion.3), channel_id=1, source_target_pairs={{0,256},{64,320},{128,384},{192,448},{256,0},{320,64},{384,128},{4... | collective-permute-start | bytes 196616 | tf_op jit(solution)/shard_map/ppermute | solution.py:25
  61.0 7.7 %collective-permute-done.2 = bf16[128,256]{1,0:T(8,128)(2,1)S(1)} collective-permute-done((bf16[128,256]{1,0:T(8,128)(2,1)S(1)}, bf16[128,256]{1,0:T(8,128)(2,1)S(1)}, u32[]{:S(2)}, u32[]{:S(2)}) %collective-permute-start.2) | collective-permute-done | bytes 65568 | tf_op jit(solution)/shard_map/ppermute | solution.py:25
  68.7 2.7 %collective-permute-start.3 = (bf16[256,256]{1,0:T(8,128)(2,1)S(1)}, bf16[256,256]{1,0:T(8,128)(2,1)S(1)}, u32[]{:S(2)}, u32[]{:S(2)}) collective-permute-start(bf16[256,256]{1,0:T(8,128)(2,1)S(1)} %pad_maximum_fusion.2), channel_id=1, source_target_pairs={{0,16},{16,0},{32,48},{48,32},{1,17},{17,1},{33,49},{49,33},{2,18}... | collective-permute-start | bytes 393224 | tf_op jit(solution)/shard_map/ppermute | solution.py:25
  71.4 5.0 %collective-permute-done.3 = bf16[256,256]{1,0:T(8,128)(2,1)S(1)} collective-permute-done((bf16[256,256]{1,0:T(8,128)(2,1)S(1)}, bf16[256,256]{1,0:T(8,128)(2,1)S(1)}, u32[]{:S(2)}, u32[]{:S(2)}) %collective-permute-start.3) | collective-permute-done | bytes 131104 | tf_op jit(solution)/shard_map/ppermute | solution.py:25
  76.4 3.2 %collective-permute-start.4 = (bf16[512,256]{1,0:T(8,128)(2,1)S(1)}, bf16[512,256]{1,0:T(8,128)(2,1)S(1)}, u32[]{:S(2)}, u32[]{:S(2)}) collective-permute-start(bf16[512,256]{1,0:T(8,128)(2,1)S(1)} %pad_maximum_fusion.1), channel_id=1, source_target_pairs={{0,32},{16,48},{32,0},{48,16},{1,33},{17,49},{33,1},{49,17},{2,34}... | collective-permute-start | bytes 786440 | tf_op jit(solution)/shard_map/ppermute | solution.py:25
  79.6 6.6 %collective-permute-done.4 = bf16[512,256]{1,0:T(8,128)(2,1)S(1)} collective-permute-done((bf16[512,256]{1,0:T(8,128)(2,1)S(1)}, bf16[512,256]{1,0:T(8,128)(2,1)S(1)}, u32[]{:S(2)}, u32[]{:S(2)}) %collective-permute-start.4) | collective-permute-done | bytes 262176 | tf_op jit(solution)/shard_map/ppermute | solution.py:25
  86.2 1.9 %collective-permute-start.5 = (bf16[1024,256]{1,0:T(8,128)(2,1)S(1)}, bf16[1024,256]{1,0:T(8,128)(2,1)S(1)}, u32[]{:S(2)}, u32[]{:S(2)}) collective-permute-start(bf16[1024,256]{1,0:T(8,128)(2,1)S(1)} %pad_maximum_fusion.mine_in), channel_id=1, source_target_pairs={{0,8},{8,0},{1,9},{9,1},{2,10},{10,2},{3,11},{11,3},{4,12},{12,4},... | collective-permute-start | bytes 1572872 | tf_op jit(solution)/shard_map/ppermute | solution.py:25
  88.8 1.3 collective-permute-done.5.other_in
  90.0 0.8 copy-done.5
  90.8 4.3 %shard_map.165 = (bf16[32,1024]{1,0:T(8,128)(2,1)}, bf16[1024,256]{1,0:T(8,128)(2,1)}, bf16[1024,256]{1,0:T(8,128)(2,1)}) custom-call(s32[2]{0:T(128)} %pad_add_fusion.1.where, bf16[32,1024]{1,0:T(8,128)(2,1)} %query.1, bf16[32,1024]{1,0:T(8,128)(2,1)} %grad.1, bf16[1024,256]{1,0:T(8,128)(2,1)} %copy-done, bf16[1024,256]{1,0:T(8,128)(2,1)} %copy-done.5), custom_call_target="tpu_custom_call" | custom-call | flops 1000000000 | bytes 4000000 | tf_op jit(solution)/shard_map/pallas_call | solution.py:34
  95.1 2.1 %collective-permute-start.6 = (bf16[1024,256]{1,0:T(8,128)(2,1)}, bf16[1024,256]{1,0:T(8,128)(2,1)S(1)}, u32[]{:S(2)}, u32[]{:S(2)}) collective-permute-start(bf16[1024,256]{1,0:T(8,128)(2,1)} %get-tuple-element.28), channel_id=1, source_target_pairs={{0,8},{8,0},{1,9},{9,1},{2,10},{10,2},{3,11},{11,3},{4,12},{12,4},... | collective-permute-start | bytes 1572872 | tf_op jit(solution)/shard_map/ppermute | solution.py:25
  97.2 1.9 %collective-permute-done.6 = bf16[1024,256]{1,0:T(8,128)(2,1)S(1)} collective-permute-done((bf16[1024,256]{1,0:T(8,128)(2,1)}, bf16[1024,256]{1,0:T(8,128)(2,1)S(1)}, u32[]{:S(2)}, u32[]{:S(2)}) %collective-permute-start.6) | collective-permute-done | bytes 524320 | tf_op jit(solution)/shard_map/ppermute | solution.py:25
  99.1 1.2 add_convert_fusion
  100.3 22.4 %all_to_all.26 = bf16[32,32,256]{2,1,0:T(8,128)(2,1)S(1)} all-to-all(bf16[32,32,256]{2,1,0:T(8,128)(2,1)S(1)} %bitcast.18), channel_id=1, replica_groups=mesh['z'=8,'x'=4,'c'=2,'ta'=8] {'z','x'}, dimensions={0} | all-to-all | bytes 1048576 | tf_op jit(solution)/shard_map/all_to_all | solution.py:20
  123.4 7.1 %all-to-all-start.4 = ((bf16[8,32,256]{2,1,0:T(8,128)(2,1)}), bf16[8,32,256]{2,1,0:T(8,128)(2,1)S(1)}, u32[]{:S(2)}, u32[]{:S(2)}) async-start(bf16[8,32,256]{2,1,0:T(8,128)(2,1)} %broadcast_in_dim.18), calls=%async_computation.4 | async-start | bytes 262144 | tf_op jit(solution)/shard_map/all_to_all | solution.py:20
  131.2 6.3 %expert.1 = (bf16[192,512]{1,0:T(8,128)(2,1)}, bf16[192,512]{1,0:T(8,128)(2,1)}, bf16[192,512]{1,0:T(8,128)(2,1)}, f32[64,1,128]{2,1,0:T(1,128)}) custom-call(bf16[192,4096]{1,0:T(8,128)(2,1)} %bitcast.19, bf16[512,4096]{1,0:T(8,128)(2,1)} %all-gather.2.cloned.1.call-done.rows, bf16[192,512]{1,0:T(8,128)(2,1)} %bitcast.22, bf16[192,512]{1,0:T(8,128)(2,1)} %bitcast.23, ...), custom_call_target="tpu_custom_call" | custom-call | flops 1000000000 | bytes 7000000 | tf_op jit(solution)/shard_map/expert/pallas_call | solution.py:260
  137.5 2.1 %all-to-all-done.4.terms = bf16[8,32,256]{2,1,0:T(8,128)(2,1)S(1)} async-done(((bf16[8,32,256]{2,1,0:T(8,128)(2,1)}), bf16[8,32,256]{2,1,0:T(8,128)(2,1)S(1)}, u32[]{:S(2)}, u32[]{:S(2)}) %all-to-all-start.4) | async-done | bytes 131104 | tf_op jit(solution)/shard_map/all_to_all | solution.py:20
  139.6 6.0 %all-to-all-start.1 = ((f32[64,1,128]{2,1,0:T(1,128)}), f32[64,1,128]{2,1,0:T(1,128)S(1)}, u32[]{:S(2)}, u32[]{:S(2)}) async-start(f32[64,1,128]{2,1,0:T(1,128)} %get-tuple-element.24), calls=%async_computation.1 | async-start | bytes 65536 | tf_op jit(solution)/shard_map/all_to_all | solution.py:20
  145.6 1.6 shard_map.166
  147.2 6.3 %all-to-all-done.1.returned = f32[64,1,128]{2,1,0:T(1,128)S(1)} async-done(((f32[64,1,128]{2,1,0:T(1,128)}), f32[64,1,128]{2,1,0:T(1,128)S(1)}, u32[]{:S(2)}, u32[]{:S(2)}) %all-to-all-start.1) | async-done | bytes 32800 | tf_op jit(solution)/shard_map/all_to_all | solution.py:20
  154.1 2.0 %shard_map.163 = f32[8,8,128]{2,1,0:T(8,128)} custom-call(s32[3]{0:T(128)} %pad_add_fusion.where, s32[8,32]{1,0:T(8,128)} %bitcast.25, s32[8,32]{1,0:T(8,128)} %get-tuple-element.23.ranks, f32[64,1,128]{2,1,0:T(1,128)} %copy-done.2), custom_call_target="tpu_custom_call" | custom-call | flops 1000000 | bytes 100000 | tf_op jit(solution)/shard_map/pallas_call | solution.py:34
  156.2 5.1 %all-to-all-start.2 = ((f32[8,8,128]{2,1,0:T(8,128)}), f32[8,8,128]{2,1,0:T(8,128)S(1)}, u32[]{:S(2)}, u32[]{:S(2)}) async-start(f32[8,8,128]{2,1,0:T(8,128)} %shard_map.163), calls=%async_computation.2 | async-start | bytes 65536 | tf_op jit(solution)/shard_map/all_to_all | solution.py:20
  161.3 4.8 %down.1 = bf16[192,4096]{1,0:T(8,128)(2,1)} custom-call(bf16[192,512]{1,0:T(8,128)(2,1)} %get-tuple-element.20.weighted, bf16[512,4096]{1,0:T(8,128)(2,1)} %all-gather.2.cloned.1.call-done.rows), custom_call_target="tpu_custom_call" | custom-call | flops 1000000000 | bytes 6000000 | tf_op jit(solution)/shard_map/down/pallas_call | solution.py:278
  166.1 3.2 %all-to-all-done.2.terms = f32[8,8,128]{2,1,0:T(8,128)S(1)} async-done(((f32[8,8,128]{2,1,0:T(8,128)}), f32[8,8,128]{2,1,0:T(8,128)S(1)}, u32[]{:S(2)}, u32[]{:S(2)}) %all-to-all-start.2) | async-done | bytes 32800 | tf_op jit(solution)/shard_map/all_to_all | solution.py:20
  169.9 1.4 shard_map.164
  (24 shorter events, 4.0 us)
Async XLA Ops:
  7.2 124.0 %all-gather.2.cloned.1.call-start = ((), (), s32[]{:S(2)}) async-start(), calls=%async_computation.5 | async-start | bytes 4718592 | tf_op jit(solution)/shard_map/all_gather | solution.py:221
  10.7 35.2 %copy-start.4 = (bf16[32,256]{1,0:T(8,128)(2,1)S(1)}, bf16[32,256]{1,0:T(8,128)(2,1)}, u32[]{:S(2)}) copy-start(bf16[32,256]{1,0:T(8,128)(2,1)} %get-tuple-element.25) | copy-start | bytes 49156
  45.9 5.6 %collective-permute-start = (bf16[32,256]{1,0:T(8,128)(2,1)S(1)}, bf16[32,256]{1,0:T(8,128)(2,1)S(1)}, u32[]{:S(2)}, u32[]{:S(2)}) collective-permute-start(bf16[32,256]{1,0:T(8,128)(2,1)S(1)} %copy-done.4), channel_id=1, source_target_pairs={{0,64},{64,0},{128,192},{192,128},{256,320},{320,256},{384,448},{4... | collective-permute-start | bytes 49160 | tf_op jit(solution)/shard_map/ppermute | solution.py:25
  51.5 7.0 %collective-permute-start.1 = (bf16[64,256]{1,0:T(8,128)(2,1)S(1)}, bf16[64,256]{1,0:T(8,128)(2,1)S(1)}, u32[]{:S(2)}, u32[]{:S(2)}) collective-permute-start(bf16[64,256]{1,0:T(8,128)(2,1)S(1)} %pad_maximum_fusion.4), channel_id=1, source_target_pairs={{0,128},{64,192},{128,0},{192,64},{256,384},{320,448},{384,256},{4... | collective-permute-start | bytes 98312 | tf_op jit(solution)/shard_map/ppermute | solution.py:25
  58.5 10.2 %collective-permute-start.2 = (bf16[128,256]{1,0:T(8,128)(2,1)S(1)}, bf16[128,256]{1,0:T(8,128)(2,1)S(1)}, u32[]{:S(2)}, u32[]{:S(2)}) collective-permute-start(bf16[128,256]{1,0:T(8,128)(2,1)S(1)} %pad_maximum_fusion.3), channel_id=1, source_target_pairs={{0,256},{64,320},{128,384},{192,448},{256,0},{320,64},{384,128},{4... | collective-permute-start | bytes 196616 | tf_op jit(solution)/shard_map/ppermute | solution.py:25
  68.7 7.7 %collective-permute-start.3 = (bf16[256,256]{1,0:T(8,128)(2,1)S(1)}, bf16[256,256]{1,0:T(8,128)(2,1)S(1)}, u32[]{:S(2)}, u32[]{:S(2)}) collective-permute-start(bf16[256,256]{1,0:T(8,128)(2,1)S(1)} %pad_maximum_fusion.2), channel_id=1, source_target_pairs={{0,16},{16,0},{32,48},{48,32},{1,17},{17,1},{33,49},{49,33},{2,18}... | collective-permute-start | bytes 393224 | tf_op jit(solution)/shard_map/ppermute | solution.py:25
  76.4 9.8 %collective-permute-start.4 = (bf16[512,256]{1,0:T(8,128)(2,1)S(1)}, bf16[512,256]{1,0:T(8,128)(2,1)S(1)}, u32[]{:S(2)}, u32[]{:S(2)}) collective-permute-start(bf16[512,256]{1,0:T(8,128)(2,1)S(1)} %pad_maximum_fusion.1), channel_id=1, source_target_pairs={{0,32},{16,48},{32,0},{48,16},{1,33},{17,49},{33,1},{49,17},{2,34}... | collective-permute-start | bytes 786440 | tf_op jit(solution)/shard_map/ppermute | solution.py:25
  86.2 3.8 %copy-start = (bf16[1024,256]{1,0:T(8,128)(2,1)}, bf16[1024,256]{1,0:T(8,128)(2,1)S(1)}, u32[]{:S(2)}) copy-start(bf16[1024,256]{1,0:T(8,128)(2,1)S(1)} %pad_maximum_fusion.mine_in) | copy-start | bytes 1572868
  86.2 3.8 %collective-permute-start.5 = (bf16[1024,256]{1,0:T(8,128)(2,1)S(1)}, bf16[1024,256]{1,0:T(8,128)(2,1)S(1)}, u32[]{:S(2)}, u32[]{:S(2)}) collective-permute-start(bf16[1024,256]{1,0:T(8,128)(2,1)S(1)} %pad_maximum_fusion.mine_in), channel_id=1, source_target_pairs={{0,8},{8,0},{1,9},{9,1},{2,10},{10,2},{3,11},{11,3},{4,12},{12,4},... | collective-permute-start | bytes 1572872 | tf_op jit(solution)/shard_map/ppermute | solution.py:25
  90.0 0.8 copy-start.5
  95.1 4.0 %collective-permute-start.6 = (bf16[1024,256]{1,0:T(8,128)(2,1)}, bf16[1024,256]{1,0:T(8,128)(2,1)S(1)}, u32[]{:S(2)}, u32[]{:S(2)}) collective-permute-start(bf16[1024,256]{1,0:T(8,128)(2,1)} %get-tuple-element.28), channel_id=1, source_target_pairs={{0,8},{8,0},{1,9},{9,1},{2,10},{10,2},{3,11},{11,3},{4,12},{12,4},... | collective-permute-start | bytes 1572872 | tf_op jit(solution)/shard_map/ppermute | solution.py:25
  123.4 16.2 %all-to-all-start.4 = ((bf16[8,32,256]{2,1,0:T(8,128)(2,1)}), bf16[8,32,256]{2,1,0:T(8,128)(2,1)S(1)}, u32[]{:S(2)}, u32[]{:S(2)}) async-start(bf16[8,32,256]{2,1,0:T(8,128)(2,1)} %broadcast_in_dim.18), calls=%async_computation.4 | async-start | bytes 262144 | tf_op jit(solution)/shard_map/all_to_all | solution.py:20
  139.6 6.0 %copy-start.1 = (bf16[8,32,256]{2,1,0:T(8,128)(2,1)}, bf16[8,32,256]{2,1,0:T(8,128)(2,1)S(1)}, u32[]{:S(2)}) copy-start(bf16[8,32,256]{2,1,0:T(8,128)(2,1)S(1)} %all-to-all-done.4.terms) | copy-start | bytes 393220
  139.6 13.9 %all-to-all-start.1 = ((f32[64,1,128]{2,1,0:T(1,128)}), f32[64,1,128]{2,1,0:T(1,128)S(1)}, u32[]{:S(2)}, u32[]{:S(2)}) async-start(f32[64,1,128]{2,1,0:T(1,128)} %get-tuple-element.24), calls=%async_computation.1 | async-start | bytes 65536 | tf_op jit(solution)/shard_map/all_to_all | solution.py:20
  153.5 0.6 copy-start.2
  156.2 13.1 %all-to-all-start.2 = ((f32[8,8,128]{2,1,0:T(8,128)}), f32[8,8,128]{2,1,0:T(8,128)S(1)}, u32[]{:S(2)}, u32[]{:S(2)}) async-start(f32[8,8,128]{2,1,0:T(8,128)} %shard_map.163), calls=%async_computation.2 | async-start | bytes 65536 | tf_op jit(solution)/shard_map/all_to_all | solution.py:20
  169.3 0.6 copy-start.3
Sparse Core Ops, SparseCore 0:
  46.0 53.6 all-gather.1

commit v5 on v4

v5 whole, which is shorter than its diff:
```python
import jax
import jax.numpy as jnp
from jax import lax
from jax.experimental import pallas as pl
from jax.experimental.pallas import tpu as pltpu
from jax.sharding import Mesh, PartitionSpec as P

H = 64
KVH = 4
HD = 128
GX = ("z", "x", "c")
ZX = ("z", "x")
NT = (((1,), (1,)), ((), ()))
TN = (((0,), (0,)), ((), ()))
F32 = jnp.float32
BF16 = jnp.bfloat16


def exchange(values, axes):
    return lax.all_to_all(values, axes, split_axis=0, concat_axis=0, tiled=True)


def to_partner(values):
    return lax.ppermute(values, "c", [(0, 1), (1, 0)])


def iota(shape, dim):
    return lax.broadcasted_iota(jnp.int32, shape, dim)


def call(body, outs, ins, flops, size):
    vmem = pl.BlockSpec(memory_space=pltpu.VMEM)
    return pl.pallas_call(
        body,
        out_shape=outs,
        in_specs=[pl.BlockSpec(memory_space=pltpu.SMEM)] + [vmem] * (len(ins) - 1),
        out_specs=jax.tree.map(lambda _: vmem, outs),
        cost_estimate=pl.CostEstimate(flops=flops, bytes_accessed=size, transcendentals=0),
    )(*ins)


def pack_body(where, kept, ids, gates, d_out, keys, values, message, kv, ranks):
    top, rows = ids.shape
    slots = message.shape[0]
    tok_dev, width = d_out.shape
    chips = kv.shape[0] // rows
    cap = 8
    head = pl.multiple_of(where[0] * HD, HD)
    slot = iota((slots, rows), 0)
    expert = slot // cap
    place = (slot % cap).astype(F32)
    named = jnp.zeros((slots, rows), F32)
    weight = jnp.zeros((slots, rows), F32)
    for j in range(top):
        hit = ids[j : j + 1, :] == expert
        named = jnp.where(hit, 1.0, named)
        weight = jnp.where(hit, gates[j : j + 1, :].astype(F32), weight)
    before = jnp.where(iota((rows, rows), 0) < iota((rows, rows), 1), 1.0, 0.0).astype(BF16)
    rank = jnp.dot(named.astype(BF16), before, preferred_element_type=F32)
    taken = jnp.where((named > 0.0) & (rank == place), 1.0, 0.0)
    pick = jnp.where(kept[...] % tok_dev == iota((tok_dev, rows), 0), 1.0, 0.0).astype(BF16)
    picked = lax.dot_general(pick, d_out[...], TN, preferred_element_type=F32).astype(BF16)
    message[:, :width] = jnp.dot(
        taken.astype(BF16), picked, preferred_element_type=F32
    ).astype(BF16)
    message[:, width:] = jnp.dot(
        (taken * weight).astype(BF16), jnp.ones((rows, HD), BF16), preferred_element_type=F32
    ).astype(BF16)
    for at, source in ((0, keys), (HD, values)):
        kv[:, at : at + HD] = jnp.broadcast_to(
            source[:, pl.ds(head, HD)][None], (chips, rows, HD)
        ).reshape(chips * rows, HD)
    for j in range(top):
        mine = jnp.where((ids[j : j + 1, :] == expert) & (taken > 0.0), place, 0.0)
        ranks[j : j + 1, :] = jnp.sum(mine, axis=0, keepdims=True).astype(jnp.int32)


def attention_body(where, query, grad, mine, other, d_query, keep, send):
    core, block = where[0], where[1]
    keep_dev = query.shape[0]
    heads = query.shape[1] // HD
    rows = keep_dev * heads
    half = mine.shape[0]
    scale = HD ** (-0.5)

    def stacked(ref):
        return jnp.concatenate([ref[:, g * HD : (g + 1) * HD] for g in range(heads)], axis=0)

    q = stacked(query)
    o = stacked(grad)
    query_pos = block * keep_dev + iota((rows, half), 0) % keep_dev
    column = iota((rows, half), 1)
    base = column // keep_dev * (2 * keep_dev) + column % keep_dev
    scores = []
    for ref, owner in ((mine, core), (other, 1 - core)):
        s = lax.dot_general(q, ref[:, :HD], NT, preferred_element_type=F32) * scale
        scores.append(jnp.where(base + owner * keep_dev <= query_pos, s, -1e30))
    top = jnp.maximum(*[jnp.max(s, axis=1, keepdims=True) for s in scores])
    expo = [jnp.exp(s - top) for s in scores]
    inv = 1.0 / sum(jnp.sum(e, axis=1, keepdims=True) for e in expo)
    probs = [e * inv for e in expo]
    dps = [
        lax.dot_general(o, ref[:, HD:], NT, preferred_element_type=F32) for ref in (mine, other)
    ]
    mean = sum(jnp.sum(p * dp, axis=1, keepdims=True) for p, dp in zip(probs, dps))
    dq = jnp.zeros((rows, HD), F32)
    for ref, p, dp, out in zip((other, mine), probs[::-1], dps[::-1], (send, keep)):
        ds = (p * (dp - mean)).astype(BF16)
        dk = lax.dot_general(ds, q, TN, preferred_element_type=F32) * scale
        dv = lax.dot_general(p.astype(BF16), o, TN, preferred_element_type=F32)
        out[:, :HD] = dk.astype(BF16)
        out[:, HD:] = dv.astype(BF16)
        dq = dq + jnp.dot(ds, ref[:, :HD], preferred_element_type=F32)
    dq = (dq * scale).astype(BF16)
    for g in range(heads):
        d_query[:, g * HD : (g + 1) * HD] = dq[g * keep_dev : (g + 1) * keep_dev]


def gates_body(where, ids, ranks, returned, owned, out):
    top, rows = ids.shape
    experts = returned.shape[0]
    keep_dev = owned.shape[0]
    table = returned[...].reshape(experts, returned.shape[2])
    result = jnp.zeros((top, HD), F32)
    for j in range(top):
        expert = jnp.concatenate([ids[j : j + 1, :]] * (HD // rows), axis=1)
        rank = jnp.concatenate([ranks[j : j + 1, :]] * (HD // rows), axis=1)
        pick = jnp.where(expert == iota((experts, HD), 0), 1.0, 0.0)
        found = lax.dot_general(
            table, pick, TN, preferred_element_type=F32, precision=lax.Precision.HIGHEST
        )
        hit = jnp.where(iota(found.shape, 0) == rank, found, 0.0)
        result = jnp.where(iota((top, HD), 0) == j, jnp.sum(hit, axis=0, keepdims=True), result)
    high = result.astype(BF16)
    low = (result - high.astype(F32)).astype(BF16)
    for i in range(out.shape[0]):
        out[i, :keep_dev] = owned[...]
        out[i, keep_dev:, :HD] = high
        out[i, keep_dev:, HD:] = low


def final_body(where, terms, d_key, d_value, d_gates):
    keep_dev = d_key.shape[0]
    per = terms.shape[0] // KVH
    for h in range(KVH):
        both = sum(terms[h * per + i, :keep_dev].astype(F32) for i in range(per))
        d_key[:, h * HD : (h + 1) * HD] = both[:, :HD]
        d_value[:, h * HD : (h + 1) * HD] = both[:, HD:]
    parts = jnp.sum(terms[:, keep_dev:, :].astype(F32), axis=0)
    d_gates[...] = (parts[:, :HD] + parts[:, HD:])[:, : d_gates.shape[1]]


def on_device(
    d_out, kept, expert_ids, gates, down_weight, gate_pre, up_pre, query, keys, values, d_attn
):
    core = lax.axis_index("c")
    chips = lax.axis_size(ZX)
    me = lax.axis_index("ta")
    n_experts = lax.axis_size(GX)
    n_ta = lax.axis_size("ta")
    keep_dev = kept.shape[0]
    width = d_out.shape[1]
    top = expert_ids.shape[1]
    slots = gate_pre.shape[2]
    cap = slots // n_experts
    struct = jax.ShapeDtypeStruct
    ids = expert_ids.T

    local_heads = query.shape[1] // HD
    first_kv = (me * local_heads // (H // KVH)).astype(jnp.int32)
    where = jnp.stack([first_kv, core.astype(jnp.int32), lax.axis_index(GX).astype(jnp.int32)])
    message, kv, ranks = call(
        pack_body,
        (
            struct((slots, width + HD), BF16),
            struct((chips * keep_dev, 2 * HD), BF16),
            struct((top, keep_dev), jnp.int32),
        ),
        (where, kept.reshape(1, keep_dev), ids, gates.T, d_out, keys, values),
        200_000_000,
        3_000_000,
    )
    arrived = exchange(message.reshape(n_experts, cap, -1), GX).reshape(slots, -1)
    slot_rows = lax.all_gather(arrived[:, :width], "ta", axis=1, tiled=True)
    slot_gate = arrived[:, width].astype(F32)

    kv_mine = exchange(kv.reshape(chips, keep_dev, 2 * HD), ZX).reshape(-1, 2 * HD)
    kv_other = to_partner(kv_mine)
    half = chips * keep_dev
    d_query, keep, send = call(
        attention_body,
        (
            struct((keep_dev, local_heads * HD), BF16),
            struct((half, 2 * HD), BF16),
            struct((half, 2 * HD), BF16),
        ),
        (where[1:], query, d_attn, kv_mine, kv_other),
        1_000_000_000,
        4_000_000,
    )
    chip_part = (keep.astype(F32) + to_partner(send).astype(F32)).astype(BF16)
    summed = exchange(chip_part.reshape(chips, keep_dev, 2 * HD), ZX)
    owned = jnp.sum(summed.astype(F32), axis=0).astype(BF16)

    z = lax.dot_general(down_weight[0], slot_rows, NT, preferred_element_type=F32)
    g = gate_pre[0].astype(F32)
    u = up_pre[0].astype(F32)
    sig = jax.nn.sigmoid(g)
    act = g * sig
    mixed = act * u
    dots = jnp.sum(mixed * z, axis=0)
    grad_hidden = z * slot_gate[None, :]
    d_up = (grad_hidden * act).astype(BF16)
    d_gate = (grad_hidden * u * sig * (1.0 + g * (1.0 - sig))).astype(BF16)
    weighted = (mixed * slot_gate[None, :]).astype(BF16)
    d_down = jnp.dot(weighted, slot_rows, preferred_element_type=F32).astype(BF16)
    returned = exchange(dots.reshape(n_experts, 1, cap), GX)
    merged = call(
        gates_body,
        struct((n_ta, keep_dev + top, 2 * HD), BF16),
        (where, ids, ranks, returned, owned),
        1_000_000,
        200_000,
    )
    d_key, d_value, d_gates = call(
        final_body,
        (
            struct((keep_dev, KVH * HD), F32),
            struct((keep_dev, KVH * HD), F32),
            struct((top, keep_dev), F32),
        ),
        (where, exchange(merged, "ta")),
        1_000_000,
        300_000,
    )
    return (d_down[None], d_gate[None], d_up[None], d_gates.T, d_query, d_key, d_value)


def solution(mesh):
    shape = dict(mesh.shape)
    fine = Mesh(mesh.devices.reshape(8, shape["gx"] // 16, 2, shape["ta"]), GX + ("ta",))
    in_specs = (
        P(GX, "ta"),
        P(GX),
        P(GX, None),
        P(GX, None),
        P(GX, "ta", None),
        P(GX, "ta", None),
        P(GX, "ta", None),
        P(GX, "ta"),
        P(GX, None),
        P(GX, None),
        P(GX, "ta"),
    )
    out_specs = (
        P(GX, "ta", None),
        P(GX, "ta", None),
        P(GX, "ta", None),
        P(GX, None),
        P(GX, "ta"),
        P(GX, None),
        P(GX, None),
    )
    return jax.shard_map(
        on_device, mesh=fine, in_specs=in_specs, out_specs=out_specs, check_vma=False
    )
```

time: 180 us -> 151 us (0.84)
  waiting for transfers between devices: 41.2 us -> 27.5 us
  Pallas kernels: 23.2 us -> 10.6 us
  starting transfers between devices: 36.2 us -> 24.3 us
  matrix products: 0 us -> 8.98 us
    ppermute x7 -> x2, waiting for transfers between devices: 29.5 us -> 3.23 us  [to_partner(): return lax.ppermute(values, 'c', [(0, 1), (1, 0)])]
    ppermute x7 -> x2, starting transfers between devices: 18 us -> 3.96 us  [to_partner(): return lax.ppermute(values, 'c', [(0, 1), (1, 0)])]
    pallas_call x2 -> x0, Pallas kernels: 11.1 us -> none  [the longest x1 6.29 us: on_device(): pl.pallas_call(expert_body, grid=(steps,), in_specs=[pl.BlockSpec((hidden...]
    all_gather x1, waiting for transfers between devices: 0.01 us -> 11 us  [on_device(): slot_rows = lax.all_gather(arrived[:, :width], 'ta', axis=1, tiled=True)]
    dot_general x0 -> x2, matrix products: none -> 8.98 us  [the longest x1 4.6 us: on_device(): lax.dot_general(down_weight[0], slot_rows, NT, preferred_element_type=F32)]
    all_to_all x3, starting transfers between devices: 18.2 us -> 20.3 us  [exchange(): return lax.all_to_all(values, axes, split_axis=0, concat_axis=0, tiled=True)]
    pallas_call x5 -> x4, Pallas kernels: 12 us -> 10.6 us  [call(): pl.pallas_call(body, out_shape=outs, in_specs=[pl.BlockSpec(memory_space=...]
  transfers between devices with their start and end apart: 11 -> 6, of which waited for: 10 -> 6; matrix products, arithmetic and copies ran while one was open for 2% -> 9% of each run, Pallas kernels for 10% -> 3%
where the time goes in v5:
time: 151 us; the launch traced here: 150 us
  blocking collectives  56.4 us (37%)
  waiting for transfers between devices  27.5 us (18%)
  starting transfers between devices  24.3 us (16%)
  between operations  14.1 us (9%)
  Pallas kernels  10.6 us (7%)
  matrix products  8.98 us (6%)
  other arithmetic  4.02 us (3%)
  local copies, waits for them, and re-layouts  3.68 us (2%)
    all_to_all x2, blocking collectives, exchange(): return lax.all_to_all(values, axes, split_axis=0, concat_axis=0, tiled=True)  56.4 us
    all_to_all x3, starting transfers between devices, exchange(): return lax.all_to_all(values, axes, split_axis=0, concat_axis=0, tiled=True)  20.3 us
    all_to_all x3, waiting for transfers between devices, exchange(): return lax.all_to_all(values, axes, split_axis=0, concat_axis=0, tiled=True)  13.2 us
    all_gather x1, waiting for transfers between devices, on_device(): slot_rows = lax.all_gather(arrived[:, :width], 'ta', axis=1, tiled=True)  11 us
    pallas_call x4, Pallas kernels, call(): pl.pallas_call(body, out_shape=outs, in_specs=[pl.BlockSpec(memory_space=...  10.6 us
    dot_general x1, matrix products, on_device(): lax.dot_general(down_weight[0], slot_rows, NT, preferred_element_type=F32)  4.6 us
    dot_general x1, matrix products, on_device(): jnp.dot(weighted, slot_rows, preferred_element_type=F32).astype(BF16)  4.37 us
    ppermute x2, starting transfers between devices, to_partner(): return lax.ppermute(values, 'c', [(0, 1), (1, 0)])  3.96 us
  transfers between devices with their start and end apart: 6, of which 6 were waited for; matrix products, arithmetic and copies ran while one was open for 9% of the time, Pallas kernels for 3%

profile of v5, /device:TPU:6, one launch (start us, length us, event | category | flops | bytes accessed | tf_op | source)
XLA Modules:
  0.0 149.6 jit_solution(11235445653452112840)
XLA Ops:
  7.2 0.0 copy-start
  7.2 0.0 all-gather.2.cloned.1.call-start
  7.2 0.7 pad_add_fusion.where
  7.9 3.0 %shard_map.162 = (bf16[512,640]{1,0:T(8,128)(2,1)}, bf16[1024,256]{1,0:T(8,128)(2,1)}, s32[8,32]{1,0:T(8,128)}) custom-call(s32[3]{0:T(128)} %pad_add_fusion.where, s32[1,32]{1,0:T(1,128)} %bitcast.65, s32[8,32]{1,0:T(8,128)} %bitcast.61, bf16[8,32]{1,0:T(8,128)(2,1)} %bitcast.64, bf16[256,512]{1,0:T(8,128)(2,1)} %d_out.1, bf16[32,512]{1,0:T(8,128)(2,1)} %keys.1, ...), custom_call_target="tpu_custom_call" | custom-call | flops 200000000 | bytes 3000000 | tf_op jit(solution)/shard_map/pallas_call | solution.py:33
  10.9 34.2 %all_to_all.25 = bf16[64,8,640]{2,1,0:T(8,128)(2,1)S(1)} all-to-all(bf16[64,8,640]{2,1,0:T(8,128)(2,1)} %bitcast.57), channel_id=1, replica_groups=mesh['z'=8,'x'=4,'c'=2,'ta'=8] {'z','x','c'}, dimensions={0} | all-to-all | bytes 1310720 | tf_op jit(solution)/shard_map/all_to_all | solution.py:20
  45.0 0.8 slice.11
  45.9 0.0 all-gather.2.cloned.1.call-update
  45.9 22.2 %all_to_all.26 = bf16[32,32,256]{2,1,0:T(8,128)(2,1)S(1)} all-to-all(bf16[32,32,256]{2,1,0:T(8,128)(2,1)} %bitcast.60), channel_id=1, replica_groups=mesh['z'=8,'x'=4,'c'=2,'ta'=8] {'z','x'}, dimensions={0} | all-to-all | bytes 1048576 | tf_op jit(solution)/shard_map/all_to_all | solution.py:20
  68.1 1.9 %collective-permute-start = (bf16[1024,256]{1,0:T(8,128)(2,1)S(1)}, bf16[1024,256]{1,0:T(8,128)(2,1)S(1)}, u32[]{:S(2)}, u32[]{:S(2)}) collective-permute-start(bf16[1024,256]{1,0:T(8,128)(2,1)S(1)} %bitcast.58), channel_id=1, source_target_pairs={{0,8},{8,0},{1,9},{9,1},{2,10},{10,2},{3,11},{11,3},{4,12},{12,4},... | collective-permute-start | bytes 1572872 | tf_op jit(solution)/shard_map/ppermute | solution.py:24
  70.0 0.6 pad_add_fusion.1.where
  70.6 1.3 collective-permute-done.other
  71.9 0.8 copy-done.4
  72.8 4.2 %shard_map.163 = (bf16[32,1024]{1,0:T(8,128)(2,1)}, bf16[1024,256]{1,0:T(8,128)(2,1)}, bf16[1024,256]{1,0:T(8,128)(2,1)}) custom-call(s32[2]{0:T(128)} %pad_add_fusion.1.where, bf16[32,1024]{1,0:T(8,128)(2,1)} %query.1, bf16[32,1024]{1,0:T(8,128)(2,1)} %grad.1, bf16[1024,256]{1,0:T(8,128)(2,1)} %bitcast.59, bf16[1024,256]{1,0:T(8,128)(2,1)} %copy-done.4), custom_call_target="tpu_custom_call" | custom-call | flops 1000000000 | bytes 4000000 | tf_op jit(solution)/shard_map/pallas_call | solution.py:33
  77.0 2.1 %collective-permute-start.1 = (bf16[1024,256]{1,0:T(8,128)(2,1)}, bf16[1024,256]{1,0:T(8,128)(2,1)S(1)}, u32[]{:S(2)}, u32[]{:S(2)}) collective-permute-start(bf16[1024,256]{1,0:T(8,128)(2,1)} %get-tuple-element.20), channel_id=1, source_target_pairs={{0,8},{8,0},{1,9},{9,1},{2,10},{10,2},{3,11},{11,3},{4,12},{12,4},... | collective-permute-start | bytes 1572872 | tf_op jit(solution)/shard_map/ppermute | solution.py:24
  79.0 1.9 %collective-permute-done.1 = bf16[1024,256]{1,0:T(8,128)(2,1)S(1)} collective-permute-done((bf16[1024,256]{1,0:T(8,128)(2,1)}, bf16[1024,256]{1,0:T(8,128)(2,1)S(1)}, u32[]{:S(2)}, u32[]{:S(2)}) %collective-permute-start.1) | collective-permute-done | bytes 524320 | tf_op jit(solution)/shard_map/ppermute | solution.py:24
  81.0 2.0 %add_convert_fusion = bf16[1024,256]{1,0:T(8,128)(2,1)} fusion(bf16[1024,256]{1,0:T(8,128)(2,1)S(1)} %collective-permute-done.1, bf16[1024,256]{1,0:T(8,128)(2,1)} %get-tuple-element.19), kind=kLoop, calls=%fused_computation.5 | loop fusion | flops 1048576 | bytes 1572864 | tf_op jit(solution)/shard_map/convert_element_type | solution.py:201
  82.9 5.6 %all-to-all-start.3 = ((bf16[32,32,256]{2,1,0:T(8,128)(2,1)}), bf16[32,32,256]{2,1,0:T(8,128)(2,1)S(1)}, u32[]{:S(2)}, u32[]{:S(2)}) async-start(bf16[32,32,256]{2,1,0:T(8,128)(2,1)} %bitcast.20), calls=%async_computation.3 | async-start | bytes 1048576 | tf_op jit(solution)/shard_map/all_to_all | solution.py:20
  88.5 0.1 convert_reduce_fusion
  88.7 11.0 %all-gather.2.cloned.1.call-done = bf16[512,4096]{1,0:T(8,128)(2,1)} async-done(((bf16[512,512]{1,0:T(8,128)(2,1)}), bf16[512,4096]{1,0:T(8,128)(2,1)}) %all-gather.2.cloned.1.call-update) | async-done | bytes 4194320 | tf_op jit(solution)/shard_map/all_gather | solution.py:184
  99.7 4.6 %multiply_reduce_fusion = (f32[512]{0:T(512)S(1)}, bf16[1,192,512]{2,1,0:T(8,128)(2,1)}, bf16[1,192,512]{2,1,0:T(8,128)(2,1)}) fusion(bf16[1,192,512]{2,1,0:T(8,128)(2,1)S(1)} %copy-done.5, bf16[1,192,512]{2,1,0:T(8,128)(2,1)} %param.16, f32[512]{0:T(512)S(1)} %convert_reduce_fusion, bf16[512,4096]{1,0:T(8,128)(2,1)} %all-gather.2.cloned.1.call-done, ...), kind=kOutput, calls=%fused_computation.18 | convolution fusion | flops 807173632 | bytes 6557696 | tf_op jit(solution)/shard_map/dot_general | solution.py:205
  104.3 0.7 reshape.49
  105.0 0.7 all-to-all-done.3
  105.7 10.2 %all-to-all-start.1 = ((f32[64,1,8]{2,1,0:T(1,128)}), f32[64,1,8]{2,1,0:T(1,128)S(1)}, u32[]{:S(2)}, u32[]{:S(2)}) async-start(f32[64,1,8]{2,1,0:T(1,128)} %bitcast.17), calls=%async_computation.1 | async-start | bytes 65536 | tf_op jit(solution)/shard_map/all_to_all | solution.py:20
  115.9 0.7 reduce_sum.22.owned
  116.6 7.1 %all-to-all-done.1.returned = f32[64,1,8]{2,1,0:T(1,128)S(1)} async-done(((f32[64,1,8]{2,1,0:T(1,128)}), f32[64,1,8]{2,1,0:T(1,128)S(1)}, u32[]{:S(2)}, u32[]{:S(2)}) %all-to-all-start.1) | async-done | bytes 2080 | tf_op jit(solution)/shard_map/all_to_all | solution.py:20
  123.7 0.6 copy-done.3
  124.4 1.9 %shard_map.164 = bf16[8,40,256]{2,1,0:T(8,128)(2,1)} custom-call(s32[3]{0:T(128)} %pad_add_fusion.where, s32[8,32]{1,0:T(8,128)} %bitcast.62, s32[8,32]{1,0:T(8,128)} %get-tuple-element.17.ranks, f32[64,1,8]{2,1,0:T(1,128)} %copy-done.3, bf16[32,256]{1,0:T(8,128)(2,1)} %reduce_sum.22.owned), custom_call_target="tpu_custom_call" | custom-call | flops 1000000 | bytes 200000 | tf_op jit(solution)/shard_map/pallas_call | solution.py:33
  126.2 4.5 %all-to-all-start.4 = ((bf16[8,40,256]{2,1,0:T(8,128)(2,1)}), bf16[8,40,256]{2,1,0:T(8,128)(2,1)S(1)}, u32[]{:S(2)}, u32[]{:S(2)}) async-start(bf16[8,40,256]{2,1,0:T(8,128)(2,1)} %shard_map.164), calls=%async_computation.4 | async-start | bytes 327680 | tf_op jit(solution)/shard_map/all_to_all | solution.py:20
  130.7 4.4 %fusion = bf16[1,192,4096]{2,1,0:T(8,128)(2,1)} fusion(bf16[512,4096]{1,0:T(8,128)(2,1)} %all-gather.2.cloned.1.call-done, bf16[1,192,512]{2,1,0:T(8,128)(2,1)S(1)} %copy-done.5, f32[512]{0:T(512)S(1)} %convert_reduce_fusion, bf16[1,192,512]{2,1,0:T(8,128)(2,1)S(1)} %copy-done.6), kind=kOutput, calls=%fused_computation.1 | convolution fusion | flops 806977536 | bytes 6162432 | tf_op jit(solution)/shard_map/dot_general | solution.py:216
  135.1 5.4 %all-to-all-done.4.terms = bf16[8,40,256]{2,1,0:T(8,128)(2,1)S(1)} async-done(((bf16[8,40,256]{2,1,0:T(8,128)(2,1)}), bf16[8,40,256]{2,1,0:T(8,128)(2,1)S(1)}, u32[]{:S(2)}, u32[]{:S(2)}) %all-to-all-start.4) | async-done | bytes 163872 | tf_op jit(solution)/shard_map/all_to_all | solution.py:20
  140.5 0.7 copy-done.1
  141.2 1.6 %shard_map.165 = (f32[32,512]{1,0:T(8,128)}, f32[32,512]{1,0:T(8,128)}, f32[8,32]{1,0:T(8,128)}) custom-call(s32[3]{0:T(128)} %pad_add_fusion.where, bf16[8,40,256]{2,1,0:T(8,128)(2,1)} %copy-done.1), custom_call_target="tpu_custom_call" | custom-call | flops 1000000 | bytes 300000 | tf_op jit(solution)/shard_map/pallas_call | solution.py:33
  (10 shorter events, 0.0 us)
Async XLA Ops:
  7.2 92.5 %copy-start = (bf16[1,192,4096]{2,1,0:T(8,128)(2,1)S(1)}, bf16[1,192,4096]{2,1,0:T(8,128)(2,1)}, u32[]{:S(2)}) copy-start(bf16[1,192,4096]{2,1,0:T(8,128)(2,1)} %param.15) | copy-start | bytes 4718596
  7.2 92.5 %all-gather.2.cloned.1.call-start = ((), (), s32[]{:S(2)}) async-start(), calls=%async_computation.5 | async-start | bytes 4718592 | tf_op jit(solution)/shard_map/all_gather | solution.py:184
  45.9 53.8 %copy-start.5 = (bf16[1,192,512]{2,1,0:T(8,128)(2,1)S(1)}, bf16[1,192,512]{2,1,0:T(8,128)(2,1)}, u32[]{:S(2)}) copy-start(bf16[1,192,512]{2,1,0:T(8,128)(2,1)} %param.17) | copy-start | bytes 589828
  68.1 3.8 %copy-start.2 = (bf16[32,32,256]{2,1,0:T(8,128)(2,1)}, bf16[32,32,256]{2,1,0:T(8,128)(2,1)S(1)}, u32[]{:S(2)}) copy-start(bf16[32,32,256]{2,1,0:T(8,128)(2,1)S(1)} %all_to_all.26) | copy-start | bytes 1572868
  68.1 3.8 %collective-permute-start = (bf16[1024,256]{1,0:T(8,128)(2,1)S(1)}, bf16[1024,256]{1,0:T(8,128)(2,1)S(1)}, u32[]{:S(2)}, u32[]{:S(2)}) collective-permute-start(bf16[1024,256]{1,0:T(8,128)(2,1)S(1)} %bitcast.58), channel_id=1, source_target_pairs={{0,8},{8,0},{1,9},{9,1},{2,10},{10,2},{3,11},{11,3},{4,12},{12,4},... | collective-permute-start | bytes 1572872 | tf_op jit(solution)/shard_map/ppermute | solution.py:24
  71.9 0.8 copy-start.4
  77.0 4.0 %collective-permute-start.1 = (bf16[1024,256]{1,0:T(8,128)(2,1)}, bf16[1024,256]{1,0:T(8,128)(2,1)S(1)}, u32[]{:S(2)}, u32[]{:S(2)}) collective-permute-start(bf16[1024,256]{1,0:T(8,128)(2,1)} %get-tuple-element.20), channel_id=1, source_target_pairs={{0,8},{8,0},{1,9},{9,1},{2,10},{10,2},{3,11},{11,3},{4,12},{12,4},... | collective-permute-start | bytes 1572872 | tf_op jit(solution)/shard_map/ppermute | solution.py:24
  82.9 22.7 %all-to-all-start.3 = ((bf16[32,32,256]{2,1,0:T(8,128)(2,1)}), bf16[32,32,256]{2,1,0:T(8,128)(2,1)S(1)}, u32[]{:S(2)}, u32[]{:S(2)}) async-start(bf16[32,32,256]{2,1,0:T(8,128)(2,1)} %bitcast.20), calls=%async_computation.3 | async-start | bytes 1048576 | tf_op jit(solution)/shard_map/all_to_all | solution.py:20
  88.6 42.1 %copy-start.6 = (bf16[1,192,512]{2,1,0:T(8,128)(2,1)S(1)}, bf16[1,192,512]{2,1,0:T(8,128)(2,1)}, u32[]{:S(2)}) copy-start(bf16[1,192,512]{2,1,0:T(8,128)(2,1)} %param.16) | copy-start | bytes 589828
  105.7 18.1 %all-to-all-start.1 = ((f32[64,1,8]{2,1,0:T(1,128)}), f32[64,1,8]{2,1,0:T(1,128)S(1)}, u32[]{:S(2)}, u32[]{:S(2)}) async-start(f32[64,1,8]{2,1,0:T(1,128)} %bitcast.17), calls=%async_computation.1 | async-start | bytes 65536 | tf_op jit(solution)/shard_map/all_to_all | solution.py:20
  123.7 0.6 copy-start.3
  126.2 14.3 %all-to-all-start.4 = ((bf16[8,40,256]{2,1,0:T(8,128)(2,1)}), bf16[8,40,256]{2,1,0:T(8,128)(2,1)S(1)}, u32[]{:S(2)}, u32[]{:S(2)}) async-start(bf16[8,40,256]{2,1,0:T(8,128)(2,1)} %shard_map.164), calls=%async_computation.4 | async-start | bytes 327680 | tf_op jit(solution)/shard_map/all_to_all | solution.py:20
  140.5 0.7 copy-start.1
Sparse Core Ops, SparseCore 0:
  46.0 53.6 all-gather.1

commit v6 on v5

--- a/solution.py
+++ b/solution.py
@@ -39,44 +39,52 @@
     )(*ins)
 
 
-def pack_body(where, kept, ids, gates, d_out, keys, values, message, kv, ranks):
+def named_slots(ids, slots):
     top, rows = ids.shape
-    slots = message.shape[0]
-    tok_dev, width = d_out.shape
-    chips = kv.shape[0] // rows
-    cap = 8
-    head = pl.multiple_of(where[0] * HD, HD)
     slot = iota((slots, rows), 0)
-    expert = slot // cap
-    place = (slot % cap).astype(F32)
+    expert = slot // 8
+    place = (slot % 8).astype(F32)
     named = jnp.zeros((slots, rows), F32)
-    weight = jnp.zeros((slots, rows), F32)
     for j in range(top):
-        hit = ids[j : j + 1, :] == expert
-        named = jnp.where(hit, 1.0, named)
-        weight = jnp.where(hit, gates[j : j + 1, :].astype(F32), weight)
+        named = jnp.where(ids[j : j + 1, :] == expert, 1.0, named)
     before = jnp.where(iota((rows, rows), 0) < iota((rows, rows), 1), 1.0, 0.0).astype(BF16)
     rank = jnp.dot(named.astype(BF16), before, preferred_element_type=F32)
-    taken = jnp.where((named > 0.0) & (rank == place), 1.0, 0.0)
+    return jnp.where((named > 0.0) & (rank == place), 1.0, 0.0), expert, place
+
+
+def pack_body(where, kept, ids, d_out, message):
+    rows = ids.shape[1]
+    tok_dev = d_out.shape[0]
+    taken, _, _ = named_slots(ids, message.shape[0])
     pick = jnp.where(kept[...] % tok_dev == iota((tok_dev, rows), 0), 1.0, 0.0).astype(BF16)
     picked = lax.dot_general(pick, d_out[...], TN, preferred_element_type=F32).astype(BF16)
-    message[:, :width] = jnp.dot(
-        taken.astype(BF16), picked, preferred_element_type=F32
-    ).astype(BF16)
-    message[:, width:] = jnp.dot(
-        (taken * weight).astype(BF16), jnp.ones((rows, HD), BF16), preferred_element_type=F32
-    ).astype(BF16)
+    message[...] = jnp.dot(taken.astype(BF16), picked, preferred_element_type=F32).astype(BF16)
+
+
+def tables_body(where, ids, gates, keys, values, kv, ranks, table):
+    top, rows = ids.shape
+    experts = table.shape[0]
+    chips = kv.shape[0] // rows
+    head = pl.multiple_of(where[0] * HD, HD)
     for at, source in ((0, keys), (HD, values)):
         kv[:, at : at + HD] = jnp.broadcast_to(
             source[:, pl.ds(head, HD)][None], (chips, rows, HD)
         ).reshape(chips * rows, HD)
+    taken, expert, place = named_slots(ids, experts * 8)
+    weight = jnp.zeros(taken.shape, F32)
     for j in range(top):
-        mine = jnp.where((ids[j : j + 1, :] == expert) & (taken > 0.0), place, 0.0)
-        ranks[j : j + 1, :] = jnp.sum(mine, axis=0, keepdims=True).astype(jnp.int32)
+        hit = (ids[j : j + 1, :] == expert) & (taken > 0.0)
+        weight = jnp.where(hit, gates[j : j + 1, :].astype(F32), weight)
+        ranks[j : j + 1, :] = jnp.sum(
+            jnp.where(hit, place, 0.0), axis=0, keepdims=True
+        ).astype(jnp.int32)
+    column = jnp.dot(weight.astype(BF16), jnp.ones((rows, HD), BF16), preferred_element_type=F32)
+    own = jnp.where(iota(column.shape, 0) % 8 == iota(column.shape, 1), column, 0.0)
+    table[...] = jnp.sum(own.reshape(experts, 8, HD), axis=1)
 
 
 def attention_body(where, query, grad, mine, other, d_query, keep, send):
-    core, block = where[0], where[1]
+    core, block = where[1], where[2]
     keep_dev = query.shape[0]
     heads = query.shape[1] // HD
     rows = keep_dev * heads
@@ -120,7 +128,7 @@
     top, rows = ids.shape
     experts = returned.shape[0]
     keep_dev = owned.shape[0]
-    table = returned[...].reshape(experts, returned.shape[2])
+    table = returned[...].reshape(experts, returned.shape[2])[:, :8]
     result = jnp.zeros((top, HD), F32)
     for j in range(top):
         expert = jnp.concatenate([ids[j : j + 1, :]] * (HD // rows), axis=1)
@@ -169,20 +177,26 @@
     local_heads = query.shape[1] // HD
     first_kv = (me * local_heads // (H // KVH)).astype(jnp.int32)
     where = jnp.stack([first_kv, core.astype(jnp.int32), lax.axis_index(GX).astype(jnp.int32)])
-    message, kv, ranks = call(
+    message = call(
         pack_body,
+        struct((slots, width), BF16),
+        (where, kept.reshape(1, keep_dev), ids, d_out),
+        200_000_000,
+        2_000_000,
+    )
+    arrived = exchange(message.reshape(n_experts, cap, width), GX)
+    kv, ranks, table = call(
+        tables_body,
         (
-            struct((slots, width + HD), BF16),
             struct((chips * keep_dev, 2 * HD), BF16),
             struct((top, keep_dev), jnp.int32),
+            struct((n_experts, HD), F32),
         ),
-        (where, kept.reshape(1, keep_dev), ids, gates.T, d_out, keys, values),
-        200_000_000,
-        3_000_000,
-    )
-    arrived = exchange(message.reshape(n_experts, cap, -1), GX).reshape(slots, -1)
-    slot_rows = lax.all_gather(arrived[:, :width], "ta", axis=1, tiled=True)
-    slot_gate = arrived[:, width].astype(F32)
+        (where, ids, gates.T, keys, values),
+        10_000_000,
+        1_000_000,
+    )
+    slot_rows = lax.all_gather(arrived.reshape(slots, width), "ta", axis=1, tiled=True)
 
     kv_mine = exchange(kv.reshape(chips, keep_dev, 2 * HD), ZX).reshape(-1, 2 * HD)
     kv_other = to_partner(kv_mine)
@@ -194,7 +208,7 @@
             struct((half, 2 * HD), BF16),
             struct((half, 2 * HD), BF16),
         ),
-        (where[1:], query, d_attn, kv_mine, kv_other),
+        (where, query, d_attn, kv_mine, kv_other),
         1_000_000_000,
         4_000_000,
     )
@@ -209,12 +223,16 @@
     act = g * sig
     mixed = act * u
     dots = jnp.sum(mixed * z, axis=0)
-    grad_hidden = z * slot_gate[None, :]
+    both = jnp.concatenate(
+        [dots.reshape(n_experts, 1, cap), table[:, :cap].reshape(n_experts, 1, cap)], axis=2
+    )
+    returned = exchange(both, GX)
+    slot_weight = returned[:, 0, cap:].reshape(1, slots)
+    grad_hidden = z * slot_weight
     d_up = (grad_hidden * act).astype(BF16)
     d_gate = (grad_hidden * u * sig * (1.0 + g * (1.0 - sig))).astype(BF16)
-    weighted = (mixed * slot_gate[None, :]).astype(BF16)
+    weighted = (mixed * slot_weight).astype(BF16)
     d_down = jnp.dot(weighted, slot_rows, preferred_element_type=F32).astype(BF16)
-    returned = exchange(dots.reshape(n_experts, 1, cap), GX)
     merged = call(
         gates_body,
         struct((n_ta, keep_dev + top, 2 * HD), BF16),

time: 151 us -> 148 us (0.980)
  blocking collectives: 56.4 us -> 53.6 us
  Pallas kernels: 10.6 us -> 12.5 us
  starting transfers between devices: 24.3 us -> 22.6 us
    all_to_all x2, blocking collectives: 56.4 us -> 53.6 us  [exchange(): return lax.all_to_all(values, axes, split_axis=0, concat_axis=0, tiled=True)]
    all_gather x1, waiting for transfers between devices: 11 us -> 8.72 us  [on_device(): lax.all_gather(arrived.reshape(slots, width), 'ta', axis=1, tiled=True)]
    pallas_call x4 -> x5, Pallas kernels: 10.6 us -> 12.5 us  [call(): pl.pallas_call(body, out_shape=outs, in_specs=[pl.BlockSpec(memory_space=...]
    all_to_all x3, starting transfers between devices: 20.3 us -> 18.6 us  [exchange(): return lax.all_to_all(values, axes, split_axis=0, concat_axis=0, tiled=True)]
  transfers between devices with their start and end apart: 6 -> 6, of which waited for: 6 -> 6; matrix products, arithmetic and copies ran while one was open for 9% -> 9% of each run, Pallas kernels for 3% -> 5%
where the time goes in v6:
time: 148 us; the launch traced here: 146 us
  blocking collectives  53.6 us (36%)
  waiting for transfers between devices  26.9 us (18%)
  starting transfers between devices  22.6 us (15%)
  between operations  14.1 us (10%)
  Pallas kernels  12.5 us (8%)
  matrix products  8.12 us (5%)
  other arithmetic  4.98 us (3%)
  local copies, waits for them, and re-layouts  3.2 us (2%)
    all_to_all x2, blocking collectives, exchange(): return lax.all_to_all(values, axes, split_axis=0, concat_axis=0, tiled=True)  53.6 us
    all_to_all x3, starting transfers between devices, exchange(): return lax.all_to_all(values, axes, split_axis=0, concat_axis=0, tiled=True)  18.6 us
    all_to_all x3, waiting for transfers between devices, exchange(): return lax.all_to_all(values, axes, split_axis=0, concat_axis=0, tiled=True)  14.4 us
    pallas_call x5, Pallas kernels, call(): pl.pallas_call(body, out_shape=outs, in_specs=[pl.BlockSpec(memory_space=...  12.5 us
    all_gather x1, waiting for transfers between devices, on_device(): lax.all_gather(arrived.reshape(slots, width), 'ta', axis=1, tiled=True)  8.72 us
    dot_general x1, matrix products, on_device(): jnp.dot(weighted, slot_rows, preferred_element_type=F32).astype(BF16)  4.37 us
    ppermute x2, starting transfers between devices, to_partner(): return lax.ppermute(values, 'c', [(0, 1), (1, 0)])  3.96 us
    ppermute x2, waiting for transfers between devices, to_partner(): return lax.ppermute(values, 'c', [(0, 1), (1, 0)])  3.82 us
  transfers between devices with their start and end apart: 6, of which 6 were waited for; matrix products, arithmetic and copies ran while one was open for 9% of the time, Pallas kernels for 5%

profile of v6, /device:TPU:6, one launch (start us, length us, event | category | flops | bytes accessed | tf_op | source)
XLA Modules:
  0.0 146.1 jit_solution(16519137116768250902)
XLA Ops:
  7.2 0.0 all-gather.2.cloned.1.call-start
  7.2 0.6 pad_add_fusion.where
  7.9 2.3 %shard_map.162 = bf16[512,512]{1,0:T(8,128)(2,1)} custom-call(s32[3]{0:T(128)} %pad_add_fusion.where, s32[1,32]{1,0:T(1,128)} %bitcast.66, s32[8,32]{1,0:T(8,128)} %bitcast.61, bf16[256,512]{1,0:T(8,128)(2,1)} %d_out.1), custom_call_target="tpu_custom_call" | custom-call | flops 200000000 | bytes 2000000 | tf_op jit(solution)/shard_map/pallas_call | solution.py:33
  10.1 31.5 %all_to_all.25 = bf16[64,8,512]{2,1,0:T(8,128)(2,1)} all-to-all(bf16[64,8,512]{2,1,0:T(8,128)(2,1)} %bitcast.56), channel_id=1, replica_groups=mesh['z'=8,'x'=4,'c'=2,'ta'=8] {'z','x','c'}, dimensions={0} | all-to-all | bytes 1048576 | tf_op jit(solution)/shard_map/all_to_all | solution.py:20
  41.6 2.5 %shard_map.163 = (bf16[1024,256]{1,0:T(8,128)(2,1)}, s32[8,32]{1,0:T(8,128)}, f32[64,128]{1,0:T(8,128)}) custom-call(s32[3]{0:T(128)} %pad_add_fusion.where, s32[8,32]{1,0:T(8,128)} %bitcast.62, bf16[8,32]{1,0:T(8,128)(2,1)} %bitcast.65, bf16[32,512]{1,0:T(8,128)(2,1)} %keys.1, bf16[32,512]{1,0:T(8,128)(2,1)} %values.1), custom_call_target="tpu_custom_call" | custom-call | flops 10000000 | bytes 1000000 | tf_op jit(solution)/shard_map/pallas_call | solution.py:33
  44.2 22.2 %all_to_all.26 = bf16[32,32,256]{2,1,0:T(8,128)(2,1)S(1)} all-to-all(bf16[32,32,256]{2,1,0:T(8,128)(2,1)} %bitcast.59), channel_id=1, replica_groups=mesh['z'=8,'x'=4,'c'=2,'ta'=8] {'z','x'}, dimensions={0} | all-to-all | bytes 1048576 | tf_op jit(solution)/shard_map/all_to_all | solution.py:20
  66.3 1.9 %collective-permute-start = (bf16[1024,256]{1,0:T(8,128)(2,1)S(1)}, bf16[1024,256]{1,0:T(8,128)(2,1)S(1)}, u32[]{:S(2)}, u32[]{:S(2)}) collective-permute-start(bf16[1024,256]{1,0:T(8,128)(2,1)S(1)} %bitcast.57), channel_id=1, source_target_pairs={{0,8},{8,0},{1,9},{9,1},{2,10},{10,2},{3,11},{11,3},{4,12},{12,4},... | collective-permute-start | bytes 1572872 | tf_op jit(solution)/shard_map/ppermute | solution.py:24
  68.2 1.9 %collective-permute-done.other = bf16[1024,256]{1,0:T(8,128)(2,1)S(1)} collective-permute-done((bf16[1024,256]{1,0:T(8,128)(2,1)S(1)}, bf16[1024,256]{1,0:T(8,128)(2,1)S(1)}, u32[]{:S(2)}, u32[]{:S(2)}) %collective-permute-start) | collective-permute-done | bytes 524320 | tf_op jit(solution)/shard_map/ppermute | solution.py:24
  70.1 0.8 copy-done.7
  70.9 4.2 %shard_map.164 = (bf16[32,1024]{1,0:T(8,128)(2,1)}, bf16[1024,256]{1,0:T(8,128)(2,1)}, bf16[1024,256]{1,0:T(8,128)(2,1)}) custom-call(s32[3]{0:T(128)} %pad_add_fusion.where, bf16[32,1024]{1,0:T(8,128)(2,1)} %query.1, bf16[32,1024]{1,0:T(8,128)(2,1)} %grad.1, bf16[1024,256]{1,0:T(8,128)(2,1)} %bitcast.58, bf16[1024,256]{1,0:T(8,128)(2,1)} %copy-done.7), custom_call_target="tpu_custom_call" | custom-call | flops 1000000000 | bytes 4000000 | tf_op jit(solution)/shard_map/pallas_call | solution.py:33
  75.2 2.1 %collective-permute-start.1 = (bf16[1024,256]{1,0:T(8,128)(2,1)}, bf16[1024,256]{1,0:T(8,128)(2,1)S(1)}, u32[]{:S(2)}, u32[]{:S(2)}) collective-permute-start(bf16[1024,256]{1,0:T(8,128)(2,1)} %get-tuple-element.20), channel_id=1, source_target_pairs={{0,8},{8,0},{1,9},{9,1},{2,10},{10,2},{3,11},{11,3},{4,12},{12,4},... | collective-permute-start | bytes 1572872 | tf_op jit(solution)/shard_map/ppermute | solution.py:24
  77.2 1.9 %collective-permute-done.1 = bf16[1024,256]{1,0:T(8,128)(2,1)S(1)} collective-permute-done((bf16[1024,256]{1,0:T(8,128)(2,1)}, bf16[1024,256]{1,0:T(8,128)(2,1)S(1)}, u32[]{:S(2)}, u32[]{:S(2)}) %collective-permute-start.1) | collective-permute-done | bytes 524320 | tf_op jit(solution)/shard_map/ppermute | solution.py:24
  79.2 2.0 %add_convert_fusion = bf16[1024,256]{1,0:T(8,128)(2,1)} fusion(bf16[1024,256]{1,0:T(8,128)(2,1)S(1)} %collective-permute-done.1, bf16[1024,256]{1,0:T(8,128)(2,1)} %get-tuple-element.19), kind=kLoop, calls=%fused_computation.5 | loop fusion | flops 1048576 | bytes 1572864 | tf_op jit(solution)/shard_map/convert_element_type | solution.py:215
  81.1 5.6 %all-to-all-start.3 = ((bf16[32,32,256]{2,1,0:T(8,128)(2,1)}), bf16[32,32,256]{2,1,0:T(8,128)(2,1)S(1)}, u32[]{:S(2)}, u32[]{:S(2)}) async-start(bf16[32,32,256]{2,1,0:T(8,128)(2,1)} %bitcast.21), calls=%async_computation.3 | async-start | bytes 1048576 | tf_op jit(solution)/shard_map/all_to_all | solution.py:20
  86.7 8.7 %all-gather.2.cloned.1.call-done = bf16[512,4096]{1,0:T(8,128)(2,1)} async-done(((bf16[512,512]{1,0:T(8,128)(2,1)}), bf16[512,4096]{1,0:T(8,128)(2,1)}) %all-gather.2.cloned.1.call-update) | async-done | bytes 4194320 | tf_op jit(solution)/shard_map/all_gather | solution.py:199
  95.4 3.7 %multiply_reduce_fusion = (f32[512]{0:T(512)S(1)}, f32[192,512]{1,0:T(8,128)S(1)}) fusion(bf16[1,192,512]{2,1,0:T(8,128)(2,1)S(1)} %copy-done.4, bf16[1,192,512]{2,1,0:T(8,128)(2,1)S(1)} %copy-done.5, bf16[512,4096]{1,0:T(8,128)(2,1)} %all-gather.2.cloned.1.call-done, bf16[1,192,4096]{2,1,0:T(8,128)(2,1)S(1)} %copy-done), kind=kOutput, calls=%fused_computation.20 | convolution fusion | flops 806190592 | bytes 6555648 | tf_op jit(solution)/shard_map/dot_general | solution.py:219
  99.2 0.1 reshape.46
  99.3 0.8 pad_maximum_fusion
  100.1 3.8 %all-to-all-done.3 = bf16[32,32,256]{2,1,0:T(8,128)(2,1)S(1)} async-done(((bf16[32,32,256]{2,1,0:T(8,128)(2,1)}), bf16[32,32,256]{2,1,0:T(8,128)(2,1)S(1)}, u32[]{:S(2)}, u32[]{:S(2)}) %all-to-all-start.3) | async-done | bytes 524320 | tf_op jit(solution)/shard_map/all_to_all | solution.py:20
  103.9 7.1 %all-to-all-start.1 = ((f32[64,1,16]{2,1,0:T(1,128)}), f32[64,1,16]{2,1,0:T(1,128)S(1)}, u32[]{:S(2)}, u32[]{:S(2)}) async-start(f32[64,1,16]{2,1,0:T(1,128)} %pad_maximum_fusion), calls=%async_computation.1 | async-start | bytes 65536 | tf_op jit(solution)/shard_map/all_to_all | solution.py:20
  111.0 0.7 reduce_sum.22.owned
  111.7 7.1 %all-to-all-done.1.returned = f32[64,1,16]{2,1,0:T(1,128)S(1)} async-done(((f32[64,1,16]{2,1,0:T(1,128)}), f32[64,1,16]{2,1,0:T(1,128)S(1)}, u32[]{:S(2)}, u32[]{:S(2)}) %all-to-all-start.1) | async-done | bytes 4128 | tf_op jit(solution)/shard_map/all_to_all | solution.py:20
  118.8 0.6 copy-done.3
  119.4 1.9 %shard_map.165 = bf16[8,40,256]{2,1,0:T(8,128)(2,1)} custom-call(s32[3]{0:T(128)} %pad_add_fusion.where, s32[8,32]{1,0:T(8,128)} %bitcast.63, s32[8,32]{1,0:T(8,128)} %get-tuple-element.17.ranks, f32[64,1,16]{2,1,0:T(1,128)} %copy-done.3, bf16[32,256]{1,0:T(8,128)(2,1)} %reduce_sum.22.owned), custom_call_target="tpu_custom_call" | custom-call | flops 1000000 | bytes 200000 | tf_op jit(solution)/shard_map/pallas_call | solution.py:33
  121.3 6.0 %all-to-all-start.4 = ((bf16[8,40,256]{2,1,0:T(8,128)(2,1)}), bf16[8,40,256]{2,1,0:T(8,128)(2,1)S(1)}, u32[]{:S(2)}, u32[]{:S(2)}) async-start(bf16[8,40,256]{2,1,0:T(8,128)(2,1)} %shard_map.165), calls=%async_computation.4 | async-start | bytes 327680 | tf_op jit(solution)/shard_map/all_to_all | solution.py:20
  127.2 0.9 slice_reduce_fusion
  128.2 0.1 mul.55
  128.3 4.4 %fusion = bf16[1,192,4096]{2,1,0:T(8,128)(2,1)} fusion(bf16[512,4096]{1,0:T(8,128)(2,1)} %all-gather.2.cloned.1.call-done, bf16[1,192,512]{2,1,0:T(8,128)(2,1)S(1)} %copy-done.4, f32[512]{0:T(512)S(1)} %mul.55, bf16[1,192,512]{2,1,0:T(8,128)(2,1)S(1)} %copy-done.5), kind=kOutput, calls=%fused_computation.1 | convolution fusion | flops 806977536 | bytes 6162432 | tf_op jit(solution)/shard_map/dot_general | solution.py:235
  132.6 0.9 fusion.13
  133.6 3.5 %all-to-all-done.4.terms = bf16[8,40,256]{2,1,0:T(8,128)(2,1)S(1)} async-done(((bf16[8,40,256]{2,1,0:T(8,128)(2,1)}), bf16[8,40,256]{2,1,0:T(8,128)(2,1)S(1)}, u32[]{:S(2)}, u32[]{:S(2)}) %all-to-all-start.4) | async-done | bytes 163872 | tf_op jit(solution)/shard_map/all_to_all | solution.py:20
  137.0 0.7 copy-done.1
  137.7 1.6 %shard_map.166 = (f32[32,512]{1,0:T(8,128)}, f32[32,512]{1,0:T(8,128)}, f32[8,32]{1,0:T(8,128)}) custom-call(s32[3]{0:T(128)} %pad_add_fusion.where, bf16[8,40,256]{2,1,0:T(8,128)(2,1)} %copy-done.1), custom_call_target="tpu_custom_call" | custom-call | flops 1000000 | bytes 300000 | tf_op jit(solution)/shard_map/pallas_call | solution.py:33
  (14 shorter events, 0.0 us)
Async XLA Ops:
  7.2 88.3 %copy-start = (bf16[1,192,4096]{2,1,0:T(8,128)(2,1)S(1)}, bf16[1,192,4096]{2,1,0:T(8,128)(2,1)}, u32[]{:S(2)}) copy-start(bf16[1,192,4096]{2,1,0:T(8,128)(2,1)} %param.15) | copy-start | bytes 4718596
  7.2 88.3 %all-gather.2.cloned.1.call-start = ((), (), s32[]{:S(2)}) async-start(), calls=%async_computation.5 | async-start | bytes 4718592 | tf_op jit(solution)/shard_map/all_gather | solution.py:199
  41.6 53.9 %copy-start.4 = (bf16[1,192,512]{2,1,0:T(8,128)(2,1)S(1)}, bf16[1,192,512]{2,1,0:T(8,128)(2,1)}, u32[]{:S(2)}) copy-start(bf16[1,192,512]{2,1,0:T(8,128)(2,1)} %param.17) | copy-start | bytes 589828
  41.6 53.9 %copy-start.5 = (bf16[1,192,512]{2,1,0:T(8,128)(2,1)S(1)}, bf16[1,192,512]{2,1,0:T(8,128)(2,1)}, u32[]{:S(2)}) copy-start(bf16[1,192,512]{2,1,0:T(8,128)(2,1)} %param.16) | copy-start | bytes 589828
  66.3 3.8 %copy-start.2 = (bf16[32,32,256]{2,1,0:T(8,128)(2,1)}, bf16[32,32,256]{2,1,0:T(8,128)(2,1)S(1)}, u32[]{:S(2)}) copy-start(bf16[32,32,256]{2,1,0:T(8,128)(2,1)S(1)} %all_to_all.26) | copy-start | bytes 1572868
  66.3 3.8 %collective-permute-start = (bf16[1024,256]{1,0:T(8,128)(2,1)S(1)}, bf16[1024,256]{1,0:T(8,128)(2,1)S(1)}, u32[]{:S(2)}, u32[]{:S(2)}) collective-permute-start(bf16[1024,256]{1,0:T(8,128)(2,1)S(1)} %bitcast.57), channel_id=1, source_target_pairs={{0,8},{8,0},{1,9},{9,1},{2,10},{10,2},{3,11},{11,3},{4,12},{12,4},... | collective-permute-start | bytes 1572872 | tf_op jit(solution)/shard_map/ppermute | solution.py:24
  70.1 0.8 copy-start.7
  75.2 4.0 %collective-permute-start.1 = (bf16[1024,256]{1,0:T(8,128)(2,1)}, bf16[1024,256]{1,0:T(8,128)(2,1)S(1)}, u32[]{:S(2)}, u32[]{:S(2)}) collective-permute-start(bf16[1024,256]{1,0:T(8,128)(2,1)} %get-tuple-element.20), channel_id=1, source_target_pairs={{0,8},{8,0},{1,9},{9,1},{2,10},{10,2},{3,11},{11,3},{4,12},{12,4},... | collective-permute-start | bytes 1572872 | tf_op jit(solution)/shard_map/ppermute | solution.py:24
  81.1 22.7 %all-to-all-start.3 = ((bf16[32,32,256]{2,1,0:T(8,128)(2,1)}), bf16[32,32,256]{2,1,0:T(8,128)(2,1)S(1)}, u32[]{:S(2)}, u32[]{:S(2)}) async-start(bf16[32,32,256]{2,1,0:T(8,128)(2,1)} %bitcast.21), calls=%async_computation.3 | async-start | bytes 1048576 | tf_op jit(solution)/shard_map/all_to_all | solution.py:20
  86.7 12.6 %copy-start.6 = (f32[64,128]{1,0:T(8,128)S(1)}, f32[64,128]{1,0:T(8,128)}, u32[]{:S(2)}) copy-start(f32[64,128]{1,0:T(8,128)} %get-tuple-element.16) | copy-start | bytes 98308
  103.9 14.9 %all-to-all-start.1 = ((f32[64,1,16]{2,1,0:T(1,128)}), f32[64,1,16]{2,1,0:T(1,128)S(1)}, u32[]{:S(2)}, u32[]{:S(2)}) async-start(f32[64,1,16]{2,1,0:T(1,128)} %pad_maximum_fusion), calls=%async_computation.1 | async-start | bytes 65536 | tf_op jit(solution)/shard_map/all_to_all | solution.py:20
  118.8 0.6 copy-start.3
  121.3 15.7 %all-to-all-start.4 = ((bf16[8,40,256]{2,1,0:T(8,128)(2,1)}), bf16[8,40,256]{2,1,0:T(8,128)(2,1)S(1)}, u32[]{:S(2)}, u32[]{:S(2)}) async-start(bf16[8,40,256]{2,1,0:T(8,128)(2,1)} %shard_map.165), calls=%async_computation.4 | async-start | bytes 327680 | tf_op jit(solution)/shard_map/all_to_all | solution.py:20
  137.0 0.7 copy-start.1
Sparse Core Ops, SparseCore 0:
  41.7 53.6 all-gather.1

commit v7 on v6

--- a/solution.py
+++ b/solution.py
@@ -28,14 +28,16 @@
     return lax.broadcasted_iota(jnp.int32, shape, dim)
 
 
-def call(body, outs, ins, flops, size):
+def call(body, outs, ins, flops, size, scalars=1, room=None):
     vmem = pl.BlockSpec(memory_space=pltpu.VMEM)
+    smem = pl.BlockSpec(memory_space=pltpu.SMEM)
     return pl.pallas_call(
         body,
         out_shape=outs,
-        in_specs=[pl.BlockSpec(memory_space=pltpu.SMEM)] + [vmem] * (len(ins) - 1),
+        in_specs=[smem] * scalars + [vmem] * (len(ins) - scalars),
         out_specs=jax.tree.map(lambda _: vmem, outs),
         cost_estimate=pl.CostEstimate(flops=flops, bytes_accessed=size, transcendentals=0),
+        compiler_params=pltpu.CompilerParams(vmem_limit_bytes=room and room << 20),
     )(*ins)
 
 
@@ -52,7 +54,7 @@
     return jnp.where((named > 0.0) & (rank == place), 1.0, 0.0), expert, place
 
 
-def pack_body(where, kept, ids, d_out, message):
+def pack_body(kept, ids, d_out, message):
     rows = ids.shape[1]
     tok_dev = d_out.shape[0]
     taken, _, _ = named_slots(ids, message.shape[0])
@@ -61,7 +63,7 @@
     message[...] = jnp.dot(taken.astype(BF16), picked, preferred_element_type=F32).astype(BF16)
 
 
-def tables_body(where, ids, gates, keys, values, kv, ranks, table):
+def tables_body(where, ids, gates, keys, values, kv, code, table):
     top, rows = ids.shape
     experts = table.shape[0]
     chips = kv.shape[0] // rows
@@ -72,12 +74,15 @@
         ).reshape(chips * rows, HD)
     taken, expert, place = named_slots(ids, experts * 8)
     weight = jnp.zeros(taken.shape, F32)
+    ranks = []
     for j in range(top):
         hit = (ids[j : j + 1, :] == expert) & (taken > 0.0)
         weight = jnp.where(hit, gates[j : j + 1, :].astype(F32), weight)
-        ranks[j : j + 1, :] = jnp.sum(
-            jnp.where(hit, place, 0.0), axis=0, keepdims=True
-        ).astype(jnp.int32)
+        ranks.append(
+            jnp.sum(jnp.where(hit, place, 0.0), axis=0, keepdims=True).astype(jnp.int32)
+        )
+    code[0:1, :] = jnp.concatenate([ids[j : j + 1, :] for j in range(top)], axis=1)
+    code[1:2, :] = jnp.concatenate(ranks, axis=1)
     column = jnp.dot(weight.astype(BF16), jnp.ones((rows, HD), BF16), preferred_element_type=F32)
     own = jnp.where(iota(column.shape, 0) % 8 == iota(column.shape, 1), column, 0.0)
     table[...] = jnp.sum(own.reshape(experts, 8, HD), axis=1)
@@ -124,38 +129,36 @@
         d_query[:, g * HD : (g + 1) * HD] = dq[g * keep_dev : (g + 1) * keep_dev]
 
 
-def gates_body(where, ids, ranks, returned, owned, out):
-    top, rows = ids.shape
-    experts = returned.shape[0]
+def gates_body(code, got, owned, out):
+    experts = got.shape[0]
     keep_dev = owned.shape[0]
-    table = returned[...].reshape(experts, returned.shape[2])[:, :8]
-    result = jnp.zeros((top, HD), F32)
-    for j in range(top):
-        expert = jnp.concatenate([ids[j : j + 1, :]] * (HD // rows), axis=1)
-        rank = jnp.concatenate([ranks[j : j + 1, :]] * (HD // rows), axis=1)
-        pick = jnp.where(expert == iota((experts, HD), 0), 1.0, 0.0)
-        found = lax.dot_general(
-            table, pick, TN, preferred_element_type=F32, precision=lax.Precision.HIGHEST
-        )
-        hit = jnp.where(iota(found.shape, 0) == rank, found, 0.0)
-        result = jnp.where(iota((top, HD), 0) == j, jnp.sum(hit, axis=0, keepdims=True), result)
-    high = result.astype(BF16)
-    low = (result - high.astype(F32)).astype(BF16)
+    pairs = code.shape[1]
+    pick = jnp.where(code[0:1, :] == iota((experts, pairs), 0), 1.0, 0.0)
+    table = got[...].reshape(experts, got.shape[2])[:, :8]
+    found = lax.dot_general(
+        table, pick, TN, preferred_element_type=F32, precision=lax.Precision.HIGHEST
+    )
+    hit = jnp.where(iota(found.shape, 0) == code[1:2, :], found, 0.0)
+    result = jnp.sum(hit, axis=0, keepdims=True)
+    high = result.astype(BF16).astype(F32)
+    row = iota((8, pairs), 0)
+    tail = jnp.where(row == 0, high, jnp.where(row == 1, result - high, 0.0)).astype(BF16)
     for i in range(out.shape[0]):
         out[i, :keep_dev] = owned[...]
-        out[i, keep_dev:, :HD] = high
-        out[i, keep_dev:, HD:] = low
-
-
-def final_body(where, terms, d_key, d_value, d_gates):
-    keep_dev = d_key.shape[0]
+        out[i, keep_dev:] = tail
+
+
+def final_body(terms, d_key, d_value, d_gates):
+    top, keep_dev = d_gates.shape
     per = terms.shape[0] // KVH
     for h in range(KVH):
         both = sum(terms[h * per + i, :keep_dev].astype(F32) for i in range(per))
         d_key[:, h * HD : (h + 1) * HD] = both[:, :HD]
         d_value[:, h * HD : (h + 1) * HD] = both[:, HD:]
     parts = jnp.sum(terms[:, keep_dev:, :].astype(F32), axis=0)
-    d_gates[...] = (parts[:, :HD] + parts[:, HD:])[:, : d_gates.shape[1]]
+    flat = parts[0:1] + parts[1:2]
+    for j in range(top):
+        d_gates[j : j + 1, :] = flat[:, j * keep_dev : (j + 1) * keep_dev]
 
 
 def on_device(
@@ -180,16 +183,17 @@
     message = call(
         pack_body,
         struct((slots, width), BF16),
-        (where, kept.reshape(1, keep_dev), ids, d_out),
+        (kept.reshape(1, keep_dev), ids, d_out),
         200_000_000,
         2_000_000,
+        scalars=0,
     )
     arrived = exchange(message.reshape(n_experts, cap, width), GX)
-    kv, ranks, table = call(
+    kv, code, table = call(
         tables_body,
         (
             struct((chips * keep_dev, 2 * HD), BF16),
-            struct((top, keep_dev), jnp.int32),
+            struct((2, top * keep_dev), jnp.int32),
             struct((n_experts, HD), F32),
         ),
         (where, ids, gates.T, keys, values),
@@ -211,6 +215,7 @@
         (where, query, d_attn, kv_mine, kv_other),
         1_000_000_000,
         4_000_000,
+        room=24,
     )
     chip_part = (keep.astype(F32) + to_partner(send).astype(F32)).astype(BF16)
     summed = exchange(chip_part.reshape(chips, keep_dev, 2 * HD), ZX)
@@ -236,9 +241,11 @@
     merged = call(
         gates_body,
         struct((n_ta, keep_dev + top, 2 * HD), BF16),
-        (where, ids, ranks, returned, owned),
+        (code, returned, owned),
         1_000_000,
         200_000,
+        scalars=0,
+        room=8,
     )
     d_key, d_value, d_gates = call(
         final_body,
@@ -247,9 +254,11 @@
             struct((keep_dev, KVH * HD), F32),
             struct((top, keep_dev), F32),
         ),
-        (where, exchange(merged, "ta")),
+        (exchange(merged, "ta"),),
         1_000_000,
         300_000,
+        scalars=0,
+        room=8,
     )
     return (d_down[None], d_gate[None], d_up[None], d_gates.T, d_query, d_key, d_value)
 

time: 148 us -> 144 us (0.973)
  Pallas kernels: 12.5 us -> 9.79 us
  other arithmetic: 4.98 us -> 3.3 us
    pallas_call x5, Pallas kernels: 12.5 us -> 9.79 us  [call(): pl.pallas_call(body, out_shape=outs, in_specs=[smem] * scalars + [vmem] *...]
  transfers between devices with their start and end apart: 6 -> 6, of which waited for: 6 -> 6; matrix products, arithmetic and copies ran while one was open for 9% -> 8% of each run, Pallas kernels for 5% -> 4%
where the time goes in v7:
time: 144 us; the launch traced here: 142 us
  blocking collectives  53.6 us (37%)
  waiting for transfers between devices  28.1 us (20%)
  starting transfers between devices  22.6 us (16%)
  between operations  14.1 us (10%)
  Pallas kernels  9.79 us (7%)
  matrix products  8.12 us (6%)
  other arithmetic  3.3 us (2%)
  local copies, waits for them, and re-layouts  2.7 us (2%)
    all_to_all x2, blocking collectives, exchange(): return lax.all_to_all(values, axes, split_axis=0, concat_axis=0, tiled=True)  53.6 us
    all_to_all x3, starting transfers between devices, exchange(): return lax.all_to_all(values, axes, split_axis=0, concat_axis=0, tiled=True)  18.6 us
    all_to_all x3, waiting for transfers between devices, exchange(): return lax.all_to_all(values, axes, split_axis=0, concat_axis=0, tiled=True)  15.7 us
    pallas_call x5, Pallas kernels, call(): pl.pallas_call(body, out_shape=outs, in_specs=[smem] * scalars + [vmem] *...  9.79 us
    all_gather x1, waiting for transfers between devices, on_device(): lax.all_gather(arrived.reshape(slots, width), 'ta', axis=1, tiled=True)  8.73 us
    dot_general x1, matrix products, on_device(): jnp.dot(weighted, slot_rows, preferred_element_type=F32).astype(BF16)  4.37 us
    ppermute x2, starting transfers between devices, to_partner(): return lax.ppermute(values, 'c', [(0, 1), (1, 0)])  3.94 us
    dot_general x1, matrix products, on_device(): lax.dot_general(down_weight[0], slot_rows, NT, preferred_element_type=F32)  3.75 us
  transfers between devices with their start and end apart: 6, of which 6 were waited for; matrix products, arithmetic and copies ran while one was open for 8% of the time, Pallas kernels for 4%

profile of v7, /device:TPU:6, one launch (start us, length us, event | category | flops | bytes accessed | tf_op | source)
XLA Modules:
  0.0 142.4 jit_solution(4575587853350869533)
XLA Ops:
  7.2 0.0 all-gather.2.cloned.1.call-start
  7.2 2.4 %shard_map.162 = bf16[512,512]{1,0:T(8,128)(2,1)} custom-call(s32[1,32]{1,0:T(1,128)} %bitcast.65, s32[8,32]{1,0:T(8,128)} %bitcast.62, bf16[256,512]{1,0:T(8,128)(2,1)} %d_out.1), custom_call_target="tpu_custom_call" | custom-call | flops 200000000 | bytes 2000000 | tf_op jit(solution)/shard_map/pallas_call | solution.py:34
  9.6 31.5 %all_to_all.25 = bf16[64,8,512]{2,1,0:T(8,128)(2,1)} all-to-all(bf16[64,8,512]{2,1,0:T(8,128)(2,1)} %bitcast.58), channel_id=1, replica_groups=mesh['z'=8,'x'=4,'c'=2,'ta'=8] {'z','x','c'}, dimensions={0} | all-to-all | bytes 1048576 | tf_op jit(solution)/shard_map/all_to_all | solution.py:20
  41.1 0.6 pad_add_fusion.where
  41.7 2.5 %shard_map.163 = (bf16[1024,256]{1,0:T(8,128)(2,1)}, s32[2,256]{1,0:T(2,128)}, f32[64,128]{1,0:T(8,128)}) custom-call(s32[3]{0:T(128)} %pad_add_fusion.where, s32[8,32]{1,0:T(8,128)} %bitcast.63, bf16[8,32]{1,0:T(8,128)(2,1)} %bitcast.64, bf16[32,512]{1,0:T(8,128)(2,1)} %keys.1, bf16[32,512]{1,0:T(8,128)(2,1)} %values.1), custom_call_target="tpu_custom_call" | custom-call | flops 10000000 | bytes 1000000 | tf_op jit(solution)/shard_map/pallas_call | solution.py:34
  44.2 22.2 %all_to_all.26 = bf16[32,32,256]{2,1,0:T(8,128)(2,1)S(1)} all-to-all(bf16[32,32,256]{2,1,0:T(8,128)(2,1)} %bitcast.59), channel_id=1, replica_groups=mesh['z'=8,'x'=4,'c'=2,'ta'=8] {'z','x'}, dimensions={0} | all-to-all | bytes 1048576 | tf_op jit(solution)/shard_map/all_to_all | solution.py:20
  66.4 1.9 %collective-permute-start = (bf16[1024,256]{1,0:T(8,128)(2,1)S(1)}, bf16[1024,256]{1,0:T(8,128)(2,1)S(1)}, u32[]{:S(2)}, u32[]{:S(2)}) collective-permute-start(bf16[1024,256]{1,0:T(8,128)(2,1)S(1)} %bitcast.55), channel_id=1, source_target_pairs={{0,8},{8,0},{1,9},{9,1},{2,10},{10,2},{3,11},{11,3},{4,12},{12,4},... | collective-permute-start | bytes 1572872 | tf_op jit(solution)/shard_map/ppermute | solution.py:24
  68.3 1.9 %collective-permute-done.other = bf16[1024,256]{1,0:T(8,128)(2,1)S(1)} collective-permute-done((bf16[1024,256]{1,0:T(8,128)(2,1)S(1)}, bf16[1024,256]{1,0:T(8,128)(2,1)S(1)}, u32[]{:S(2)}, u32[]{:S(2)}) %collective-permute-start) | collective-permute-done | bytes 524320 | tf_op jit(solution)/shard_map/ppermute | solution.py:24
  70.2 0.7 copy-done.2
  70.8 0.8 copy-done.3
  71.7 0.8 copy-done.4
  72.5 3.4 %shard_map.164 = (bf16[32,1024]{1,0:T(8,128)(2,1)}, bf16[1024,256]{1,0:T(8,128)(2,1)S(1)}, bf16[1024,256]{1,0:T(8,128)(2,1)S(1)}) custom-call(s32[3]{0:T(128)S(1)} %copy-done.2, bf16[32,1024]{1,0:T(8,128)(2,1)S(1)} %copy-done.3, bf16[32,1024]{1,0:T(8,128)(2,1)S(1)} %copy-done.4, bf16[1024,256]{1,0:T(8,128)(2,1)S(1)} %bitcast.56, ...), custom_call_target="tpu_custom_call" | custom-call | flops 1000000000 | bytes 4000000 | tf_op jit(solution)/shard_map/pallas_call | solution.py:34
  75.9 2.0 %collective-permute-start.1 = (bf16[1024,256]{1,0:T(8,128)(2,1)S(1)}, bf16[1024,256]{1,0:T(8,128)(2,1)S(1)}, u32[]{:S(2)}, u32[]{:S(2)}) collective-permute-start(bf16[1024,256]{1,0:T(8,128)(2,1)S(1)} %get-tuple-element.20), channel_id=1, source_target_pairs={{0,8},{8,0},{1,9},{9,1},{2,10},{10,2},{3,11},{11,3},{4,12},{12,4},... | collective-permute-start | bytes 1572872 | tf_op jit(solution)/shard_map/ppermute | solution.py:24
  77.9 1.8 %collective-permute-done.1 = bf16[1024,256]{1,0:T(8,128)(2,1)S(1)} collective-permute-done((bf16[1024,256]{1,0:T(8,128)(2,1)S(1)}, bf16[1024,256]{1,0:T(8,128)(2,1)S(1)}, u32[]{:S(2)}, u32[]{:S(2)}) %collective-permute-start.1) | collective-permute-done | bytes 524320 | tf_op jit(solution)/shard_map/ppermute | solution.py:24
  79.7 0.9 add_convert_fusion
  80.6 5.6 %all-to-all-start.3 = ((bf16[32,32,256]{2,1,0:T(8,128)(2,1)}), bf16[32,32,256]{2,1,0:T(8,128)(2,1)S(1)}, u32[]{:S(2)}, u32[]{:S(2)}) async-start(bf16[32,32,256]{2,1,0:T(8,128)(2,1)} %bitcast.21), calls=%async_computation.3 | async-start | bytes 1048576 | tf_op jit(solution)/shard_map/all_to_all | solution.py:20
  86.2 8.7 %all-gather.2.cloned.1.call-done = bf16[512,4096]{1,0:T(8,128)(2,1)} async-done(((bf16[512,512]{1,0:T(8,128)(2,1)}), bf16[512,4096]{1,0:T(8,128)(2,1)}) %all-gather.2.cloned.1.call-update) | async-done | bytes 4194320 | tf_op jit(solution)/shard_map/all_gather | solution.py:203
  94.9 3.7 %multiply_reduce_fusion = (f32[512]{0:T(512)S(1)}, f32[192,512]{1,0:T(8,128)S(1)}) fusion(bf16[1,192,512]{2,1,0:T(8,128)(2,1)S(1)} %copy-done.5, bf16[1,192,512]{2,1,0:T(8,128)(2,1)S(1)} %copy-done.6, bf16[512,4096]{1,0:T(8,128)(2,1)} %all-gather.2.cloned.1.call-done, bf16[1,192,4096]{2,1,0:T(8,128)(2,1)S(1)} %copy-done), kind=kOutput, calls=%fused_computation.20 | convolution fusion | flops 806190592 | bytes 6555648 | tf_op jit(solution)/shard_map/dot_general | solution.py:224
  98.7 0.1 reshape.46
  98.8 0.8 pad_maximum_fusion
  99.5 3.8 %all-to-all-done.3 = bf16[32,32,256]{2,1,0:T(8,128)(2,1)S(1)} async-done(((bf16[32,32,256]{2,1,0:T(8,128)(2,1)}), bf16[32,32,256]{2,1,0:T(8,128)(2,1)S(1)}, u32[]{:S(2)}, u32[]{:S(2)}) %all-to-all-start.3) | async-done | bytes 524320 | tf_op jit(solution)/shard_map/all_to_all | solution.py:20
  103.3 7.1 %all-to-all-start.1 = ((f32[64,1,16]{2,1,0:T(1,128)}), f32[64,1,16]{2,1,0:T(1,128)S(1)}, u32[]{:S(2)}, u32[]{:S(2)}) async-start(f32[64,1,16]{2,1,0:T(1,128)} %pad_maximum_fusion), calls=%async_computation.1 | async-start | bytes 65536 | tf_op jit(solution)/shard_map/all_to_all | solution.py:20
  110.4 0.1 reduce_sum.22.owned
  110.5 7.7 %all-to-all-done.1.got = f32[64,1,16]{2,1,0:T(1,128)S(1)} async-done(((f32[64,1,16]{2,1,0:T(1,128)}), f32[64,1,16]{2,1,0:T(1,128)S(1)}, u32[]{:S(2)}, u32[]{:S(2)}) %all-to-all-start.1) | async-done | bytes 4128 | tf_op jit(solution)/shard_map/all_to_all | solution.py:20
  118.3 0.9 shard_map.165
  119.2 5.9 %all-to-all-start.4 = ((bf16[8,40,256]{2,1,0:T(8,128)(2,1)}), bf16[8,40,256]{2,1,0:T(8,128)(2,1)S(1)}, u32[]{:S(2)}, u32[]{:S(2)}) async-start(bf16[8,40,256]{2,1,0:T(8,128)(2,1)} %shard_map.165), calls=%async_computation.4 | async-start | bytes 327680 | tf_op jit(solution)/shard_map/all_to_all | solution.py:20
  125.1 0.2 slice_reduce_fusion
  125.3 0.1 mul.55
  125.4 4.4 %fusion = bf16[1,192,4096]{2,1,0:T(8,128)(2,1)} fusion(bf16[512,4096]{1,0:T(8,128)(2,1)} %all-gather.2.cloned.1.call-done, bf16[1,192,512]{2,1,0:T(8,128)(2,1)S(1)} %copy-done.5, f32[512]{0:T(512)S(1)} %mul.55, bf16[1,192,512]{2,1,0:T(8,128)(2,1)S(1)} %copy-done.6), kind=kOutput, calls=%fused_computation.1 | convolution fusion | flops 806977536 | bytes 6162432 | tf_op jit(solution)/shard_map/dot_general | solution.py:240
  129.7 0.9 fusion.13
  130.7 4.2 %all-to-all-done.4.terms = bf16[8,40,256]{2,1,0:T(8,128)(2,1)S(1)} async-done(((bf16[8,40,256]{2,1,0:T(8,128)(2,1)}), bf16[8,40,256]{2,1,0:T(8,128)(2,1)S(1)}, u32[]{:S(2)}, u32[]{:S(2)}) %all-to-all-start.4) | async-done | bytes 163872 | tf_op jit(solution)/shard_map/all_to_all | solution.py:20
  134.9 0.7 shard_map.166
  (14 shorter events, 0.1 us)
Async XLA Ops:
  7.2 87.7 %copy-start = (bf16[1,192,4096]{2,1,0:T(8,128)(2,1)S(1)}, bf16[1,192,4096]{2,1,0:T(8,128)(2,1)}, u32[]{:S(2)}) copy-start(bf16[1,192,4096]{2,1,0:T(8,128)(2,1)} %param.15) | copy-start | bytes 4718596
  7.2 87.7 %all-gather.2.cloned.1.call-start = ((), (), s32[]{:S(2)}) async-start(), calls=%async_computation.5 | async-start | bytes 4718592 | tf_op jit(solution)/shard_map/all_gather | solution.py:203
  41.1 53.9 %copy-start.5 = (bf16[1,192,512]{2,1,0:T(8,128)(2,1)S(1)}, bf16[1,192,512]{2,1,0:T(8,128)(2,1)}, u32[]{:S(2)}) copy-start(bf16[1,192,512]{2,1,0:T(8,128)(2,1)} %param.17) | copy-start | bytes 589828
  41.1 53.9 %copy-start.6 = (bf16[1,192,512]{2,1,0:T(8,128)(2,1)S(1)}, bf16[1,192,512]{2,1,0:T(8,128)(2,1)}, u32[]{:S(2)}) copy-start(bf16[1,192,512]{2,1,0:T(8,128)(2,1)} %param.16) | copy-start | bytes 589828
  66.4 3.8 %collective-permute-start = (bf16[1024,256]{1,0:T(8,128)(2,1)S(1)}, bf16[1024,256]{1,0:T(8,128)(2,1)S(1)}, u32[]{:S(2)}, u32[]{:S(2)}) collective-permute-start(bf16[1024,256]{1,0:T(8,128)(2,1)S(1)} %bitcast.55), channel_id=1, source_target_pairs={{0,8},{8,0},{1,9},{9,1},{2,10},{10,2},{3,11},{11,3},{4,12},{12,4},... | collective-permute-start | bytes 1572872 | tf_op jit(solution)/shard_map/ppermute | solution.py:24
  70.2 0.7 copy-start.2
  70.8 0.8 copy-start.3
  71.6 0.8 copy-start.4
  75.9 3.8 %collective-permute-start.1 = (bf16[1024,256]{1,0:T(8,128)(2,1)S(1)}, bf16[1024,256]{1,0:T(8,128)(2,1)S(1)}, u32[]{:S(2)}, u32[]{:S(2)}) collective-permute-start(bf16[1024,256]{1,0:T(8,128)(2,1)S(1)} %get-tuple-element.20), channel_id=1, source_target_pairs={{0,8},{8,0},{1,9},{9,1},{2,10},{10,2},{3,11},{11,3},{4,12},{12,4},... | collective-permute-start | bytes 1572872 | tf_op jit(solution)/shard_map/ppermute | solution.py:24
  80.6 22.7 %all-to-all-start.3 = ((bf16[32,32,256]{2,1,0:T(8,128)(2,1)}), bf16[32,32,256]{2,1,0:T(8,128)(2,1)S(1)}, u32[]{:S(2)}, u32[]{:S(2)}) async-start(bf16[32,32,256]{2,1,0:T(8,128)(2,1)} %bitcast.21), calls=%async_computation.3 | async-start | bytes 1048576 | tf_op jit(solution)/shard_map/all_to_all | solution.py:20
  86.2 12.6 %copy-start.7 = (f32[64,128]{1,0:T(8,128)S(1)}, f32[64,128]{1,0:T(8,128)}, u32[]{:S(2)}) copy-start(f32[64,128]{1,0:T(8,128)} %get-tuple-element.16) | copy-start | bytes 98308
  86.2 32.1 %copy-start.1 = (s32[2,256]{1,0:T(2,128)S(1)}, s32[2,256]{1,0:T(2,128)}, u32[]{:S(2)}) copy-start(s32[2,256]{1,0:T(2,128)} %get-tuple-element.17.code) | copy-start | bytes 6148
  103.3 15.0 %all-to-all-start.1 = ((f32[64,1,16]{2,1,0:T(1,128)}), f32[64,1,16]{2,1,0:T(1,128)S(1)}, u32[]{:S(2)}, u32[]{:S(2)}) async-start(f32[64,1,16]{2,1,0:T(1,128)} %pad_maximum_fusion), calls=%async_computation.1 | async-start | bytes 65536 | tf_op jit(solution)/shard_map/all_to_all | solution.py:20
  119.2 15.7 %all-to-all-start.4 = ((bf16[8,40,256]{2,1,0:T(8,128)(2,1)}), bf16[8,40,256]{2,1,0:T(8,128)(2,1)S(1)}, u32[]{:S(2)}, u32[]{:S(2)}) async-start(bf16[8,40,256]{2,1,0:T(8,128)(2,1)} %shard_map.165), calls=%async_computation.4 | async-start | bytes 327680 | tf_op jit(solution)/shard_map/all_to_all | solution.py:20
Sparse Core Ops, SparseCore 0:
  41.2 53.6 all-gather.1

commit v8 on v7

--- a/solution.py
+++ b/solution.py
@@ -63,11 +63,14 @@
     message[...] = jnp.dot(taken.astype(BF16), picked, preferred_element_type=F32).astype(BF16)
 
 
-def tables_body(where, ids, gates, keys, values, kv, code, table):
+def tables_body(where, ids, gates, keys, values, query, grad, kv, code, table, q, o):
     top, rows = ids.shape
     experts = table.shape[0]
     chips = kv.shape[0] // rows
     head = pl.multiple_of(where[0] * HD, HD)
+    for to, source in ((q, query), (o, grad)):
+        for g in range(source.shape[1] // HD):
+            to[g * rows : (g + 1) * rows, :] = source[:, g * HD : (g + 1) * HD]
     for at, source in ((0, keys), (HD, values)):
         kv[:, at : at + HD] = jnp.broadcast_to(
             source[:, pl.ds(head, HD)][None], (chips, rows, HD)
@@ -90,17 +93,13 @@
 
 def attention_body(where, query, grad, mine, other, d_query, keep, send):
     core, block = where[1], where[2]
-    keep_dev = query.shape[0]
-    heads = query.shape[1] // HD
+    keep_dev = d_query.shape[0]
+    heads = d_query.shape[1] // HD
     rows = keep_dev * heads
     half = mine.shape[0]
     scale = HD ** (-0.5)
-
-    def stacked(ref):
-        return jnp.concatenate([ref[:, g * HD : (g + 1) * HD] for g in range(heads)], axis=0)
-
-    q = stacked(query)
-    o = stacked(grad)
+    q = query[...]
+    o = grad[...]
     query_pos = block * keep_dev + iota((rows, half), 0) % keep_dev
     column = iota((rows, half), 1)
     base = column // keep_dev * (2 * keep_dev) + column % keep_dev
@@ -189,16 +188,19 @@
         scalars=0,
     )
     arrived = exchange(message.reshape(n_experts, cap, width), GX)
-    kv, code, table = call(
+    kv, code, table, q_rows, o_rows = call(
         tables_body,
         (
             struct((chips * keep_dev, 2 * HD), BF16),
             struct((2, top * keep_dev), jnp.int32),
             struct((n_experts, HD), F32),
+            struct((keep_dev * local_heads, HD), BF16),
+            struct((keep_dev * local_heads, HD), BF16),
         ),
-        (where, ids, gates.T, keys, values),
+        (where, ids, gates.T, keys, values, query, d_attn),
         10_000_000,
         1_000_000,
+        room=8,
     )
     slot_rows = lax.all_gather(arrived.reshape(slots, width), "ta", axis=1, tiled=True)
 
@@ -212,7 +214,7 @@
             struct((half, 2 * HD), BF16),
             struct((half, 2 * HD), BF16),
         ),
-        (where, query, d_attn, kv_mine, kv_other),
+        (where, q_rows, o_rows, kv_mine, kv_other),
         1_000_000_000,
         4_000_000,
         room=24,

time: 144 us -> 145 us (level)
  local copies, waits for them, and re-layouts: 2.7 us -> 4.97 us
    unnamed x16 -> x18, local copies, waits for them, and re-layouts: 2.37 us -> 4.64 us
  transfers between devices with their start and end apart: 6 -> 6, of which waited for: 6 -> 6; matrix products, arithmetic and copies ran while one was open for 8% -> 8% of each run, Pallas kernels for 4% -> 3%
where the time goes in v8:
time: 145 us; the launch traced here: 143 us
  blocking collectives  53.4 us (37%)
  waiting for transfers between devices  28.1 us (19%)
  starting transfers between devices  22.6 us (16%)
  between operations  14.1 us (10%)
  Pallas kernels  8.8 us (6%)
  matrix products  8.12 us (6%)
  local copies, waits for them, and re-layouts  4.97 us (3%)
  other arithmetic  2.81 us (2%)
    all_to_all x2, blocking collectives, exchange(): return lax.all_to_all(values, axes, split_axis=0, concat_axis=0, tiled=True)  53.4 us
    all_to_all x3, starting transfers between devices, exchange(): return lax.all_to_all(values, axes, split_axis=0, concat_axis=0, tiled=True)  18.6 us
    all_to_all x3, waiting for transfers between devices, exchange(): return lax.all_to_all(values, axes, split_axis=0, concat_axis=0, tiled=True)  16.3 us
    pallas_call x5, Pallas kernels, call(): pl.pallas_call(body, out_shape=outs, in_specs=[smem] * scalars + [vmem] *...  8.8 us
    all_gather x1, waiting for transfers between devices, on_device(): lax.all_gather(arrived.reshape(slots, width), 'ta', axis=1, tiled=True)  8.15 us
    unnamed x18, local copies, waits for them, and re-layouts  4.64 us
    dot_general x1, matrix products, on_device(): jnp.dot(weighted, slot_rows, preferred_element_type=F32).astype(BF16)  4.37 us
    ppermute x2, starting transfers between devices, to_partner(): return lax.ppermute(values, 'c', [(0, 1), (1, 0)])  3.94 us
  transfers between devices with their start and end apart: 6, of which 6 were waited for; matrix products, arithmetic and copies ran while one was open for 8% of the time, Pallas kernels for 3%

profile of v8, /device:TPU:6, one launch (start us, length us, event | category | flops | bytes accessed | tf_op | source)
XLA Modules:
  0.0 143.0 jit_solution(3537238426904626826)
XLA Ops:
  7.2 2.4 %shard_map.162 = bf16[512,512]{1,0:T(8,128)(2,1)} custom-call(s32[1,32]{1,0:T(1,128)} %bitcast.65, s32[8,32]{1,0:T(8,128)} %bitcast.59, bf16[256,512]{1,0:T(8,128)(2,1)} %d_out.1), custom_call_target="tpu_custom_call" | custom-call | flops 200000000 | bytes 2000000 | tf_op jit(solution)/shard_map/pallas_call | solution.py:34
  9.6 31.5 %all_to_all.25 = bf16[64,8,512]{2,1,0:T(8,128)(2,1)} all-to-all(bf16[64,8,512]{2,1,0:T(8,128)(2,1)} %bitcast.63), channel_id=1, replica_groups=mesh['z'=8,'x'=4,'c'=2,'ta'=8] {'z','x','c'}, dimensions={0} | all-to-all | bytes 1048576 | tf_op jit(solution)/shard_map/all_to_all | solution.py:20
  41.2 0.9 copy-done.1
  42.1 0.8 copy-done.2
  42.9 0.8 copy-done.3
  43.7 0.8 copy-done.4
  44.4 0.7 copy-done.5
  45.1 0.7 copy-done.6
  45.8 1.5 %shard_map.163 = (bf16[1024,256]{1,0:T(8,128)(2,1)S(1)}, s32[2,256]{1,0:T(2,128)S(1)}, f32[64,128]{1,0:T(8,128)S(1)}, bf16[256,128]{1,0:T(8,128)(2,1)S(1)}, bf16[256,128]{1,0:T(8,128)(2,1)S(1)}) custom-call(s32[3]{0:T(128)S(1)} %pad_add_fusion.where, s32[8,32]{1,0:T(8,128)S(1)} %bitcast.60, bf16[8,32]{1,0:T(8,128)(2,1)S(1)} %bitcast.61, ...), custom_call_target="tpu_custom_call" | custom-call | flops 10000000 | bytes 1000000 | tf_op jit(solution)/shard_map/pallas_call | solution.py:34
  47.3 22.0 %all_to_all.26 = bf16[32,32,256]{2,1,0:T(8,128)(2,1)S(1)} all-to-all(bf16[32,32,256]{2,1,0:T(8,128)(2,1)S(1)} %bitcast.57), channel_id=1, replica_groups=mesh['z'=8,'x'=4,'c'=2,'ta'=8] {'z','x'}, dimensions={0} | all-to-all | bytes 1048576 | tf_op jit(solution)/shard_map/all_to_all | solution.py:20
  69.3 1.9 %collective-permute-start = (bf16[1024,256]{1,0:T(8,128)(2,1)S(1)}, bf16[1024,256]{1,0:T(8,128)(2,1)S(1)}, u32[]{:S(2)}, u32[]{:S(2)}) collective-permute-start(bf16[1024,256]{1,0:T(8,128)(2,1)S(1)} %bitcast.55), channel_id=1, source_target_pairs={{0,8},{8,0},{1,9},{9,1},{2,10},{10,2},{3,11},{11,3},{4,12},{12,4},... | collective-permute-start | bytes 1572872 | tf_op jit(solution)/shard_map/ppermute | solution.py:24
  71.2 1.9 %collective-permute-done.other = bf16[1024,256]{1,0:T(8,128)(2,1)S(1)} collective-permute-done((bf16[1024,256]{1,0:T(8,128)(2,1)S(1)}, bf16[1024,256]{1,0:T(8,128)(2,1)S(1)}, u32[]{:S(2)}, u32[]{:S(2)}) %collective-permute-start) | collective-permute-done | bytes 524320 | tf_op jit(solution)/shard_map/ppermute | solution.py:24
  73.1 3.4 %shard_map.164 = (bf16[32,1024]{1,0:T(8,128)(2,1)}, bf16[1024,256]{1,0:T(8,128)(2,1)S(1)}, bf16[1024,256]{1,0:T(8,128)(2,1)S(1)}) custom-call(s32[3]{0:T(128)S(1)} %pad_add_fusion.where, bf16[256,128]{1,0:T(8,128)(2,1)S(1)} %get-tuple-element.20.query, bf16[256,128]{1,0:T(8,128)(2,1)S(1)} %get-tuple-element.21.grad, bf16[1024,256]{1,0:T(8,128)(2,1)S(1)} %bitcast.56, ...), custom_call_target="tpu_custom_call" | custom-call | flops 1000000000 | bytes 4000000 | tf_op jit(solution)/shard_map/pallas_call | solution.py:34
  76.5 2.0 %collective-permute-start.1 = (bf16[1024,256]{1,0:T(8,128)(2,1)S(1)}, bf16[1024,256]{1,0:T(8,128)(2,1)S(1)}, u32[]{:S(2)}, u32[]{:S(2)}) collective-permute-start(bf16[1024,256]{1,0:T(8,128)(2,1)S(1)} %get-tuple-element.24), channel_id=1, source_target_pairs={{0,8},{8,0},{1,9},{9,1},{2,10},{10,2},{3,11},{11,3},{4,12},{12,4},... | collective-permute-start | bytes 1572872 | tf_op jit(solution)/shard_map/ppermute | solution.py:24
  78.5 1.7 %collective-permute-done.1 = bf16[1024,256]{1,0:T(8,128)(2,1)S(1)} collective-permute-done((bf16[1024,256]{1,0:T(8,128)(2,1)S(1)}, bf16[1024,256]{1,0:T(8,128)(2,1)S(1)}, u32[]{:S(2)}, u32[]{:S(2)}) %collective-permute-start.1) | collective-permute-done | bytes 524320 | tf_op jit(solution)/shard_map/ppermute | solution.py:24
  80.3 0.9 add_convert_fusion
  81.2 5.6 %all-to-all-start.3 = ((bf16[32,32,256]{2,1,0:T(8,128)(2,1)}), bf16[32,32,256]{2,1,0:T(8,128)(2,1)S(1)}, u32[]{:S(2)}, u32[]{:S(2)}) async-start(bf16[32,32,256]{2,1,0:T(8,128)(2,1)} %bitcast.21), calls=%async_computation.3 | async-start | bytes 1048576 | tf_op jit(solution)/shard_map/all_to_all | solution.py:20
  86.8 8.1 %all-gather.2.cloned.1.call-done = bf16[512,4096]{1,0:T(8,128)(2,1)} async-done(((bf16[512,512]{1,0:T(8,128)(2,1)}), bf16[512,4096]{1,0:T(8,128)(2,1)}) %all-gather.2.cloned.1.call-update) | async-done | bytes 4194320 | tf_op jit(solution)/shard_map/all_gather | solution.py:205
  94.9 3.7 %multiply_reduce_fusion = (f32[512]{0:T(512)S(1)}, f32[192,512]{1,0:T(8,128)S(1)}) fusion(bf16[1,192,512]{2,1,0:T(8,128)(2,1)S(1)} %copy-done.7, bf16[1,192,512]{2,1,0:T(8,128)(2,1)S(1)} %copy-done.8, bf16[512,4096]{1,0:T(8,128)(2,1)} %all-gather.2.cloned.1.call-done, bf16[1,192,4096]{2,1,0:T(8,128)(2,1)S(1)} %copy-done), kind=kOutput, calls=%fused_computation.20 | convolution fusion | flops 806190592 | bytes 6555648 | tf_op jit(solution)/shard_map/dot_general | solution.py:226
  98.8 0.8 pad_maximum_fusion
  99.5 4.4 %all-to-all-done.3 = bf16[32,32,256]{2,1,0:T(8,128)(2,1)S(1)} async-done(((bf16[32,32,256]{2,1,0:T(8,128)(2,1)}), bf16[32,32,256]{2,1,0:T(8,128)(2,1)S(1)}, u32[]{:S(2)}, u32[]{:S(2)}) %all-to-all-start.3) | async-done | bytes 524320 | tf_op jit(solution)/shard_map/all_to_all | solution.py:20
  103.9 6.5 %all-to-all-start.1 = ((f32[64,1,16]{2,1,0:T(1,128)}), f32[64,1,16]{2,1,0:T(1,128)S(1)}, u32[]{:S(2)}, u32[]{:S(2)}) async-start(f32[64,1,16]{2,1,0:T(1,128)} %pad_maximum_fusion), calls=%async_computation.1 | async-start | bytes 65536 | tf_op jit(solution)/shard_map/all_to_all | solution.py:20
  110.4 0.1 reduce_sum.22.owned
  110.5 7.7 %all-to-all-done.1.got = f32[64,1,16]{2,1,0:T(1,128)S(1)} async-done(((f32[64,1,16]{2,1,0:T(1,128)}), f32[64,1,16]{2,1,0:T(1,128)S(1)}, u32[]{:S(2)}, u32[]{:S(2)}) %all-to-all-start.1) | async-done | bytes 4128 | tf_op jit(solution)/shard_map/all_to_all | solution.py:20
  118.3 0.9 shard_map.165
  119.2 6.5 %all-to-all-start.4 = ((bf16[8,40,256]{2,1,0:T(8,128)(2,1)}), bf16[8,40,256]{2,1,0:T(8,128)(2,1)S(1)}, u32[]{:S(2)}, u32[]{:S(2)}) async-start(bf16[8,40,256]{2,1,0:T(8,128)(2,1)} %shard_map.165), calls=%async_computation.4 | async-start | bytes 327680 | tf_op jit(solution)/shard_map/all_to_all | solution.py:20
  125.7 0.2 slice_reduce_fusion
  125.9 0.1 mul.55
  126.0 4.4 %fusion = bf16[1,192,4096]{2,1,0:T(8,128)(2,1)} fusion(bf16[512,4096]{1,0:T(8,128)(2,1)} %all-gather.2.cloned.1.call-done, bf16[1,192,512]{2,1,0:T(8,128)(2,1)S(1)} %copy-done.7, f32[512]{0:T(512)S(1)} %mul.55, bf16[1,192,512]{2,1,0:T(8,128)(2,1)S(1)} %copy-done.8), kind=kOutput, calls=%fused_computation.1 | convolution fusion | flops 806977536 | bytes 6162432 | tf_op jit(solution)/shard_map/dot_general | solution.py:242
  130.3 1.0 fusion.13
  131.3 4.2 %all-to-all-done.4.terms = bf16[8,40,256]{2,1,0:T(8,128)(2,1)S(1)} async-done(((bf16[8,40,256]{2,1,0:T(8,128)(2,1)}), bf16[8,40,256]{2,1,0:T(8,128)(2,1)S(1)}, u32[]{:S(2)}, u32[]{:S(2)}) %all-to-all-start.4) | async-done | bytes 163872 | tf_op jit(solution)/shard_map/all_to_all | solution.py:20
  135.5 0.7 shard_map.166
  (16 shorter events, 0.2 us)
Async XLA Ops:
  7.2 87.7 %copy-start = (bf16[1,192,4096]{2,1,0:T(8,128)(2,1)S(1)}, bf16[1,192,4096]{2,1,0:T(8,128)(2,1)}, u32[]{:S(2)}) copy-start(bf16[1,192,4096]{2,1,0:T(8,128)(2,1)} %param.15) | copy-start | bytes 4718596
  7.2 87.7 %all-gather.2.cloned.1.call-start = ((), (), s32[]{:S(2)}) async-start(), calls=%async_computation.5 | async-start | bytes 4718592 | tf_op jit(solution)/shard_map/all_gather | solution.py:205
  41.1 53.9 %copy-start.7 = (bf16[1,192,512]{2,1,0:T(8,128)(2,1)S(1)}, bf16[1,192,512]{2,1,0:T(8,128)(2,1)}, u32[]{:S(2)}) copy-start(bf16[1,192,512]{2,1,0:T(8,128)(2,1)} %param.17) | copy-start | bytes 589828
  41.1 53.9 %copy-start.8 = (bf16[1,192,512]{2,1,0:T(8,128)(2,1)S(1)}, bf16[1,192,512]{2,1,0:T(8,128)(2,1)}, u32[]{:S(2)}) copy-start(bf16[1,192,512]{2,1,0:T(8,128)(2,1)} %param.16) | copy-start | bytes 589828
  41.2 0.9 copy-start.1
  42.1 0.8 copy-start.2
  42.9 0.8 copy-start.3
  43.7 0.8 copy-start.4
  44.4 0.7 copy-start.5
  45.1 0.7 copy-start.6
  69.3 3.8 %collective-permute-start = (bf16[1024,256]{1,0:T(8,128)(2,1)S(1)}, bf16[1024,256]{1,0:T(8,128)(2,1)S(1)}, u32[]{:S(2)}, u32[]{:S(2)}) collective-permute-start(bf16[1024,256]{1,0:T(8,128)(2,1)S(1)} %bitcast.55), channel_id=1, source_target_pairs={{0,8},{8,0},{1,9},{9,1},{2,10},{10,2},{3,11},{11,3},{4,12},{12,4},... | collective-permute-start | bytes 1572872 | tf_op jit(solution)/shard_map/ppermute | solution.py:24
  76.5 3.8 %collective-permute-start.1 = (bf16[1024,256]{1,0:T(8,128)(2,1)S(1)}, bf16[1024,256]{1,0:T(8,128)(2,1)S(1)}, u32[]{:S(2)}, u32[]{:S(2)}) collective-permute-start(bf16[1024,256]{1,0:T(8,128)(2,1)S(1)} %get-tuple-element.24), channel_id=1, source_target_pairs={{0,8},{8,0},{1,9},{9,1},{2,10},{10,2},{3,11},{11,3},{4,12},{12,4},... | collective-permute-start | bytes 1572872 | tf_op jit(solution)/shard_map/ppermute | solution.py:24
  81.2 22.7 %all-to-all-start.3 = ((bf16[32,32,256]{2,1,0:T(8,128)(2,1)}), bf16[32,32,256]{2,1,0:T(8,128)(2,1)S(1)}, u32[]{:S(2)}, u32[]{:S(2)}) async-start(bf16[32,32,256]{2,1,0:T(8,128)(2,1)} %bitcast.21), calls=%async_computation.3 | async-start | bytes 1048576 | tf_op jit(solution)/shard_map/all_to_all | solution.py:20
  103.9 14.4 %all-to-all-start.1 = ((f32[64,1,16]{2,1,0:T(1,128)}), f32[64,1,16]{2,1,0:T(1,128)S(1)}, u32[]{:S(2)}, u32[]{:S(2)}) async-start(f32[64,1,16]{2,1,0:T(1,128)} %pad_maximum_fusion), calls=%async_computation.1 | async-start | bytes 65536 | tf_op jit(solution)/shard_map/all_to_all | solution.py:20
  119.2 16.3 %all-to-all-start.4 = ((bf16[8,40,256]{2,1,0:T(8,128)(2,1)}), bf16[8,40,256]{2,1,0:T(8,128)(2,1)S(1)}, u32[]{:S(2)}, u32[]{:S(2)}) async-start(bf16[8,40,256]{2,1,0:T(8,128)(2,1)} %shard_map.165), calls=%async_computation.4 | async-start | bytes 327680 | tf_op jit(solution)/shard_map/all_to_all | solution.py:20
Sparse Core Ops, SparseCore 0:
  41.2 53.6 all-gather.1
